TPU v7x, 256 devices: a whole 4x4x8 slice. The times are simulated.
256 devices in a mesh: ctx: 128 (over z, x_lo, y, core), ch: 2 (over x_hi).
Axes of the slice: x: 4 (x_hi: 2, x_lo: 2; x = x_hi * 2 + x_lo), y: 4, z: 8, core: 2. Of those that a mesh axis runs over, the one named last changes fastest.
Arguments:
- query_proj: bfloat16 [32768, 2048], P('ctx', 'ch'), may hold values from -64 to 64
- key_proj: bfloat16 [32768, 2048], P('ctx', 'ch'), may hold values from -6 to 6
- value_proj: bfloat16 [32768, 2048], P('ctx', 'ch'), may hold values from -6 to 6
- filters: bfloat16 [1024, 2048], P('ctx', 'ch'), may hold values from -0.1875 to 0.1875
- cotangent: bfloat16 [32768, 2048], P('ctx', 'ch'), may hold values from -6 to 6
- stock_id: int32 [32768], P('ctx'), may hold values from 0 to 511
- stock_class: int32 [512], replicated, may hold values from 0 to 10
- cond_table: float32 [11, 2048], P(None, 'ch'), may hold values from -2.5 to 2.5
Outputs:
- normed_out: bfloat16 [32768, 2048], P('ctx', 'ch')
- grad_query: bfloat16 [32768, 2048], P('ctx', 'ch')
- grad_key: bfloat16 [32768, 2048], P('ctx', 'ch')
- grad_value: bfloat16 [32768, 2048], P('ctx', 'ch')
- grad_filter: float32 [1024, 2048], P('ctx', 'ch')
All inputs are finite; a program needn't handle non-finite values.
Results may differ from a plain program's by a relative error of at most 0.005.
Values may be sent and summed in bfloat16 or wider, within the bound.
No kernel may reach another device: no remote copies, remote signals or barrier semaphores. Data moves between devices by JAX's collectives and lax.ppermute only.
A program may use at most 128 MiB of HBM per device.

v0:
```python
import math

import jax
import jax.numpy as jnp
from jax import lax
from jax.sharding import PartitionSpec as P

REACH = 4


EPSILON = 1e-05
PRECISE = lax.Precision.HIGHEST
TRANSFORM = lax.Precision.HIGH


def from_behind(block, axis, distance):
    devices = range(lax.axis_size(axis))
    route = [(i - distance, i) for i in devices if i - distance in devices]
    return lax.ppermute(block, axis, route)


def product_tables(length, flipped):
    frequency = lax.broadcasted_iota(jnp.int32, (length, length), 0)
    position = lax.broadcasted_iota(jnp.int32, (length, length), 1)
    if flipped:
        position = length - 1 - position
    phase_index = (2 * frequency + 1) * position % (4 * length)
    angles = phase_index.astype(jnp.float32) * (math.pi / (2 * length))
    return (jnp.cos(angles), jnp.sin(angles))


def output_tables(length, flipped):
    position = lax.broadcasted_iota(jnp.int32, (length, length), 0)
    frequency = lax.broadcasted_iota(jnp.int32, (length, length), 1)
    if flipped:
        position = 2 * length - 1 - position
    else:
        position = length + position
    phase_index = (2 * frequency + 1) * position % (4 * length)
    angles = phase_index.astype(jnp.float32) * (math.pi / (2 * length))
    return (jnp.cos(angles) / length, jnp.sin(angles) / length)


def spectra(tables, pieces):
    cosine, sine_table = tables
    real_part = jnp.einsum("fs,nsc->fnc", cosine, pieces, precision=TRANSFORM)
    imag_part = -jnp.einsum("fs,nsc->fnc", sine_table, pieces, precision=TRANSFORM)
    return (real_part, imag_part)


def signals(tables, spectrum):
    cosine, sine_table = tables
    return jnp.einsum("tf,fnc->ntc", cosine, spectrum[0], precision=TRANSFORM) - jnp.einsum(
        "tf,fnc->ntc", sine_table, spectrum[1], precision=TRANSFORM
    )


def adjoint_spectra(tables, pieces):
    cosine, sine_table = tables
    real_part = jnp.einsum("tf,ntc->fnc", cosine, pieces, precision=TRANSFORM)
    imag_part = -jnp.einsum("tf,ntc->fnc", sine_table, pieces, precision=TRANSFORM)
    return (real_part, imag_part)


def complex_product(left_pair, right_pair):
    return (
        left_pair[0] * right_pair[0] - left_pair[1] * right_pair[1],
        left_pair[0] * right_pair[1] + left_pair[1] * right_pair[0],
    )


def complex_add(left_pair, right_pair):
    return (left_pair[0] + right_pair[0], left_pair[1] + right_pair[1])


def alternating(length):
    return jnp.where(jnp.arange(length) % 2 == 0, 1.0, -1.0).astype(jnp.float32)[:, None, None]


def filter_segments(tables, filter_full, length, reach_blocks):
    channels = filter_full.shape[1]
    lag_spectra = spectra(tables, filter_full.reshape(reach_blocks, length, channels))
    alternate = alternating(length)
    segments = []
    for distance in range(reach_blocks + 1):
        real_part = jnp.zeros((length, 1, channels), jnp.float32)
        imag_part = jnp.zeros((length, 1, channels), jnp.float32)
        if distance >= 1:
            real_part = lag_spectra[0][:, distance - 1 : distance]
            imag_part = lag_spectra[1][:, distance - 1 : distance]
        if distance < reach_blocks:
            real_part = real_part + alternate * lag_spectra[1][:, distance : distance + 1]
            imag_part = imag_part - alternate * lag_spectra[0][:, distance : distance + 1]
        segments.append((real_part, imag_part))
    return segments


def segment_grad(adjoint, spectrum):
    real_part = jnp.sum(adjoint[0] * spectrum[0] + adjoint[1] * spectrum[1], axis=1, keepdims=True)
    imag_part = jnp.sum(adjoint[1] * spectrum[0] - adjoint[0] * spectrum[1], axis=1, keepdims=True)
    return (real_part, imag_part)


def filter_gradient(tables, seg_grads, length, reach_blocks):
    alternate = alternating(length)
    grad_real = []
    grad_imag = []
    for lag_block in range(reach_blocks):
        grad_real.append(seg_grads[lag_block + 1][0] - alternate * seg_grads[lag_block][1])
        grad_imag.append(seg_grads[lag_block + 1][1] + alternate * seg_grads[lag_block][0])
    grad_real = jnp.concatenate(grad_real, axis=1)
    grad_imag = jnp.concatenate(grad_imag, axis=1)
    cosine, sine_table = tables
    lag_rows = jnp.einsum("fs,fmc->msc", cosine, grad_real, precision=TRANSFORM) - jnp.einsum(
        "fs,fmc->msc", sine_table, grad_imag, precision=TRANSFORM
    )
    return lag_rows.reshape(reach_blocks * length, lag_rows.shape[2])


def shards(query_proj, key_proj, value_proj, filters, cotangent, stock_id, stock_class, cond_table):
    length = key_proj.shape[0]
    local_channels = key_proj.shape[1]
    total_channels = local_channels * lax.axis_size("ch")
    forward_tables = product_tables(length, False)
    reverse_tables = product_tables(length, True)
    out_tables = output_tables(length, False)
    back_tables = output_tables(length, True)
    stock_hits = (
        stock_id[:, None] == jnp.arange(stock_class.shape[0], dtype=jnp.int32)[None, :]
    ).astype(jnp.float32)
    class_hits = (
        stock_class[:, None] == jnp.arange(cond_table.shape[0], dtype=jnp.int32)[None, :]
    ).astype(jnp.float32)
    event_class = jnp.dot(
        stock_hits, class_hits, precision=PRECISE, preferred_element_type=jnp.float32
    )
    cond_rows = jnp.dot(
        event_class, cond_table, precision=PRECISE, preferred_element_type=jnp.float32
    )
    gate_rows = query_proj.astype(jnp.float32) * (1.0 + cond_rows)
    mixed_in = (key_proj.astype(jnp.float32) * value_proj.astype(jnp.float32)).astype(jnp.bfloat16)
    filter_full = lax.all_gather(filters, "ctx", axis=0, tiled=True).astype(jnp.float32)
    segments = filter_segments(forward_tables, filter_full, length, REACH)
    neighbours = [spectra(forward_tables, mixed_in.astype(jnp.float32)[None])]
    moving = mixed_in
    for distance in range(1, REACH + 1):
        moving = from_behind(moving, "ctx", 1)
        neighbours.append(spectra(forward_tables, moving.astype(jnp.float32)[None]))
    accumulated = complex_product(segments[0], neighbours[0])
    for distance in range(1, REACH + 1):
        accumulated = complex_add(
            accumulated, complex_product(segments[distance], neighbours[distance])
        )
    conv_out = signals(out_tables, accumulated)[0]
    scaled = gate_rows * conv_out
    squares = lax.psum(jnp.sum(scaled * scaled, axis=1), "ch")
    inv_rms = lax.rsqrt(squares / total_channels + EPSILON)[:, None]
    normed = scaled * inv_rms
    normed_out = normed.astype(jnp.bfloat16)
    upstream = cotangent.astype(jnp.float32)
    inner_sum = lax.psum(jnp.sum(upstream * normed, axis=1), "ch")
    grad_scaled = inv_rms * (upstream - normed * (inner_sum / total_channels)[:, None])
    grad_query = (grad_scaled * conv_out * (1.0 + cond_rows)).astype(jnp.bfloat16)
    grad_conv = (grad_scaled * gate_rows).astype(jnp.bfloat16)
    own_reverse = spectra(reverse_tables, grad_conv.astype(jnp.float32)[None])
    accumulated = complex_product(segments[0], own_reverse)
    moving = grad_conv
    for distance in range(1, REACH + 1):
        moving = from_behind(moving, "ctx", -1)
        later_spec = spectra(reverse_tables, moving.astype(jnp.float32)[None])
        accumulated = complex_add(accumulated, complex_product(segments[distance], later_spec))
    grad_mixed = signals(back_tables, accumulated)[0]
    adjoint = adjoint_spectra(out_tables, grad_conv.astype(jnp.float32)[None])
    seg_grads = [segment_grad(adjoint, neighbours[distance]) for distance in range(REACH + 1)]
    filter_term = filter_gradient(forward_tables, seg_grads, length, REACH)
    grad_filter = lax.psum_scatter(filter_term, "ctx", scatter_dimension=0, tiled=True)
    grad_key = (grad_mixed * value_proj.astype(jnp.float32)).astype(jnp.bfloat16)
    grad_value = (grad_mixed * key_proj.astype(jnp.float32)).astype(jnp.bfloat16)
    return (normed_out, grad_query, grad_key, grad_value, grad_filter)


def solution(mesh):
    return jax.shard_map(
        shards,
        mesh=mesh,
        in_specs=(
            P("ctx", "ch"),
            P("ctx", "ch"),
            P("ctx", "ch"),
            P("ctx", "ch"),
            P("ctx", "ch"),
            P("ctx"),
            P(),
            P(None, "ch"),
        ),
        out_specs=(P("ctx", "ch"), P("ctx", "ch"), P("ctx", "ch"), P("ctx", "ch"), P("ctx", "ch")),
        check_vma=False,
    )
```

profile of v0, /device:TPU:1, one launch (start us, length us, event | category | flops | bytes accessed | tf_op | source)
XLA Modules:
  0.0 852.6 jit_solution(3938443588100111600)
XLA Ops:
  10.8 4.6 collective-permute-start
  18.5 2.7 fusion.209
  21.1 2.7 fusion.222
  28.6 2.7 fusion.219
  32.0 4.4 collective-permute-start.2
  42.5 4.4 collective-permute-start.3
  49.0 2.7 fusion.215
  53.0 2.7 fusion.201
  58.3 168.2 %all-gather.2.cloned.1.call-done = bf16[1024,1024]{1,0:T(8,128)(2,1)} async-done(((bf16[8,1024]{1,0:T(8,128)(2,1)}), bf16[1024,1024]{1,0:T(8,128)(2,1)}) %all-gather.2.cloned.1.call-update) | async-done | bytes 2097168 | tf_op jit(solution)/shard_map/all_gather | solution.py:142
  226.5 4.0 convolution_negate_fusion
  236.4 3.8 fusion.35
  240.2 4.9 multiply_reduce_fusion
  245.1 5.3 psum.14
  252.1 5.3 psum.15
  257.4 3.7 multiply_convert_fusion
  268.1 3.8 fusion
  271.9 6.1 fusion.16
  279.0 5.3 collective-permute-start.4
  284.4 9.0 %collective-permute-done.4 = bf16[256,1024]{1,0:T(8,128)(2,1)S(1)} collective-permute-done((bf16[256,1024]{1,0:T(8,128)(2,1)S(1)}, bf16[256,1024]{1,0:T(8,128)(2,1)S(1)}, u32[]{:S(2)}, u32[]{:S(2)}) %collective-permute-start.4) | collective-permute-done | bytes 524320 | tf_op jit(solution)/shard_map/ppermute | solution.py:19
  295.3 8.8 %collective-permute-done.5 = bf16[256,1024]{1,0:T(8,128)(2,1)S(1)} collective-permute-done((bf16[256,1024]{1,0:T(8,128)(2,1)S(1)}, bf16[256,1024]{1,0:T(8,128)(2,1)S(1)}, u32[]{:S(2)}, u32[]{:S(2)}) %collective-permute-start.5) | collective-permute-done | bytes 524320 | tf_op jit(solution)/shard_map/ppermute | solution.py:19
  322.6 3.0 collective-permute-done.7
  328.6 3.3 fusion.32
  331.9 3.6 fusion.26
  337.5 507.9 %reduce-scatter.2.cloned.1.call-done = f32[8,1024]{1,0:T(8,128)} async-done(((f32[1024,1024]{1,0:T(8,128)}), f32[8,1024]{1,0:T(8,128)}) %reduce-scatter.2.cloned.1.call-update) | async-done | bytes 32784 | tf_op jit(solution)/shard_map/reduce_scatter | solution.py:176
  (106 shorter events, 65.0 us)
Async XLA Ops:
  7.2 9.3 %copy-start = (f32[11,1024]{1,0:T(8,128)S(1)}, f32[11,1024]{1,0:T(8,128)}, u32[]{:S(2)}) copy-start(f32[11,1024]{1,0:T(8,128)} %param.15) | copy-start | bytes 135172
  7.2 219.3 %all-gather.2.cloned.1.call-start = ((), (), s32[]{:S(2)}) async-start(), calls=%async_computation.1 | async-start | bytes 2113536 | tf_op jit(solution)/shard_map/all_gather | solution.py:142
  7.9 837.6 %reduce-scatter.2.cloned.1.call-start = ((), (), s32[]{:S(2)}) async-start(), calls=%async_computation.2 | async-start | bytes 4227072 | tf_op jit(solution)/shard_map/reduce_scatter | solution.py:176
  9.2 19.3 %copy-start.22 = (bf16[256,1024]{0,1:T(8,128)(2,1)}, bf16[256,1024]{0,1:T(8,128)(2,1)S(1)}, u32[]{:S(2)}) copy-start(bf16[256,1024]{0,1:T(8,128)(2,1)S(1)} %copy.14) | copy-start | bytes 1572868
  10.7 20.6 %copy-start.24 = (bf16[256,1024]{0,1:T(8,128)(2,1)}, bf16[256,1024]{0,1:T(8,128)(2,1)S(1)}, u32[]{:S(2)}) copy-start(bf16[256,1024]{0,1:T(8,128)(2,1)S(1)} %copy.15) | copy-start | bytes 1572868
  10.8 13.0 %collective-permute-start = (bf16[256,1024]{0,1:T(8,128)(2,1)S(1)}, bf16[256,1024]{0,1:T(8,128)(2,1)S(1)}, u32[]{:S(2)}, u32[]{:S(2)}) collective-permute-start(bf16[256,1024]{0,1:T(8,128)(2,1)S(1)} %fusion.27), channel_id=1, source_target_pairs={{0,2},{2,4},{4,6},{6,8},{8,10},{10,12},{12,14},{14,16},{16,18},{18... | collective-permute-start | bytes 1572872 | tf_op jit(solution)/shard_map/ppermute | solution.py:19
  23.8 8.2 collective-permute-start.1
  32.0 10.5 %collective-permute-start.2 = (bf16[256,1024]{0,1:T(8,128)(2,1)S(1)}, bf16[256,1024]{0,1:T(8,128)(2,1)S(1)}, u32[]{:S(2)}, u32[]{:S(2)}) collective-permute-start(bf16[256,1024]{0,1:T(8,128)(2,1)S(1)} %collective-permute-done.1), channel_id=1, source_target_pairs={{0,2},{2,4},{4,6},{6,8},{8,10},{10,12},{12,14},{14,16},{16,18},{18... | collective-permute-start | bytes 1572872 | tf_op jit(solution)/shard_map/ppermute | solution.py:19
  42.5 10.5 %collective-permute-start.3 = (bf16[256,1024]{0,1:T(8,128)(2,1)S(1)}, bf16[256,1024]{0,1:T(8,128)(2,1)S(1)}, u32[]{:S(2)}, u32[]{:S(2)}) collective-permute-start(bf16[256,1024]{0,1:T(8,128)(2,1)S(1)} %collective-permute-done.2), channel_id=1, source_target_pairs={{0,2},{2,4},{4,6},{6,8},{8,10},{10,12},{12,14},{14,16},{16,18},{18... | collective-permute-start | bytes 1572872 | tf_op jit(solution)/shard_map/ppermute | solution.py:19
  226.5 6.5 copy-start.18
  230.6 9.6 %copy-start.8 = (f32[256,4,1024]{2,0,1:T(8,128)}, f32[256,4,1024]{2,0,1:T(8,128)S(1)}, u32[]{:S(2)}) copy-start(f32[256,4,1024]{2,0,1:T(8,128)S(1)} %convolution_negate_fusion) | copy-start | bytes 12582916
  230.6 5.5 copy-start.14
  230.6 5.8 copy-start.16
  232.9 7.3 copy-start.10
  257.4 6.6 copy-start.3
  257.4 6.6 copy-start.5
  257.4 6.6 copy-start.7
  279.0 14.3 %collective-permute-start.4 = (bf16[256,1024]{1,0:T(8,128)(2,1)S(1)}, bf16[256,1024]{1,0:T(8,128)(2,1)S(1)}, u32[]{:S(2)}, u32[]{:S(2)}) collective-permute-start(bf16[256,1024]{1,0:T(8,128)(2,1)S(1)} %copy-done.28), channel_id=1, source_target_pairs={{2,0},{4,2},{6,4},{8,6},{10,8},{12,10},{14,12},{16,14},{18,16},{20... | collective-permute-start | bytes 1572872 | tf_op jit(solution)/shard_map/ppermute | solution.py:19
  293.3 10.7 %collective-permute-start.5 = (bf16[256,1024]{1,0:T(8,128)(2,1)S(1)}, bf16[256,1024]{1,0:T(8,128)(2,1)S(1)}, u32[]{:S(2)}, u32[]{:S(2)}) collective-permute-start(bf16[256,1024]{1,0:T(8,128)(2,1)S(1)} %collective-permute-done.4), channel_id=1, source_target_pairs={{2,0},{4,2},{6,4},{8,6},{10,8},{12,10},{14,12},{16,14},{18,16},{20... | collective-permute-start | bytes 1572872 | tf_op jit(solution)/shard_map/ppermute | solution.py:19
  304.0 10.5 %collective-permute-start.6 = (bf16[256,1024]{1,0:T(8,128)(2,1)S(1)}, bf16[256,1024]{1,0:T(8,128)(2,1)S(1)}, u32[]{:S(2)}, u32[]{:S(2)}) collective-permute-start(bf16[256,1024]{1,0:T(8,128)(2,1)S(1)} %collective-permute-done.5), channel_id=1, source_target_pairs={{2,0},{4,2},{6,4},{8,6},{10,8},{12,10},{14,12},{16,14},{18,16},{20... | collective-permute-start | bytes 1572872 | tf_op jit(solution)/shard_map/ppermute | solution.py:19
  314.5 11.1 %collective-permute-start.7 = (bf16[256,1024]{1,0:T(8,128)(2,1)S(1)}, bf16[256,1024]{1,0:T(8,128)(2,1)S(1)}, u32[]{:S(2)}, u32[]{:S(2)}) collective-permute-start(bf16[256,1024]{1,0:T(8,128)(2,1)S(1)} %collective-permute-done.6), channel_id=1, source_target_pairs={{2,0},{4,2},{6,4},{8,6},{10,8},{12,10},{14,12},{16,14},{18,16},{20... | collective-permute-start | bytes 1572872 | tf_op jit(solution)/shard_map/ppermute | solution.py:19
  318.1 10.4 %copy-start.9 = (f32[256,4,1024]{2,0,1:T(8,128)S(1)}, f32[256,4,1024]{2,0,1:T(8,128)}, u32[]{:S(2)}) copy-start(f32[256,4,1024]{2,0,1:T(8,128)} %copy-done.8) | copy-start | bytes 12582916
  318.1 10.4 %copy-start.11 = (f32[256,4,1024]{2,0,1:T(8,128)S(1)}, f32[256,4,1024]{2,0,1:T(8,128)}, u32[]{:S(2)}) copy-start(f32[256,4,1024]{2,0,1:T(8,128)} %copy-done.10) | copy-start | bytes 12582916
  331.9 513.6 %copy-start.1 = (f32[11,1024]{1,0:T(8,128)S(1)}, f32[11,1024]{1,0:T(8,128)}, u32[]{:S(2)}) copy-start(f32[11,1024]{1,0:T(8,128)} %param.15) | copy-start | bytes 135172
  (15 other events, 43.8 us)
Sparse Core Ops, SparseCore 0:
  9.9 216.5 all-gather.1
  278.1 567.2 reduce-scatter.1
where the time goes:
time: 868 us; the launch traced here: 853 us
  waiting for transfers between devices  704 us (81%)
  matrix products  77.2 us (9%)
  starting transfers between devices  26.8 us (3%)
  between operations  14.9 us (2%)
  blocking collectives  10.6 us (1%)
  local copies, waits for them, and re-layouts  10.2 us (1%)
    reduce_scatter x1, waiting for transfers between devices, shards(): lax.psum_scatter(filter_term, 'ctx', scatter_dimension=0, tiled=True)  508 us
    all_gather x1, waiting for transfers between devices, shards(): lax.all_gather(filters, 'ctx', axis=0, tiled=True).astype(jnp.float32)  168 us
    ppermute x8, waiting for transfers between devices, from_behind(): return lax.ppermute(block, axis, route)  27.5 us
    ppermute x8, starting transfers between devices, from_behind(): return lax.ppermute(block, axis, route)  26.7 us
    dot_general x11, matrix products, spectra(): jnp.einsum('fs,nsc->fnc', sine_table, pieces, precision=TRANSFORM)  23.5 us
    dot_general x11, matrix products, spectra(): real_part = jnp.einsum('fs,nsc->fnc', cosine, pieces, precision=TRANSFORM)  22.3 us
  transfers between devices with their start and end apart: 10, of which 9 were waited for; matrix products, arithmetic and copies ran while one was open for 6% of the time, Pallas kernels for 0%

commit v1 on v0

v1 whole, which is shorter than its diff:
```python
import functools

import jax
import jax.numpy as jnp
import numpy as np
import ml_dtypes
from jax import lax
from jax.experimental import pallas as pl
from jax.experimental.pallas import tpu as pltpu
from jax.sharding import Mesh, PartitionSpec as P

GROUP = 8
REACH = 4
LEN = 256
LANES = 128
EPSILON = 1e-05
F32 = jnp.float32
BF16 = jnp.bfloat16


def split_table(table):
    high = table.astype(np.float32).astype(ml_dtypes.bfloat16)
    low = (table - high.astype(np.float64)).astype(ml_dtypes.bfloat16)
    return high, low


def transform_tables():
    number = np.concatenate([np.arange(0, LEN, 2), np.arange(1, LEN, 2)])
    angles = np.pi * ((2 * number[:, None] + 1) * np.arange(LEN)[None, :] % (4 * LEN)) / (2 * LEN)
    forward = np.concatenate([np.cos(angles), -np.sin(angles)], axis=0)
    return (*split_table(forward), *split_table(forward.T / LEN))


def dot(left, right):
    return jnp.dot(left, right, preferred_element_type=F32)


def halves(value):
    high = value.astype(BF16)
    return high, (value - high.astype(F32)).astype(BF16)


def lane(index):
    return pl.ds(pl.multiple_of(index * LANES, LANES), LANES)


def col(index):
    return slice(index * LANES, (index + 1) * LANES)


def pack_mixed(key_ref, value_ref, filters_ref, out_ref):
    for place in range(GROUP):
        product = key_ref[:, col(place)].astype(F32) * value_ref[:, col(place)].astype(F32)
        out_ref[place, :LEN, :] = product.astype(BF16)
        out_ref[place, LEN:, :] = filters_ref[:, col(place)]


def pack_gates(place_ref, query_ref, cotangent_ref, stock_ref, class_ref, *out_refs):
    place = place_ref[0]
    stocks = class_ref.shape[1]
    hits = (lax.broadcasted_iota(jnp.int32, (stocks, LEN), 0) == stock_ref[...]).astype(F32).astype(BF16)
    classes = jnp.broadcast_to(class_ref[...].astype(F32), (8, stocks)).astype(BF16)
    event_class = dot(classes, hits).astype(BF16)
    for step in range(GROUP):
        there = lane((place + step) & (GROUP - 1))
        out_refs[step][:LEN, :] = query_ref[:, there]
        out_refs[step][LEN : 2 * LEN, :] = cotangent_ref[:, there]
        out_refs[step][2 * LEN : 2 * LEN + 8, :] = event_class[:, :LANES]
        out_refs[step][2 * LEN + 8 :, :] = event_class[:, LANES:]


def unpack_gates(place_ref, table_ref, *refs):
    pieces, (gate_ref, factor_ref, upstream_ref) = refs[:GROUP], refs[GROUP:]
    place = place_ref[0]
    table = table_ref[:, lane(place)]
    table_high, rest = table.astype(BF16), table
    table_mid = (rest - table_high.astype(F32)).astype(BF16)
    table_low = (rest - table_high.astype(F32) - table_mid.astype(F32)).astype(BF16)
    rows = table.shape[0]
    for step in range(GROUP):
        there = lane((place - step) & (GROUP - 1))
        piece = pieces[step]
        event_class = jnp.concatenate(
            [piece[2 * LEN : 2 * LEN + 8, :].astype(F32)[:1], piece[2 * LEN + 8 :, :].astype(F32)[:1]], axis=1
        )
        number = lax.broadcasted_iota(jnp.int32, (rows, LEN), 0).astype(F32)
        hits = (number == event_class).astype(F32)
        hits = jnp.transpose(hits).astype(BF16)
        factor = 1.0 + (dot(hits, table_high) + dot(hits, table_mid) + dot(hits, table_low))
        factor_ref[:, there] = factor
        gate_ref[:, there] = piece[:LEN, :].astype(F32) * factor
        upstream_ref[:, there] = piece[LEN : 2 * LEN, :]


def spectrum(forward, rows):
    return dot(forward[0][...], rows) + dot(forward[1][...], rows)


def invert(inverse, spec):
    high, low = halves(spec)
    return dot(inverse[0][...], high) + (dot(inverse[0][...], low) + dot(inverse[1][...], high))


def over_frequencies(step):
    for half in range(2):
        @pl.loop(0, LEN // 16)
        def _(chunk):
            step(pl.multiple_of(half * (LEN // 2) + chunk * 8, 8), 1.0 - 2.0 * half)


def own_spectra(mixed_ref, forward_high, forward_low, out_ref):
    rows = jnp.concatenate([mixed_ref[block, :LEN, :] for block in range(GROUP)], axis=1)
    out_ref[...] = spectrum((forward_high, forward_low), rows)


def windows(real, imag, sign):
    pairs = {}
    for block in range(1, len(real)):
        pairs[block] = (real[block] - sign * imag[block - 1], imag[block] + sign * real[block - 1])
    return pairs


def read_blocks(own_ref, before_ref, row):
    real = [before_ref[pl.ds(row, 8), col(block)] for block in range(REACH)]
    real += [own_ref[pl.ds(row, 8), col(block)] for block in range(GROUP)]
    imag = [before_ref[pl.ds(row + LEN, 8), col(block)] for block in range(REACH)]
    imag += [own_ref[pl.ds(row + LEN, 8), col(block)] for block in range(GROUP)]
    return real, imag


def convolve(
    own_ref, before_ref, lags_ref, gate_ref, upstream_ref, forward_high, forward_low, inverse_high, inverse_low,
    conv_ref, before_spec_ref, lag_spec_ref, sums_ref, product_ref,
):
    forward = (forward_high, forward_low)
    before_spec_ref[...] = spectrum(forward, jnp.concatenate([before_ref[b] for b in range(REACH)], axis=1))
    lags = lags_ref[...].reshape(REACH, LEN, LANES)
    lag_spec_ref[...] = spectrum(forward, jnp.concatenate([lags[b] for b in range(REACH)], axis=1))

    def step(row, sign):
        real, imag = read_blocks(own_ref, before_spec_ref, row)
        pairs = windows(real, imag, sign)
        lag = [
            (lag_spec_ref[pl.ds(row, 8), col(d)], lag_spec_ref[pl.ds(row + LEN, 8), col(d)]) for d in range(REACH)
        ]
        for block in range(GROUP):
            total_real, total_imag = 0.0, 0.0
            for d in range(REACH):
                window = pairs[REACH + block - d]
                total_real += lag[d][0] * window[0] - lag[d][1] * window[1]
                total_imag += lag[d][0] * window[1] + lag[d][1] * window[0]
            product_ref[pl.ds(row, 8), col(block)] = total_real
            product_ref[pl.ds(row + LEN, 8), col(block)] = total_imag

    over_frequencies(step)
    conv = invert((inverse_high, inverse_low), product_ref[...])
    conv_ref[...] = conv
    scaled = gate_ref[...] * conv
    ones = jnp.ones((8, LANES), BF16)
    upstream = upstream_ref[...].astype(F32)

    def channel_sum(value):
        parts = halves(value)
        contract = (((1,), (1,)), ((), ()))
        return sum(lax.dot_general(ones, part, contract, preferred_element_type=F32) for part in parts)

    for index, value in enumerate((scaled * scaled, scaled * upstream)):
        for pair in range(GROUP // 2):
            both = jnp.concatenate(
                [channel_sum(value[:, col(2 * pair)])[:1], channel_sum(value[:, col(2 * pair + 1)])[:1]], axis=1
            )
            line = index * (GROUP // 2) + pair
            for peer in range(sums_ref.shape[0]):
                sums_ref[peer, line : line + 1, :] = both


def finish_norm(
    channels, place_ref, sums_ref, conv_ref, gate_ref, factor_ref, upstream_ref, grad_ref, first_ref, *refs
):
    out_refs, both_ref = refs[:GROUP], refs[GROUP]
    place = place_ref[0]
    total = jnp.sum(sums_ref[...], axis=0)
    half = GROUP // 2
    inv_rms = lax.rsqrt(total[:half] / channels + EPSILON)
    inner = total[half:] * inv_rms / channels
    lines = jnp.transpose(jnp.concatenate([inv_rms, inner], axis=0))
    for block in range(GROUP):
        rows = slice((block % 2) * LEN, (block % 2 + 1) * LEN)
        inv = lines[rows, block // 2 : block // 2 + 1]
        mean = lines[rows, half + block // 2 : half + block // 2 + 1]
        conv, gate = conv_ref[:, col(block)], gate_ref[:, col(block)]
        normed = gate * conv * inv
        both_ref[:LEN, col(block)] = normed.astype(BF16)
        grad_scaled = inv * (upstream_ref[:, col(block)].astype(F32) - normed * mean)
        both_ref[LEN:, col(block)] = (grad_scaled * conv * factor_ref[:, col(block)]).astype(BF16)
        grad_conv = (grad_scaled * gate).astype(BF16)
        grad_ref[:, col(block)] = grad_conv
        if block < REACH:
            first_ref[:, col(block)] = grad_conv
    for step in range(GROUP):
        out_refs[step][...] = both_ref[:, lane((place + step) & (GROUP - 1))]


def filter_terms(
    grad_ref, own_ref, before_ref, forward_high, forward_low, inverse_high, inverse_low, grad_spec_ref, out_ref,
    product_ref,
):
    grad_spec_ref[...] = spectrum((forward_high, forward_low), grad_ref[...])

    def step(row, sign):
        real, imag = read_blocks(own_ref, before_ref, row)
        pairs = windows(real, imag, sign)
        grads = [
            (grad_spec_ref[pl.ds(row, 8), col(b)], grad_spec_ref[pl.ds(row + LEN, 8), col(b)]) for b in range(GROUP)
        ]
        for d in range(REACH):
            total_real, total_imag = 0.0, 0.0
            for block in range(GROUP):
                window = pairs[REACH + block - d]
                total_real += grads[block][0] * window[0] + grads[block][1] * window[1]
                total_imag += grads[block][1] * window[0] - grads[block][0] * window[1]
            product_ref[pl.ds(row, 8), col(d)] = total_real
            product_ref[pl.ds(row + LEN, 8), col(d)] = total_imag

    over_frequencies(step)
    terms = invert((inverse_high, inverse_low), product_ref[...])
    owners, rows = out_ref.shape[0] // REACH, out_ref.shape[1]
    for d in range(REACH):
        out_ref[d * owners : (d + 1) * owners] = terms[:, col(d)].reshape(owners, rows, LANES)


def correlate_back(
    place_ref, grad_spec_ref, after_ref, lag_spec_ref, forward_high, forward_low, inverse_high, inverse_low, *refs
):
    out_refs, (after_spec_ref, product_ref, result_ref) = refs[:GROUP], refs[GROUP:]
    place = place_ref[0]
    after_spec_ref[...] = spectrum((forward_high, forward_low), after_ref[...])

    def step(row, sign):
        real = [grad_spec_ref[pl.ds(row, 8), col(b)] for b in range(GROUP)]
        real += [after_spec_ref[pl.ds(row, 8), col(b)] for b in range(REACH)]
        imag = [grad_spec_ref[pl.ds(row + LEN, 8), col(b)] for b in range(GROUP)]
        imag += [after_spec_ref[pl.ds(row + LEN, 8), col(b)] for b in range(REACH)]
        pairs = [
            (real[b] + sign * imag[b + 1], imag[b] - sign * real[b + 1]) for b in range(GROUP + REACH - 1)
        ]
        lag = [
            (lag_spec_ref[pl.ds(row, 8), col(d)], lag_spec_ref[pl.ds(row + LEN, 8), col(d)]) for d in range(REACH)
        ]
        for block in range(GROUP):
            total_real, total_imag = 0.0, 0.0
            for d in range(REACH):
                window = pairs[block + d]
                total_real += lag[d][0] * window[0] + lag[d][1] * window[1]
                total_imag += lag[d][0] * window[1] - lag[d][1] * window[0]
            product_ref[pl.ds(row, 8), col(block)] = total_real
            product_ref[pl.ds(row + LEN, 8), col(block)] = total_imag

    over_frequencies(step)
    result_ref[...] = invert((inverse_high, inverse_low), product_ref[...]).astype(BF16)
    for step_number in range(GROUP):
        out_refs[step_number][...] = result_ref[:, lane((place + step_number) & (GROUP - 1))]


def finish_forward(place_ref, *refs):
    pieces, (normed_ref, grad_query_ref) = refs[:GROUP], refs[GROUP:]
    place = place_ref[0]
    for step in range(GROUP):
        there = lane((place - step) & (GROUP - 1))
        normed_ref[:, there] = pieces[step][:LEN, :]
        grad_query_ref[:, there] = pieces[step][LEN:, :]


def finish_backward(place_ref, key_ref, value_ref, *refs):
    pieces, (grad_key_ref, grad_value_ref) = refs[:GROUP], refs[GROUP:]
    place = place_ref[0]
    for step in range(GROUP):
        there = lane((place - step) & (GROUP - 1))
        grad_mixed = pieces[step][...].astype(F32)
        grad_key_ref[:, there] = (grad_mixed * value_ref[:, there].astype(F32)).astype(BF16)
        grad_value_ref[:, there] = (grad_mixed * key_ref[:, there].astype(F32)).astype(BF16)


def sum_terms(terms_ref, out_ref):
    groups = terms_ref.shape[0] // GROUP
    for place in range(GROUP):
        total = terms_ref[place]
        for group in range(1, groups):
            total = total + terms_ref[group * GROUP + place]
        out_ref[:, col(place)] = total


def call(body, outs, *args, scalars=0, scratch=(), cost=None):
    specs = [pl.BlockSpec(memory_space=pltpu.SMEM)] * scalars
    specs += [pl.BlockSpec(memory_space=pltpu.VMEM)] * (len(args) - scalars)
    shapes = [jax.ShapeDtypeStruct(shape, dtype) for shape, dtype in outs]
    moved = sum(a.size * a.dtype.itemsize for a in args) + sum(s.size * s.dtype.itemsize for s in shapes)
    return pl.pallas_call(
        body,
        out_shape=shapes,
        in_specs=specs,
        out_specs=[pl.BlockSpec(memory_space=pltpu.VMEM)] * len(shapes),
        scratch_shapes=[pltpu.VMEM(shape, dtype) for shape, dtype in scratch],
        cost_estimate=pl.CostEstimate(flops=cost or 1000, bytes_accessed=moved, transcendentals=0),
    )(*args)


def swap(pieces):
    return [pieces[0]] + [
        lax.ppermute(pieces[step], "j", [(i, (i + step) % GROUP) for i in range(GROUP)]) for step in range(1, GROUP)
    ]


def shards(query_proj, key_proj, value_proj, filters, cotangent, stock_id, stock_class, cond_table):
    groups = lax.axis_size("g")
    parts = lax.axis_size("ch")
    lag_rows = filters.shape[0]
    wide = GROUP * LANES
    place = lax.axis_index("j").astype(jnp.int32)[None]
    forward_high, forward_low, inverse_high, inverse_low = (jnp.asarray(t) for t in transform_tables())
    forward, inverse = (forward_high, forward_low), (inverse_high, inverse_low)

    (sent,) = call(pack_mixed, [((GROUP, LEN + lag_rows, LANES), BF16)], key_proj, value_proj, filters)
    got = lax.all_to_all(sent, "j", 0, 0)
    gates = call(
        pack_gates, [((2 * LEN + 16, LANES), BF16)] * GROUP, place, query_proj, cotangent, stock_id[None, :],
        stock_class[None, :], scalars=1,
    )
    lags = got[:, LEN:, :].reshape(1, GROUP * lag_rows, LANES)
    lags = lax.all_to_all(jnp.broadcast_to(lags, (groups, *lags.shape[1:])), "g", 0, 0)
    before = lax.ppermute(got[GROUP - REACH :, :LEN, :], "g", [(i, i + 1) for i in range(groups - 1)])
    gates = swap(gates)
    (own,) = call(own_spectra, [((2 * LEN, wide), F32)], got, *forward, cost=2 * 4 * LEN * LEN * wide)
    table = jnp.pad(cond_table, ((0, 16 - cond_table.shape[0]), (0, 0)))
    gate, factor, upstream = call(
        unpack_gates, [((LEN, wide), F32), ((LEN, wide), F32), ((LEN, wide), BF16)], place, table, *gates, scalars=1
    )
    conv, before_spec, lag_spec, sums = call(
        convolve,
        [((LEN, wide), F32), ((2 * LEN, wide // 2), F32), ((2 * LEN, wide // 2), F32), ((GROUP * parts, 8, 2 * LEN), F32)],
        own, before, lags.reshape(REACH * LEN, LANES), gate, upstream, *forward, *inverse,
        scratch=[((2 * LEN, wide), F32)], cost=2 * 10 * LEN * LEN * wide,
    )
    sums = lax.all_to_all(sums, ("j", "ch"), 0, 0)
    results = call(
        functools.partial(finish_norm, wide * parts),
        [((LEN, wide), BF16), ((LEN, wide // 2), BF16)] + [((2 * LEN, LANES), BF16)] * GROUP,
        place, sums, conv, gate, factor, upstream, scalars=1, scratch=[((2 * LEN, wide), BF16)],
    )
    grad_conv, first, both = results[0], results[1], results[2:]
    after = lax.ppermute(first, "g", [(i, i - 1) for i in range(1, groups)])
    grad_spec, terms = call(
        filter_terms, [((2 * LEN, wide), F32), ((groups * GROUP, lag_rows, LANES), F32)], grad_conv, own, before_spec,
        *forward, *inverse, scratch=[((2 * LEN, wide // 2), F32)], cost=2 * 7 * LEN * LEN * wide,
    )
    terms = lax.all_to_all(terms, ("g", "j"), 0, 0)
    both = swap(both)
    mixed = call(
        correlate_back, [((LEN, LANES), BF16)] * GROUP, place, grad_spec, after, lag_spec, *forward, *inverse, scalars=1,
        scratch=[((2 * LEN, wide // 2), F32), ((2 * LEN, wide), F32), ((LEN, wide), BF16)],
        cost=2 * 8 * LEN * LEN * wide,
    )
    mixed = swap(mixed)
    normed_out, grad_query = call(finish_forward, [((LEN, wide), BF16)] * 2, place, *both, scalars=1)
    grad_key, grad_value = call(
        finish_backward, [((LEN, wide), BF16)] * 2, place, key_proj, value_proj, *mixed, scalars=1
    )
    (grad_filter,) = call(sum_terms, [((lag_rows, wide), F32)], terms)
    return normed_out, grad_query, grad_key, grad_value, grad_filter


def solution(mesh):
    ctx, ch = mesh.devices.shape
    inner = Mesh(mesh.devices.reshape(ctx // GROUP, GROUP, ch), ("g", "j", "ch"))
    rows = ("g", "j")
    return jax.shard_map(
        shards,
        mesh=inner,
        in_specs=(P(rows, "ch"),) * 5 + (P(rows), P(), P(None, "ch")),
        out_specs=(P(rows, "ch"),) * 5,
        check_vma=False,
    )
```

time: 868 us -> 146 us (0.17)
  the two profiles are of different devices: /device:TPU:1 before, /device:TPU:3 now
where the time goes in v1:
time: 146 us; the launch traced here: 145 us
  starting transfers between devices  53.4 us (37%)
  Pallas kernels  41.3 us (28%)
  blocking collectives  29 us (20%)
  waiting for transfers between devices  16.3 us (11%)
  local copies, waits for them, and re-layouts  4.45 us (3%)
    pallas_call x11, Pallas kernels, call(): pl.pallas_call(body, out_shape=shapes, in_specs=specs, out_specs=[pl.Bloc...  41.3 us
    ppermute x21, starting transfers between devices, swap(): lax.ppermute(pieces[step], 'j', [(i, (i + step) % GROUP) for i in range(G...  28.6 us
    all_to_all x1, blocking collectives, shards(): got = lax.all_to_all(sent, 'j', 0, 0)  15.4 us
    ppermute x21, waiting for transfers between devices, swap(): lax.ppermute(pieces[step], 'j', [(i, (i + step) % GROUP) for i in range(G...  14.7 us
    all_to_all x1, blocking collectives, shards(): sums = lax.all_to_all(sums, ('j', 'ch'), 0, 0)  13.7 us
    all_to_all x1, starting transfers between devices, shards(): terms = lax.all_to_all(terms, ('g', 'j'), 0, 0)  10.3 us
    all_to_all x1, starting transfers between devices, shards(): lax.all_to_all(jnp.broadcast_to(lags, (groups, *lags.shape[1:])), 'g', 0, 0)  9.38 us
    ppermute x1, starting transfers between devices, shards(): lax.ppermute(got[GROUP - REACH:, :LEN, :], 'g', [(i, i + 1) for i in rang...  3.09 us
  transfers between devices with their start and end apart: 25, of which 8 were waited for; matrix products, arithmetic and copies ran while one was open for 0% of the time, Pallas kernels for 14%

profile of v1, /device:TPU:3, one launch (start us, length us, event | category | flops | bytes accessed | tf_op | source)
XLA Modules:
  0.0 145.5 jit_solution(1345169949111326604)
XLA Ops:
  0.6 2.2 %shard_map.155 = bf16[8,264,128]{2,1,0:T(8,128)(2,1)} custom-call(bf16[256,1024]{1,0:T(8,128)(2,1)} %key_ref.3, bf16[256,1024]{1,0:T(8,128)(2,1)} %value_ref.3, bf16[8,1024]{1,0:T(8,128)(2,1)} %filters_ref.1), custom_call_target="tpu_custom_call" | custom-call | flops 1000 | bytes 1605632 | tf_op jit(solution)/shard_map/pallas_call | solution.py:298
  2.8 15.4 %all_to_all.20.mixed_ref = bf16[8,264,128]{2,1,0:T(8,128)(2,1)S(1)} all-to-all(bf16[8,264,128]{2,1,0:T(8,128)(2,1)} %shard_map.155), channel_id=1, replica_groups=mesh['g'=16,'j'=8,'ch'=2] {'j'}, dimensions={0} | all-to-all | bytes 1081344 | tf_op jit(solution)/shard_map/all_to_all | solution.py:324
  19.0 9.4 %all-to-all-start.1 = ((bf16[16,64,128]{2,1,0:T(8,128)(2,1)}), bf16[16,64,128]{2,1,0:T(8,128)(2,1)S(1)}, u32[]{:S(2)}, u32[]{:S(2)}) async-start(bf16[16,64,128]{2,1,0:T(8,128)(2,1)} %broadcast_in_dim.18), calls=%async_computation.1 | async-start | bytes 524288 | tf_op jit(solution)/shard_map/all_to_all | solution.py:330
  28.4 2.4 %shard_map.157 = (bf16[528,128]{1,0:T(8,128)(2,1)}, bf16[528,128]{1,0:T(8,128)(2,1)}, bf16[528,128]{1,0:T(8,128)(2,1)}, bf16[528,128]{1,0:T(8,128)(2,1)}, bf16[5...) custom-call(s32[1]{0:T(128)} %bitcast.place_ref, ...), custom_call_target="tpu_custom_call" | custom-call | flops 1000 | bytes 2132996 | tf_op jit(solution)/shard_map/pallas_call | solution.py:298
  32.2 1.9 %collective-permute-start.3 = (bf16[528,128]{1,0:T(8,128)(2,1)}, bf16[528,128]{1,0:T(8,128)(2,1)S(1)}, u32[]{:S(2)}, u32[]{:S(2)}) collective-permute-start(bf16[528,128]{1,0:T(8,128)(2,1)} %get-tuple-element.47), channel_id=1, source_target_pairs={{0,6},{2,8},{4,10},{6,12},{8,14},{10,0},{12,2},{14,4},{1,7},{3,9},... | collective-permute-start | bytes 405512 | tf_op jit(solution)/shard_map/ppermute | solution.py:310
  34.1 3.1 %collective-permute-start = (bf16[4,256,128]{2,1,0:T(8,128)(2,1)S(1)}, bf16[4,256,128]{2,1,0:T(8,128)(2,1)S(1)}, u32[]{:S(2)}, u32[]{:S(2)}) collective-permute-start(bf16[4,256,128]{2,1,0:T(8,128)(2,1)S(1)} %slice.8), channel_id=1, source_target_pairs={{0,16},{16,32},{32,48},{48,64},{64,80},{80,96},{96,112},{112,128},... | collective-permute-start | bytes 786440 | tf_op jit(solution)/shard_map/ppermute | solution.py:331
  38.8 2.9 %collective-permute-start.5 = (bf16[528,128]{1,0:T(8,128)(2,1)}, bf16[528,128]{1,0:T(8,128)(2,1)S(1)}, u32[]{:S(2)}, u32[]{:S(2)}) collective-permute-start(bf16[528,128]{1,0:T(8,128)(2,1)} %get-tuple-element.49), channel_id=1, source_target_pairs={{0,10},{2,12},{4,14},{6,0},{8,2},{10,4},{12,6},{14,8},{1,11},{3,13... | collective-permute-start | bytes 405512 | tf_op jit(solution)/shard_map/ppermute | solution.py:310
  41.7 5.4 %collective-permute-done.3.refs_3_ = bf16[528,128]{1,0:T(8,128)(2,1)S(1)} collective-permute-done((bf16[528,128]{1,0:T(8,128)(2,1)}, bf16[528,128]{1,0:T(8,128)(2,1)S(1)}, u32[]{:S(2)}, u32[]{:S(2)}) %collective-permute-start.3) | collective-permute-done | bytes 135200 | tf_op jit(solution)/shard_map/ppermute | solution.py:310
  49.5 2.3 %collective-permute-done.7.refs_7_ = bf16[528,128]{1,0:T(8,128)(2,1)S(1)} collective-permute-done((bf16[528,128]{1,0:T(8,128)(2,1)}, bf16[528,128]{1,0:T(8,128)(2,1)S(1)}, u32[]{:S(2)}, u32[]{:S(2)}) %collective-permute-start.7) | collective-permute-done | bytes 135200 | tf_op jit(solution)/shard_map/ppermute | solution.py:310
  52.4 3.5 %shard_map.158 = (f32[256,1024]{1,0:T(8,128)}, f32[256,1024]{1,0:T(8,128)}, bf16[256,1024]{1,0:T(8,128)(2,1)}) custom-call(s32[1]{0:T(128)} %bitcast.place_ref, f32[16,1024]{1,0:T(8,128)} %pad.4.table_ref, bf16[528,128]{1,0:T(8,128)(2,1)} %get-tuple-element.44.refs_0_, bf16[528,128]{1,0:T(8,128)(2,1)} %copy-done.5, bf16[528,128]{1,0:T(8,128)(2,1)} %copy-done.6, ...), custom_call_target="tpu_custom_call" | custom-call | flops 1000 | bytes 3768324 | tf_op jit(solution)/shard_map/pallas_call | solution.py:298
  56.0 3.2 %shard_map.156.own_ref = f32[512,1024]{1,0:T(8,128)} custom-call(bf16[8,264,128]{2,1,0:T(8,128)(2,1)} %copy-done, bf16[512,256]{1,0:T(8,128)(2,1)} %constant.17.clone.forward_high, bf16[512,256]{1,0:T(8,128)(2,1)} %constant.18.clone.forward_low), custom_call_target="tpu_custom_call" | custom-call | flops 536870912 | bytes 3162112 | tf_op jit(solution)/shard_map/pallas_call | solution.py:298
  60.0 7.0 %shard_map.159 = (f32[256,1024]{1,0:T(8,128)}, f32[512,512]{1,0:T(8,128)}, f32[512,512]{1,0:T(8,128)}, f32[16,8,512]{2,1,0:T(8,128)}) custom-call(f32[512,1024]{1,0:T(8,128)} %shard_map.156.own_ref, bf16[4,256,128]{2,1,0:T(8,128)(2,1)} %copy-done.3, bf16[1024,128]{1,0:T(8,128)(2,1)} %bitcast.6, f32[256,1024]{1,0:T(8,128)} %get-tuple-element.52.gate_ref, ...), custom_call_target="tpu_custom_call" | custom-call | flops 1342177280 | bytes 8650752 | tf_op jit(solution)/shard_map/pallas_call | solution.py:298
  67.0 13.7 %all_to_all.21.sums_ref = f32[16,8,512]{2,1,0:T(8,128)} all-to-all(f32[16,8,512]{2,1,0:T(8,128)} %get-tuple-element.54), channel_id=1, replica_groups=mesh['g'=16,'j'=8,'ch'=2] {'j','ch'}, dimensions={0} | all-to-all | bytes 524288 | tf_op jit(solution)/shard_map/all_to_all | solution.py:344
  80.6 4.4 %shard_map.160 = (bf16[256,1024]{1,0:T(8,128)(2,1)}, bf16[256,512]{1,0:T(8,128)(2,1)}, bf16[512,128]{1,0:T(8,128)(2,1)}, bf16[512,128]{1,0:T(8,128)(2,1)}, bf16[...) custom-call(s32[1]{0:T(128)} %bitcast.place_ref, ...), custom_call_target="tpu_custom_call" | custom-call | flops 1000 | bytes 5767172 | tf_op jit(solution)/shard_map/pallas_call | solution.py:298
  85.1 6.0 %shard_map.162 = (f32[512,1024]{1,0:T(8,128)}, f32[128,8,128]{2,1,0:T(8,128)}) custom-call(bf16[256,1024]{1,0:T(8,128)(2,1)} %get-tuple-element.67.grad_ref, f32[512,1024]{1,0:T(8,128)} %shard_map.156.own_ref, f32[512,512]{1,0:T(8,128)} %get-tuple-element.68.before_ref, bf16[512,256]{1,0:T(8,128)(2,1)} %constant.17.clone.forward_high, ...), custom_call_target="tpu_custom_call" | custom-call | flops 939524096 | bytes 7340032 | tf_op jit(solution)/shard_map/pallas_call | solution.py:298
  91.0 10.3 %all-to-all-start.3 = ((f32[128,8,128]{2,1,0:T(8,128)}), f32[128,8,128]{2,1,0:T(8,128)S(1)}, u32[]{:S(2)}, u32[]{:S(2)}) async-start(f32[128,8,128]{2,1,0:T(8,128)} %get-tuple-element.82), calls=%async_computation.3 | async-start | bytes 1048576 | tf_op jit(solution)/shard_map/all_to_all | solution.py:356
  101.4 2.0 %collective-permute-start.15 = (bf16[256,512]{1,0:T(8,128)(2,1)S(1)}, bf16[256,512]{1,0:T(8,128)(2,1)S(1)}, u32[]{:S(2)}, u32[]{:S(2)}) collective-permute-start(bf16[256,512]{1,0:T(8,128)(2,1)S(1)} %copy-done.27), channel_id=1, source_target_pairs={{16,0},{32,16},{48,32},{64,48},{80,64},{96,80},{112,96},{128,112},... | collective-permute-start | bytes 786440 | tf_op jit(solution)/shard_map/ppermute | solution.py:351
  103.4 1.9 %collective-permute-start.8 = (bf16[512,128]{1,0:T(8,128)(2,1)S(1)}, bf16[512,128]{1,0:T(8,128)(2,1)S(1)}, u32[]{:S(2)}, u32[]{:S(2)}) collective-permute-start(bf16[512,128]{1,0:T(8,128)(2,1)S(1)} %copy-done.34), channel_id=1, source_target_pairs={{0,2},{2,4},{4,6},{6,8},{8,10},{10,12},{12,14},{14,0},{1,3},{3,5},... | collective-permute-start | bytes 393224 | tf_op jit(solution)/shard_map/ppermute | solution.py:310
  109.8 4.5 %collective-permute-start.12 = (bf16[512,128]{1,0:T(8,128)(2,1)S(1)}, bf16[512,128]{1,0:T(8,128)(2,1)S(1)}, u32[]{:S(2)}, u32[]{:S(2)}) collective-permute-start(bf16[512,128]{1,0:T(8,128)(2,1)S(1)} %copy-done.30), channel_id=1, source_target_pairs={{0,10},{2,12},{4,14},{6,0},{8,2},{10,4},{12,6},{14,8},{1,11},{3,13... | collective-permute-start | bytes 393224 | tf_op jit(solution)/shard_map/ppermute | solution.py:310
  114.2 3.2 %collective-permute-done.9.refs_2_ = bf16[512,128]{1,0:T(8,128)(2,1)S(1)} collective-permute-done((bf16[512,128]{1,0:T(8,128)(2,1)S(1)}, bf16[512,128]{1,0:T(8,128)(2,1)S(1)}, u32[]{:S(2)}, u32[]{:S(2)}) %collective-permute-start.9) | collective-permute-done | bytes 131104 | tf_op jit(solution)/shard_map/ppermute | solution.py:310
  120.8 5.9 %shard_map.163 = (bf16[256,128]{1,0:T(8,128)(2,1)}, bf16[256,128]{1,0:T(8,128)(2,1)}, bf16[256,128]{1,0:T(8,128)(2,1)}, bf16[256,128]{1,0:T(8,128)(2,1)}, bf16[2...) custom-call(s32[1]{0:T(128)} %bitcast.place_ref, ...), custom_call_target="tpu_custom_call" | custom-call | flops 1073741824 | bytes 4980740 | tf_op jit(solution)/shard_map/pallas_call | solution.py:298
  132.5 2.5 %collective-permute-start.20 = (bf16[256,128]{1,0:T(8,128)(2,1)}, bf16[256,128]{1,0:T(8,128)(2,1)S(1)}, u32[]{:S(2)}, u32[]{:S(2)}) collective-permute-start(bf16[256,128]{1,0:T(8,128)(2,1)} %get-tuple-element.77), channel_id=1, source_target_pairs={{0,10},{2,12},{4,14},{6,0},{8,2},{10,4},{12,6},{14,8},{1,11},{3,13... | collective-permute-start | bytes 196616 | tf_op jit(solution)/shard_map/ppermute | solution.py:310
  136.2 2.6 %shard_map.161 = (bf16[256,1024]{1,0:T(8,128)(2,1)}, bf16[256,1024]{1,0:T(8,128)(2,1)}) custom-call(s32[1]{0:T(128)} %bitcast.place_ref, bf16[512,128]{1,0:T(8,128)(2,1)} %get-tuple-element.57.refs_0_, bf16[512,128]{1,0:T(8,128)(2,1)} %copy-done.12, bf16[512,128]{1,0:T(8,128)(2,1)} %copy-done.13, bf16[512,128]{1,0:T(8,128)(2,1)} %copy-done.14, ...), custom_call_target="tpu_custom_call" | custom-call | flops 1000 | bytes 2097156 | tf_op jit(solution)/shard_map/pallas_call | solution.py:298
  140.4 2.5 %shard_map.164 = (bf16[256,1024]{1,0:T(8,128)(2,1)}, bf16[256,1024]{1,0:T(8,128)(2,1)}) custom-call(s32[1]{0:T(128)} %bitcast.place_ref, bf16[256,1024]{1,0:T(8,128)(2,1)} %key_ref.3, bf16[256,1024]{1,0:T(8,128)(2,1)} %value_ref.3, bf16[256,128]{1,0:T(8,128)(2,1)} %get-tuple-element.72.refs_0_, bf16[256,128]{1,0:T(8,128)(2,1)} %copy-done.19, ...), custom_call_target="tpu_custom_call" | custom-call | flops 1000 | bytes 2621444 | tf_op jit(solution)/shard_map/pallas_call | solution.py:298
  (113 shorter events, 26.4 us)
Async XLA Ops:
  19.0 40.2 %all-to-all-start.1 = ((bf16[16,64,128]{2,1,0:T(8,128)(2,1)}), bf16[16,64,128]{2,1,0:T(8,128)(2,1)S(1)}, u32[]{:S(2)}, u32[]{:S(2)}) async-start(bf16[16,64,128]{2,1,0:T(8,128)(2,1)} %broadcast_in_dim.18), calls=%async_computation.1 | async-start | bytes 524288 | tf_op jit(solution)/shard_map/all_to_all | solution.py:330
  30.8 8.0 %collective-permute-start.1 = (bf16[528,128]{1,0:T(8,128)(2,1)}, bf16[528,128]{1,0:T(8,128)(2,1)S(1)}, u32[]{:S(2)}, u32[]{:S(2)}) collective-permute-start(bf16[528,128]{1,0:T(8,128)(2,1)} %get-tuple-element.45), channel_id=1, source_target_pairs={{0,2},{2,4},{4,6},{6,8},{8,10},{10,12},{12,14},{14,0},{1,3},{3,5},... | collective-permute-start | bytes 405512 | tf_op jit(solution)/shard_map/ppermute | solution.py:310
  32.0 9.7 %collective-permute-start.2 = (bf16[528,128]{1,0:T(8,128)(2,1)}, bf16[528,128]{1,0:T(8,128)(2,1)S(1)}, u32[]{:S(2)}, u32[]{:S(2)}) collective-permute-start(bf16[528,128]{1,0:T(8,128)(2,1)} %get-tuple-element.46), channel_id=1, source_target_pairs={{0,4},{2,6},{4,8},{6,10},{8,12},{10,14},{12,0},{14,2},{1,5},{3,7},... | collective-permute-start | bytes 405512 | tf_op jit(solution)/shard_map/ppermute | solution.py:310
  32.2 14.9 %collective-permute-start.3 = (bf16[528,128]{1,0:T(8,128)(2,1)}, bf16[528,128]{1,0:T(8,128)(2,1)S(1)}, u32[]{:S(2)}, u32[]{:S(2)}) collective-permute-start(bf16[528,128]{1,0:T(8,128)(2,1)} %get-tuple-element.47), channel_id=1, source_target_pairs={{0,6},{2,8},{4,10},{6,12},{8,14},{10,0},{12,2},{14,4},{1,7},{3,9},... | collective-permute-start | bytes 405512 | tf_op jit(solution)/shard_map/ppermute | solution.py:310
  34.1 25.1 %collective-permute-start = (bf16[4,256,128]{2,1,0:T(8,128)(2,1)S(1)}, bf16[4,256,128]{2,1,0:T(8,128)(2,1)S(1)}, u32[]{:S(2)}, u32[]{:S(2)}) collective-permute-start(bf16[4,256,128]{2,1,0:T(8,128)(2,1)S(1)} %slice.8), channel_id=1, source_target_pairs={{0,16},{16,32},{32,48},{48,64},{64,80},{80,96},{96,112},{112,128},... | collective-permute-start | bytes 786440 | tf_op jit(solution)/shard_map/ppermute | solution.py:331
  37.2 10.6 %collective-permute-start.4 = (bf16[528,128]{1,0:T(8,128)(2,1)}, bf16[528,128]{1,0:T(8,128)(2,1)S(1)}, u32[]{:S(2)}, u32[]{:S(2)}) collective-permute-start(bf16[528,128]{1,0:T(8,128)(2,1)} %get-tuple-element.48), channel_id=1, source_target_pairs={{0,8},{2,10},{4,12},{6,14},{8,0},{10,2},{12,4},{14,6},{1,9},{3,11}... | collective-permute-start | bytes 405512 | tf_op jit(solution)/shard_map/ppermute | solution.py:310
  38.8 9.0 %collective-permute-start.5 = (bf16[528,128]{1,0:T(8,128)(2,1)}, bf16[528,128]{1,0:T(8,128)(2,1)S(1)}, u32[]{:S(2)}, u32[]{:S(2)}) collective-permute-start(bf16[528,128]{1,0:T(8,128)(2,1)} %get-tuple-element.49), channel_id=1, source_target_pairs={{0,10},{2,12},{4,14},{6,0},{8,2},{10,4},{12,6},{14,8},{1,11},{3,13... | collective-permute-start | bytes 405512 | tf_op jit(solution)/shard_map/ppermute | solution.py:310
  41.7 7.8 %collective-permute-start.6 = (bf16[528,128]{1,0:T(8,128)(2,1)}, bf16[528,128]{1,0:T(8,128)(2,1)S(1)}, u32[]{:S(2)}, u32[]{:S(2)}) collective-permute-start(bf16[528,128]{1,0:T(8,128)(2,1)} %get-tuple-element.50), channel_id=1, source_target_pairs={{0,12},{2,14},{4,0},{6,2},{8,4},{10,6},{12,8},{14,10},{1,13},{3,15... | collective-permute-start | bytes 405512 | tf_op jit(solution)/shard_map/ppermute | solution.py:310
  47.1 4.6 %collective-permute-start.7 = (bf16[528,128]{1,0:T(8,128)(2,1)}, bf16[528,128]{1,0:T(8,128)(2,1)S(1)}, u32[]{:S(2)}, u32[]{:S(2)}) collective-permute-start(bf16[528,128]{1,0:T(8,128)(2,1)} %get-tuple-element.51), channel_id=1, source_target_pairs={{0,14},{2,0},{4,2},{6,4},{8,6},{10,8},{12,10},{14,12},{1,15},{3,1}... | collective-permute-start | bytes 405512 | tf_op jit(solution)/shard_map/ppermute | solution.py:310
  91.0 52.0 %all-to-all-start.3 = ((f32[128,8,128]{2,1,0:T(8,128)}), f32[128,8,128]{2,1,0:T(8,128)S(1)}, u32[]{:S(2)}, u32[]{:S(2)}) async-start(f32[128,8,128]{2,1,0:T(8,128)} %get-tuple-element.82), calls=%async_computation.3 | async-start | bytes 1048576 | tf_op jit(solution)/shard_map/all_to_all | solution.py:356
  101.4 18.5 %collective-permute-start.15 = (bf16[256,512]{1,0:T(8,128)(2,1)S(1)}, bf16[256,512]{1,0:T(8,128)(2,1)S(1)}, u32[]{:S(2)}, u32[]{:S(2)}) collective-permute-start(bf16[256,512]{1,0:T(8,128)(2,1)S(1)} %copy-done.27), channel_id=1, source_target_pairs={{16,0},{32,16},{48,32},{64,48},{80,64},{96,80},{112,96},{128,112},... | collective-permute-start | bytes 786440 | tf_op jit(solution)/shard_map/ppermute | solution.py:351
  103.4 6.4 %collective-permute-start.8 = (bf16[512,128]{1,0:T(8,128)(2,1)S(1)}, bf16[512,128]{1,0:T(8,128)(2,1)S(1)}, u32[]{:S(2)}, u32[]{:S(2)}) collective-permute-start(bf16[512,128]{1,0:T(8,128)(2,1)S(1)} %copy-done.34), channel_id=1, source_target_pairs={{0,2},{2,4},{4,6},{6,8},{8,10},{10,12},{12,14},{14,0},{1,3},{3,5},... | collective-permute-start | bytes 393224 | tf_op jit(solution)/shard_map/ppermute | solution.py:310
  105.3 12.1 %collective-permute-start.9 = (bf16[512,128]{1,0:T(8,128)(2,1)S(1)}, bf16[512,128]{1,0:T(8,128)(2,1)S(1)}, u32[]{:S(2)}, u32[]{:S(2)}) collective-permute-start(bf16[512,128]{1,0:T(8,128)(2,1)S(1)} %copy-done.33), channel_id=1, source_target_pairs={{0,4},{2,6},{4,8},{6,10},{8,12},{10,14},{12,0},{14,2},{1,5},{3,7},... | collective-permute-start | bytes 393224 | tf_op jit(solution)/shard_map/ppermute | solution.py:310
  106.5 20.2 %collective-permute-start.10 = (bf16[512,128]{1,0:T(8,128)(2,1)S(1)}, bf16[512,128]{1,0:T(8,128)(2,1)S(1)}, u32[]{:S(2)}, u32[]{:S(2)}) collective-permute-start(bf16[512,128]{1,0:T(8,128)(2,1)S(1)} %copy-done.32), channel_id=1, source_target_pairs={{0,6},{2,8},{4,10},{6,12},{8,14},{10,0},{12,2},{14,4},{1,7},{3,9},... | collective-permute-start | bytes 393224 | tf_op jit(solution)/shard_map/ppermute | solution.py:310
  108.1 20.5 %collective-permute-start.11 = (bf16[512,128]{1,0:T(8,128)(2,1)S(1)}, bf16[512,128]{1,0:T(8,128)(2,1)S(1)}, u32[]{:S(2)}, u32[]{:S(2)}) collective-permute-start(bf16[512,128]{1,0:T(8,128)(2,1)S(1)} %copy-done.31), channel_id=1, source_target_pairs={{0,8},{2,10},{4,12},{6,14},{8,0},{10,2},{12,4},{14,6},{1,9},{3,11}... | collective-permute-start | bytes 393224 | tf_op jit(solution)/shard_map/ppermute | solution.py:310
  109.8 19.9 %collective-permute-start.12 = (bf16[512,128]{1,0:T(8,128)(2,1)S(1)}, bf16[512,128]{1,0:T(8,128)(2,1)S(1)}, u32[]{:S(2)}, u32[]{:S(2)}) collective-permute-start(bf16[512,128]{1,0:T(8,128)(2,1)S(1)} %copy-done.30), channel_id=1, source_target_pairs={{0,10},{2,12},{4,14},{6,0},{8,2},{10,4},{12,6},{14,8},{1,11},{3,13... | collective-permute-start | bytes 393224 | tf_op jit(solution)/shard_map/ppermute | solution.py:310
  117.5 13.9 %collective-permute-start.13 = (bf16[512,128]{1,0:T(8,128)(2,1)S(1)}, bf16[512,128]{1,0:T(8,128)(2,1)S(1)}, u32[]{:S(2)}, u32[]{:S(2)}) collective-permute-start(bf16[512,128]{1,0:T(8,128)(2,1)S(1)} %copy-done.29), channel_id=1, source_target_pairs={{0,12},{2,14},{4,0},{6,2},{8,4},{10,6},{12,8},{14,10},{1,13},{3,15... | collective-permute-start | bytes 393224 | tf_op jit(solution)/shard_map/ppermute | solution.py:310
  119.8 12.7 %collective-permute-start.14 = (bf16[512,128]{1,0:T(8,128)(2,1)S(1)}, bf16[512,128]{1,0:T(8,128)(2,1)S(1)}, u32[]{:S(2)}, u32[]{:S(2)}) collective-permute-start(bf16[512,128]{1,0:T(8,128)(2,1)S(1)} %copy-done.28), channel_id=1, source_target_pairs={{0,14},{2,0},{4,2},{6,4},{8,6},{10,8},{12,10},{14,12},{1,15},{3,1}... | collective-permute-start | bytes 393224 | tf_op jit(solution)/shard_map/ppermute | solution.py:310
  126.7 8.3 %collective-permute-start.16 = (bf16[256,128]{1,0:T(8,128)(2,1)}, bf16[256,128]{1,0:T(8,128)(2,1)S(1)}, u32[]{:S(2)}, u32[]{:S(2)}) collective-permute-start(bf16[256,128]{1,0:T(8,128)(2,1)} %get-tuple-element.73), channel_id=1, source_target_pairs={{0,2},{2,4},{4,6},{6,8},{8,10},{10,12},{12,14},{14,0},{1,3},{3,5},... | collective-permute-start | bytes 196616 | tf_op jit(solution)/shard_map/ppermute | solution.py:310
  128.6 6.5 %collective-permute-start.17 = (bf16[256,128]{1,0:T(8,128)(2,1)}, bf16[256,128]{1,0:T(8,128)(2,1)S(1)}, u32[]{:S(2)}, u32[]{:S(2)}) collective-permute-start(bf16[256,128]{1,0:T(8,128)(2,1)} %get-tuple-element.74), channel_id=1, source_target_pairs={{0,4},{2,6},{4,8},{6,10},{8,12},{10,14},{12,0},{14,2},{1,5},{3,7},... | collective-permute-start | bytes 196616 | tf_op jit(solution)/shard_map/ppermute | solution.py:310
  129.7 9.1 %collective-permute-start.18 = (bf16[256,128]{1,0:T(8,128)(2,1)}, bf16[256,128]{1,0:T(8,128)(2,1)S(1)}, u32[]{:S(2)}, u32[]{:S(2)}) collective-permute-start(bf16[256,128]{1,0:T(8,128)(2,1)} %get-tuple-element.75), channel_id=1, source_target_pairs={{0,6},{2,8},{4,10},{6,12},{8,14},{10,0},{12,2},{14,4},{1,7},{3,9},... | collective-permute-start | bytes 196616 | tf_op jit(solution)/shard_map/ppermute | solution.py:310
  131.4 7.4 %collective-permute-start.19 = (bf16[256,128]{1,0:T(8,128)(2,1)}, bf16[256,128]{1,0:T(8,128)(2,1)S(1)}, u32[]{:S(2)}, u32[]{:S(2)}) collective-permute-start(bf16[256,128]{1,0:T(8,128)(2,1)} %get-tuple-element.76), channel_id=1, source_target_pairs={{0,8},{2,10},{4,12},{6,14},{8,0},{10,2},{12,4},{14,6},{1,9},{3,11}... | collective-permute-start | bytes 196616 | tf_op jit(solution)/shard_map/ppermute | solution.py:310
  132.5 6.3 %collective-permute-start.20 = (bf16[256,128]{1,0:T(8,128)(2,1)}, bf16[256,128]{1,0:T(8,128)(2,1)S(1)}, u32[]{:S(2)}, u32[]{:S(2)}) collective-permute-start(bf16[256,128]{1,0:T(8,128)(2,1)} %get-tuple-element.77), channel_id=1, source_target_pairs={{0,10},{2,12},{4,14},{6,0},{8,2},{10,4},{12,6},{14,8},{1,11},{3,13... | collective-permute-start | bytes 196616 | tf_op jit(solution)/shard_map/ppermute | solution.py:310
  135.1 4.7 %collective-permute-start.22 = (bf16[256,128]{1,0:T(8,128)(2,1)}, bf16[256,128]{1,0:T(8,128)(2,1)S(1)}, u32[]{:S(2)}, u32[]{:S(2)}) collective-permute-start(bf16[256,128]{1,0:T(8,128)(2,1)} %get-tuple-element.79), channel_id=1, source_target_pairs={{0,14},{2,0},{4,2},{6,4},{8,6},{10,8},{12,10},{14,12},{1,15},{3,1}... | collective-permute-start | bytes 196616 | tf_op jit(solution)/shard_map/ppermute | solution.py:310
  (36 other events, 410.7 us)

commit v2 on v1

v2 whole, which is shorter than its diff:
```python
import functools

import jax
import jax.numpy as jnp
import numpy as np
import ml_dtypes
from jax import lax
from jax.experimental import pallas as pl
from jax.experimental.pallas import tpu as pltpu
from jax.sharding import Mesh, PartitionSpec as P

GROUP = 8
REACH = 4
LEN = 256
LANES = 128
EPSILON = 1e-05
F32 = jnp.float32
BF16 = jnp.bfloat16


def split_table(table):
    high = table.astype(np.float32).astype(ml_dtypes.bfloat16)
    low = (table - high.astype(np.float64)).astype(ml_dtypes.bfloat16)
    return high, low


def transform_tables():
    number = np.concatenate([np.arange(0, LEN, 2), np.arange(1, LEN, 2)])
    angles = np.pi * ((2 * number[:, None] + 1) * np.arange(LEN)[None, :] % (4 * LEN)) / (2 * LEN)
    forward = np.concatenate([np.cos(angles), -np.sin(angles)], axis=0)
    return (*split_table(forward), *split_table(forward.T / LEN))


def dot(left, right):
    return jnp.dot(left, right, preferred_element_type=F32)


def halves(value):
    high = value.astype(BF16)
    return high, (value - high.astype(F32)).astype(BF16)


def lane(index):
    return pl.ds(pl.multiple_of(index * LANES, LANES), LANES)


def col(index):
    return slice(index * LANES, (index + 1) * LANES)


def event_classes(stock_ref, class_ref):
    stocks = class_ref.shape[1]
    hits = (lax.broadcasted_iota(jnp.int32, (stocks, LEN), 0) == stock_ref[...]).astype(F32).astype(BF16)
    classes = jnp.broadcast_to(class_ref[...].astype(F32), (8, stocks)).astype(BF16)
    return dot(classes, hits)


def modulation(event_class, table):
    high = table.astype(BF16)
    mid = (table - high.astype(F32)).astype(BF16)
    low = (table - high.astype(F32) - mid.astype(F32)).astype(BF16)
    number = lax.broadcasted_iota(jnp.int32, (table.shape[0], LEN), 0).astype(F32)
    hits = jnp.transpose((number == event_class).astype(F32)).astype(BF16)
    return 1.0 + (dot(hits, high) + dot(hits, mid) + dot(hits, low))


def copy_out(source, target, sem):
    copy = pltpu.make_async_copy(source, target, sem)
    copy.start()
    return copy


QUERY, UPSTREAM, CLASS, ROWS = LEN, 2 * LEN, 3 * LEN, 3 * LEN + 16


def pack(key_ref, value_ref, query_ref, cotangent_ref, stock_ref, class_ref, out_hbm, out_ref, sems):
    event_class = event_classes(stock_ref, class_ref).astype(BF16)
    copies = []
    for place in range(GROUP):
        product = key_ref[:, col(place)].astype(F32) * value_ref[:, col(place)].astype(F32)
        out_ref[place, :LEN, :] = product.astype(BF16)
        out_ref[place, QUERY:UPSTREAM, :] = query_ref[:, col(place)]
        out_ref[place, UPSTREAM:CLASS, :] = cotangent_ref[:, col(place)]
        out_ref[place, CLASS : CLASS + 8, :] = event_class[:, :LANES]
        out_ref[place, CLASS + 8 :, :] = event_class[:, LANES:]
        copies.append(copy_out(out_ref.at[place], out_hbm.at[place], sems.at[place]))
    for copy in copies:
        copy.wait()


def pack_lags(*refs):
    out_ref, first = refs[-1], 0
    for lags_ref in refs[:-1]:
        rows = lags_ref.shape[1]
        for high in range(lags_ref.shape[0]):
            for place in range(GROUP):
                out_ref[place, first : first + rows, :] = lags_ref[high, :, col(place)]
            first += rows


def spectrum(forward, rows):
    return dot(forward[0][...], rows) + dot(forward[1][...], rows)


def invert(inverse, spec):
    high, low = halves(spec)
    return dot(inverse[0][...], high) + (dot(inverse[0][...], low) + dot(inverse[1][...], high))


def over_frequencies(step):
    for half in range(2):
        @pl.loop(0, LEN // 16)
        def _(chunk):
            step(pl.multiple_of(half * (LEN // 2) + chunk * 8, 8), 1.0 - 2.0 * half)


def windows(real, imag, sign):
    pairs = {}
    for block in range(1, len(real)):
        pairs[block] = (real[block] - sign * imag[block - 1], imag[block] + sign * real[block - 1])
    return pairs


def read_blocks(own_ref, before_ref, row):
    real = [before_ref[pl.ds(row, 8), col(block)] for block in range(REACH)]
    real += [own_ref[pl.ds(row, 8), col(block)] for block in range(GROUP)]
    imag = [before_ref[pl.ds(row + LEN, 8), col(block)] for block in range(REACH)]
    imag += [own_ref[pl.ds(row + LEN, 8), col(block)] for block in range(GROUP)]
    return real, imag


def prepare(place_ref, table_ref, got_ref, forward_high, forward_low, own_out, gate_out, own_ref, gate_ref, sems):
    rows = jnp.concatenate([got_ref[b, :LEN, :] for b in range(GROUP)], axis=1)
    own_ref[...] = spectrum((forward_high, forward_low), rows)
    copies = [copy_out(own_ref, own_out, sems.at[0])]
    table = table_ref[:, lane(place_ref[0])]
    for block in range(GROUP):
        classes = got_ref[block, CLASS:, :].astype(F32)
        event_class = jnp.concatenate([classes[:1], classes[8:9]], axis=1)
        gate_ref[:, col(block)] = got_ref[block, QUERY:UPSTREAM, :].astype(F32) * modulation(event_class, table)
    copies.append(copy_out(gate_ref, gate_out, sems.at[1]))
    for copy in copies:
        copy.wait()


def convolve(near_groups, far_groups, place_ref, own_hbm, gate_hbm, got_hbm, before_ref, lags_ref, *refs):
    forward, inverse, outs = refs[:2], refs[2:4], refs[4:9]
    before_spec_ref, lag_spec_ref, conv_ref, rounded_ref, sums_ref = refs[9:14]
    own_ref, gate_ref, upstream_ref, product_ref, sorted_ref, sems = refs[14:]
    loads = [
        copy_out(own_hbm, own_ref, sems.at[0]),
        copy_out(gate_hbm, gate_ref, sems.at[1]),
        copy_out(got_hbm.at[:, UPSTREAM:CLASS, :], upstream_ref, sems.at[2]),
    ]
    group = place_ref[1]
    before_spec_ref[...] = spectrum(forward, jnp.concatenate([before_ref[b] for b in range(REACH)], axis=1))
    rows = lags_ref.shape[1] // (near_groups * far_groups)
    for low in range(near_groups):
        for high in range(far_groups):
            at = (low * far_groups + high) * rows
            first = (group ^ (high * near_groups + low)) * (GROUP * rows)
            row = pl.multiple_of(first & (LEN - 1), GROUP * rows)
            piece = lags_ref[:, at : at + rows, :].astype(F32).reshape(GROUP * rows, LANES)
            sorted_ref[pl.ds(row, GROUP * rows), lane(first // LEN)] = piece
    lag_spec_ref[...] = spectrum(forward, sorted_ref[...].astype(BF16))
    copies = [copy_out(before_spec_ref, outs[0], sems.at[3]), copy_out(lag_spec_ref, outs[1], sems.at[4])]
    loads[0].wait()

    def step(row, sign):
        real, imag = read_blocks(own_ref, before_spec_ref, row)
        pairs = windows(real, imag, sign)
        lag = [
            (lag_spec_ref[pl.ds(row, 8), col(d)], lag_spec_ref[pl.ds(row + LEN, 8), col(d)]) for d in range(REACH)
        ]
        for block in range(GROUP):
            total_real, total_imag = 0.0, 0.0
            for d in range(REACH):
                window = pairs[REACH + block - d]
                total_real += lag[d][0] * window[0] - lag[d][1] * window[1]
                total_imag += lag[d][0] * window[1] + lag[d][1] * window[0]
            product_ref[pl.ds(row, 8), col(block)] = total_real
            product_ref[pl.ds(row + LEN, 8), col(block)] = total_imag

    over_frequencies(step)
    conv = invert(inverse, product_ref[...])
    conv_ref[...] = conv
    rounded_ref[...] = conv.astype(BF16)
    copies += [copy_out(conv_ref, outs[2], sems.at[5]), copy_out(rounded_ref, outs[3], sems.at[6])]
    loads[1].wait()
    loads[2].wait()
    ones = jnp.ones((8, LANES), BF16)

    def channel_sum(value):
        contract = (((1,), (1,)), ((), ()))
        return sum(lax.dot_general(ones, part, contract, preferred_element_type=F32) for part in halves(value))[:1]

    lines = [[], []]
    for block in range(GROUP):
        scaled = gate_ref[:, col(block)] * conv[:, col(block)]
        lines[0].append(channel_sum(scaled * scaled))
        lines[1].append(channel_sum(scaled * upstream_ref[block].astype(F32)))
    for index in range(2):
        for pair in range(GROUP // 2):
            both = jnp.concatenate(lines[index][2 * pair : 2 * pair + 2], axis=1)
            line = index * (GROUP // 2) + pair
            for peer in range(sums_ref.shape[0]):
                sums_ref[peer, line : line + 1, :] = both
    copies.append(copy_out(sums_ref, outs[4], sems.at[7]))
    for copy in copies:
        copy.wait()


def row_lines(channels, sums_ref):
    total = jnp.sum(sums_ref[...], axis=0)
    half = GROUP // 2
    inv_rms = lax.rsqrt(total[:half] / channels + EPSILON)
    return jnp.transpose(jnp.concatenate([inv_rms, total[half:] * inv_rms / channels], axis=0))


def finish_norm(
    channels, sums_ref, conv_hbm, gate_hbm, got_hbm, grad_ref, first_ref, conv_ref, gate_ref, upstream_ref, sems
):
    loads = [
        copy_out(conv_hbm, conv_ref, sems.at[0]),
        copy_out(gate_hbm, gate_ref, sems.at[1]),
        copy_out(got_hbm.at[:, UPSTREAM:CLASS, :], upstream_ref, sems.at[2]),
    ]
    lines = row_lines(channels, sums_ref)
    half = GROUP // 2
    for load in loads:
        load.wait()
    for block in range(GROUP):
        rows = slice((block % 2) * LEN, (block % 2 + 1) * LEN)
        inv = lines[rows, block // 2 : block // 2 + 1]
        mean = lines[rows, half + block // 2 : half + block // 2 + 1]
        gate = gate_ref[:, col(block)]
        normed = gate * conv_ref[:, col(block)] * inv
        grad_conv = (inv * (upstream_ref[block].astype(F32) - normed * mean) * gate).astype(BF16)
        grad_ref[:, col(block)] = grad_conv
        if block < REACH:
            first_ref[:, col(block)] = grad_conv


def filter_terms(
    grad_ref, own_hbm, before_hbm, forward_high, forward_low, inverse_high, inverse_low, spec_out,
    terms_out, product_ref, terms_ref, grad_spec_ref, own_ref, before_ref, sems,
):
    copies = [copy_out(own_hbm, own_ref, sems.at[0]), copy_out(before_hbm, before_ref, sems.at[1])]
    grad_spec_ref[...] = spectrum((forward_high, forward_low), grad_ref[...])
    for copy in copies:
        copy.wait()
    copies = [copy_out(grad_spec_ref, spec_out, sems.at[2])]

    def step(row, sign):
        real, imag = read_blocks(own_ref, before_ref, row)
        pairs = windows(real, imag, sign)
        grads = [
            (grad_spec_ref[pl.ds(row, 8), col(b)], grad_spec_ref[pl.ds(row + LEN, 8), col(b)]) for b in range(GROUP)
        ]
        for d in range(REACH):
            total_real, total_imag = 0.0, 0.0
            for block in range(GROUP):
                window = pairs[REACH + block - d]
                total_real += grads[block][0] * window[0] + grads[block][1] * window[1]
                total_imag += grads[block][1] * window[0] - grads[block][0] * window[1]
            product_ref[pl.ds(row, 8), col(d)] = total_real
            product_ref[pl.ds(row + LEN, 8), col(d)] = total_imag

    over_frequencies(step)
    terms = invert((inverse_high, inverse_low), product_ref[...])
    for d in range(REACH):
        terms_ref[d] = terms[:, col(d)].astype(BF16)
    copies.append(copy_out(terms_ref, terms_out, sems.at[3]))
    for copy in copies:
        copy.wait()


def correlate_back(
    grad_spec_ref, after_ref, lag_spec_ref, forward_high, forward_low, inverse_high, inverse_low, result_ref,
    after_spec_ref, product_ref,
):
    after_spec_ref[...] = spectrum((forward_high, forward_low), after_ref[...])

    def step(row, sign):
        real = [grad_spec_ref[pl.ds(row, 8), col(b)] for b in range(GROUP)]
        real += [after_spec_ref[pl.ds(row, 8), col(b)] for b in range(REACH)]
        imag = [grad_spec_ref[pl.ds(row + LEN, 8), col(b)] for b in range(GROUP)]
        imag += [after_spec_ref[pl.ds(row + LEN, 8), col(b)] for b in range(REACH)]
        pairs = [
            (real[b] + sign * imag[b + 1], imag[b] - sign * real[b + 1]) for b in range(GROUP + REACH - 1)
        ]
        lag = [
            (lag_spec_ref[pl.ds(row, 8), col(d)], lag_spec_ref[pl.ds(row + LEN, 8), col(d)]) for d in range(REACH)
        ]
        for block in range(GROUP):
            total_real, total_imag = 0.0, 0.0
            for d in range(REACH):
                window = pairs[block + d]
                total_real += lag[d][0] * window[0] + lag[d][1] * window[1]
                total_imag += lag[d][0] * window[1] - lag[d][1] * window[0]
            product_ref[pl.ds(row, 8), col(block)] = total_real
            product_ref[pl.ds(row + LEN, 8), col(block)] = total_imag

    over_frequencies(step)
    result_ref[...] = invert((inverse_high, inverse_low), product_ref[...]).astype(BF16)


def pack_back(place_ref, result_ref, rounded_ref, *out_refs):
    for step in range(GROUP):
        there = lane((place_ref[0] + step) & (GROUP - 1))
        out_refs[step][:LEN, :] = result_ref[:, there]
        out_refs[step][LEN:, :] = rounded_ref[:, there]


def sum_terms(terms_ref, out_ref):
    groups = terms_ref.shape[0] // GROUP
    for place in range(GROUP):
        out_ref[:, col(place)] = sum(terms_ref[group * GROUP + place].astype(F32) for group in range(groups))


def finish(
    channels, place_ref, sums_ref, query_ref, key_ref, value_ref, cotangent_ref, stock_ref, class_ref, table_ref, *refs
):
    pieces, (normed_ref, grad_query_ref, grad_key_ref, grad_value_ref, lines_ref) = (
        refs[:GROUP], refs[GROUP:]
    )
    place = place_ref[0]
    half = GROUP // 2
    lines_ref[...] = row_lines(channels, sums_ref)
    lines = lines_ref[pl.ds(pl.multiple_of((place & 1) * LEN, LEN), LEN), :]
    number = lax.broadcasted_iota(jnp.int32, (LEN, GROUP), 1)
    inv = jnp.sum(jnp.where(number == place >> 1, lines, 0.0), axis=1, keepdims=True)
    mean = jnp.sum(jnp.where(number == half + (place >> 1), lines, 0.0), axis=1, keepdims=True)
    event_class = event_classes(stock_ref, class_ref)[:1]
    for step in range(GROUP):
        there = lane((place - step) & (GROUP - 1))
        piece = pieces[step]
        factor = modulation(event_class, table_ref[:, there])
        conv = piece[LEN:, :].astype(F32)
        normed = query_ref[:, there].astype(F32) * factor * conv * inv
        normed_ref[:, there] = normed.astype(BF16)
        grad_scaled = inv * (cotangent_ref[:, there].astype(F32) - normed * mean)
        grad_query_ref[:, there] = (grad_scaled * conv * factor).astype(BF16)
        grad_mixed = piece[:LEN, :].astype(F32)
        grad_key_ref[:, there] = (grad_mixed * value_ref[:, there].astype(F32)).astype(BF16)
        grad_value_ref[:, there] = (grad_mixed * key_ref[:, there].astype(F32)).astype(BF16)


def on_chip(shape, dtype):
    return pltpu.VMEM(shape, dtype)


def off_chip(shape, dtype):
    return pltpu.HBM(shape, dtype)


def near(value):
    return pltpu.with_memory_space_constraint(value, pltpu.VMEM)


def far(value):
    return pltpu.with_memory_space_constraint(value, pltpu.HBM)


def call(body, outs, *args, scalars=0, scratch=(), copies=0, left=(), manual=False, cost=1000):
    specs = [pl.BlockSpec(memory_space=pltpu.SMEM)] * scalars
    specs += [
        pl.BlockSpec(memory_space=pl.ANY if index in left else pltpu.VMEM) for index in range(scalars, len(args))
    ]
    moved = sum(a.size * a.dtype.itemsize for a in args)
    return pl.pallas_call(
        body,
        out_shape=list(outs),
        in_specs=specs,
        out_specs=[pl.BlockSpec(memory_space=pl.ANY if manual else pltpu.VMEM)] * len(outs),
        scratch_shapes=[pltpu.VMEM(shape, dtype) for shape, dtype in scratch]
        + ([pltpu.SemaphoreType.DMA(copies)] if copies else []),
        cost_estimate=pl.CostEstimate(flops=cost, bytes_accessed=moved, transcendentals=0),
        compiler_params=pltpu.CompilerParams(vmem_limit_bytes=20 << 20),
    )(*args)


def swap(pieces):
    return [pieces[0]] + [
        lax.ppermute(pieces[step], "j", [(i, (i + step) % GROUP) for i in range(GROUP)]) for step in range(1, GROUP)
    ]


def trade(value, mask, groups):
    return lax.ppermute(value, "g", [(i, i ^ mask) for i in range(groups)])


def shards(query_proj, key_proj, value_proj, filters, cotangent, stock_id, stock_class, cond_table):
    groups = lax.axis_size("g")
    parts = lax.axis_size("ch")
    near_groups = min(4, groups)
    far_groups = groups // near_groups
    lag_rows = filters.shape[0]
    wide = GROUP * LANES
    half = wide // 2
    place = jnp.stack([lax.axis_index("j"), lax.axis_index("g")]).astype(jnp.int32)
    tables = [jnp.asarray(t) for t in transform_tables()]
    far_tables, near_tables = list(map(far, tables)), list(map(near, tables))
    stock_id, stock_class = far(stock_id[None, :]), far(stock_class[None, :])
    table = far(jnp.pad(cond_table, ((0, 16 - cond_table.shape[0]), (0, 0))))

    (sent,) = call(
        pack, [off_chip((GROUP, ROWS, LANES), BF16)], *map(far, (key_proj, value_proj, query_proj, cotangent)),
        stock_id, stock_class, manual=True, copies=(GROUP,), scratch=[((GROUP, ROWS, LANES), BF16)],
    )
    got = lax.all_to_all(sent, "j", 0, 0)
    lags = filters[None]
    lags = jnp.concatenate([lags] + [trade(lags, high * near_groups, groups) for high in range(1, far_groups)])
    lags = [lags] + [trade(lags, low, groups) for low in range(1, near_groups)]
    (lags,) = call(pack_lags, [off_chip((GROUP, groups * lag_rows, LANES), BF16)], *map(near, lags))
    got, lags = lax.optimization_barrier((got, lags))
    before = lax.ppermute(got[GROUP - REACH :, :LEN, :], "g", [(i, i + 1) for i in range(groups - 1)])
    got, lags = far(got), near(lax.all_to_all(lags, "j", 0, 0))
    own, gate = call(
        prepare, [off_chip((2 * LEN, wide), F32), off_chip((LEN, wide), F32)], place, table, got, *far_tables[:2],
        scalars=1, copies=(2,), manual=True, scratch=[((2 * LEN, wide), F32), ((LEN, wide), F32)],
        cost=2 * 4 * LEN * LEN * wide,
    )
    before_spec, lag_spec, conv, rounded, sums = call(
        functools.partial(convolve, near_groups, far_groups),
        [
            off_chip((2 * LEN, half), F32), off_chip((2 * LEN, half), F32), off_chip((LEN, wide), F32),
            off_chip((LEN, wide), BF16), off_chip((GROUP * parts, 8, 2 * LEN), F32),
        ],
        place, far(own), far(gate), got, before, lags, *far_tables, scalars=1, copies=(8,), manual=True, left=(1, 2, 3),
        scratch=[
            ((2 * LEN, half), F32), ((2 * LEN, half), F32), ((LEN, wide), F32), ((LEN, wide), BF16),
            ((GROUP * parts, 8, 2 * LEN), F32), ((2 * LEN, wide), F32), ((LEN, wide), F32),
            ((GROUP, LEN, LANES), BF16), ((2 * LEN, wide), F32), ((LEN, half), F32),
        ],
        cost=2 * 10 * LEN * LEN * wide,
    )
    sums = lax.all_to_all(sums, ("j", "ch"), 0, 0)
    grad_conv, first = call(
        functools.partial(finish_norm, wide * parts), [on_chip((LEN, wide), BF16), on_chip((LEN, half), BF16)],
        far(sums), far(conv), far(gate), got, left=(1, 2, 3), copies=(3,),
        scratch=[((LEN, wide), F32), ((LEN, wide), F32), ((GROUP, LEN, LANES), BF16)],
    )
    after = lax.ppermute(first, "g", [(i, i - 1) for i in range(1, groups)])
    grad_spec, terms = call(
        filter_terms, [off_chip((2 * LEN, wide), F32), off_chip((REACH, LEN, LANES), BF16)],
        near(grad_conv), far(own), far(before_spec), *far_tables, left=(1, 2), manual=True, copies=(4,),
        scratch=[
            ((2 * LEN, half), F32), ((REACH, LEN, LANES), BF16), ((2 * LEN, wide), F32), ((2 * LEN, wide), F32),
            ((2 * LEN, half), F32),
        ],
        cost=2 * 7 * LEN * LEN * wide,
    )
    terms = lax.all_to_all(terms.reshape(groups * GROUP, lag_rows, LANES), ("g", "j"), 0, 0)
    (back,) = call(
        correlate_back, [off_chip((LEN, wide), BF16)], far(grad_spec), after, far(lag_spec), *far_tables,
        scratch=[((2 * LEN, half), F32), ((2 * LEN, wide), F32)], cost=2 * 8 * LEN * LEN * wide,
    )
    back = call(pack_back, [on_chip((2 * LEN, LANES), BF16)] * GROUP, place, back, rounded, scalars=1)
    back = swap(back)
    (grad_filter,) = call(sum_terms, [off_chip((lag_rows, wide), F32)], terms)
    outs = call(
        functools.partial(finish, wide * parts),
        [off_chip((LEN, wide), BF16)] * 4,
        place, near(sums), *map(near, (query_proj, key_proj, value_proj, cotangent)), stock_id, stock_class, table,
        *map(near, back), scalars=1, scratch=[((2 * LEN, GROUP), F32)],
    )
    return *outs, grad_filter


def solution(mesh):
    ctx, ch = mesh.devices.shape
    inner = Mesh(mesh.devices.reshape(ctx // GROUP, GROUP, ch), ("g", "j", "ch"))
    rows = ("g", "j")
    return jax.shard_map(
        shards,
        mesh=inner,
        in_specs=(P(rows, "ch"),) * 5 + (P(rows), P(), P(None, "ch")),
        out_specs=(P(rows, "ch"),) * 5,
        check_vma=False,
    )
```

time: 146 us -> 122 us (0.84)
  the two profiles are of different devices: /device:TPU:3 before, /device:TPU:1 now
where the time goes in v2:
time: 122 us; the launch traced here: 121 us
  starting transfers between devices  46.7 us (38%)
  Pallas kernels  35.3 us (29%)
  waiting for transfers between devices  21.4 us (18%)
  blocking collectives  14.7 us (12%)
  local copies, waits for them, and re-layouts  1.75 us (1%)
    pallas_call x10, Pallas kernels, call(): pl.pallas_call(body, out_shape=list(outs), in_specs=specs, out_specs=[pl....  35.3 us
    all_to_all x1, blocking collectives, shards(): sums = lax.all_to_all(sums, ('j', 'ch'), 0, 0)  14.7 us
    all_to_all x1, starting transfers between devices, shards(): lax.all_to_all(terms.reshape(groups * GROUP, lag_rows, LANES), ('g', 'j')...  13.3 us
    ppermute x6, starting transfers between devices, trade(): return lax.ppermute(value, 'g', [(i, i ^ mask) for i in range(groups)])  10.2 us
    ppermute x7, waiting for transfers between devices, swap(): lax.ppermute(pieces[step], 'j', [(i, (i + step) % GROUP) for i in range(G...  9.47 us
    ppermute x6, waiting for transfers between devices, trade(): return lax.ppermute(value, 'g', [(i, i ^ mask) for i in range(groups)])  8.26 us
    ppermute x7, starting transfers between devices, swap(): lax.ppermute(pieces[step], 'j', [(i, (i + step) % GROUP) for i in range(G...  7.53 us
    all_to_all x1, starting transfers between devices, shards(): got = lax.all_to_all(sent, 'j', 0, 0)  6.87 us
  transfers between devices with their start and end apart: 18, of which 11 were waited for; matrix products, arithmetic and copies ran while one was open for 1% of the time, Pallas kernels for 17%

profile of v2, /device:TPU:1, one launch (start us, length us, event | category | flops | bytes accessed | tf_op | source)
XLA Modules:
  0.0 120.9 jit_solution(15010938703364649914)
XLA Ops:
  0.6 3.0 %shard_map.155 = bf16[8,784,128]{2,1,0:T(8,128)(2,1)} custom-call(bf16[256,1024]{1,0:T(8,128)(2,1)} %key_ref.3, bf16[256,1024]{1,0:T(8,128)(2,1)} %value_ref.3, bf16[256,1024]{1,0:T(8,128)(2,1)} %query_ref.3, bf16[256,1024]{1,0:T(8,128)(2,1)} %cotangent_ref.3, s32[1,256]{1,0:T(1,128)} %bitcast.13, s32[1,512]{1,0:T(1,128)} %bitcast.11), custom_call_target="tpu_custom_call" | custom-call | flops 1000 | bytes 2100224 | tf_op jit(solution)/shard_map/pallas_call | solution.py:371
  3.6 6.9 %all-to-all-start = ((bf16[8,784,128]{2,1,0:T(8,128)(2,1)}), bf16[8,784,128]{2,1,0:T(8,128)(2,1)S(1)}, u32[]{:S(2)}, u32[]{:S(2)}) async-start(bf16[8,784,128]{2,1,0:T(8,128)(2,1)} %shard_map.155), calls=%async_computation | async-start | bytes 3211264 | tf_op jit(solution)/shard_map/all_to_all | solution.py:411
  10.5 5.3 %collective-permute-start.2 = (bf16[1,8,1024]{2,1,0:T(8,128)(2,1)S(1)}, bf16[1,8,1024]{2,1,0:T(8,128)(2,1)S(1)}, u32[]{:S(2)}, u32[]{:S(2)}) collective-permute-start(bf16[1,8,1024]{2,1,0:T(8,128)(2,1)S(1)} %bitcast.7), channel_id=1, source_target_pairs={{0,192},{16,208},{32,224},{48,240},{64,128},{80,144},{96,160},{112... | collective-permute-start | bytes 49160 | tf_op jit(solution)/shard_map/ppermute | solution.py:390
  18.0 4.4 %collective-permute-done.1 = bf16[1,8,1024]{2,1,0:T(8,128)(2,1)S(1)} collective-permute-done((bf16[1,8,1024]{2,1,0:T(8,128)(2,1)S(1)}, bf16[1,8,1024]{2,1,0:T(8,128)(2,1)S(1)}, u32[]{:S(2)}, u32[]{:S(2)}) %collective-permute-start.1) | collective-permute-done | bytes 16416 | tf_op jit(solution)/shard_map/ppermute | solution.py:390
  22.4 1.7 %collective-permute-start.5 = (bf16[4,8,1024]{2,1,0:T(8,128)(2,1)S(1)}, bf16[4,8,1024]{2,1,0:T(8,128)(2,1)S(1)}, u32[]{:S(2)}, u32[]{:S(2)}) collective-permute-start(bf16[4,8,1024]{2,1,0:T(8,128)(2,1)S(1)} %pad_maximum_fusion.refs_0_), channel_id=1, source_target_pairs={{0,48},{16,32},{32,16},{48,0},{64,112},{80,96},{96,80},{112,64},{1... | collective-permute-start | bytes 196616 | tf_op jit(solution)/shard_map/ppermute | solution.py:390
  25.1 1.6 %collective-permute-done.5.refs_3_ = bf16[4,8,1024]{2,1,0:T(8,128)(2,1)S(1)} collective-permute-done((bf16[4,8,1024]{2,1,0:T(8,128)(2,1)S(1)}, bf16[4,8,1024]{2,1,0:T(8,128)(2,1)S(1)}, u32[]{:S(2)}, u32[]{:S(2)}) %collective-permute-start.5) | collective-permute-done | bytes 65568 | tf_op jit(solution)/shard_map/ppermute | solution.py:390
  27.2 1.8 %collective-permute-done.3.refs_1_ = bf16[4,8,1024]{2,1,0:T(8,128)(2,1)S(1)} collective-permute-done((bf16[4,8,1024]{2,1,0:T(8,128)(2,1)S(1)}, bf16[4,8,1024]{2,1,0:T(8,128)(2,1)S(1)}, u32[]{:S(2)}, u32[]{:S(2)}) %collective-permute-start.3) | collective-permute-done | bytes 65568 | tf_op jit(solution)/shard_map/ppermute | solution.py:390
  29.7 1.9 %all-to-all-done.got_ref.got_hbm = bf16[8,784,128]{2,1,0:T(8,128)(2,1)S(1)} async-done(((bf16[8,784,128]{2,1,0:T(8,128)(2,1)}), bf16[8,784,128]{2,1,0:T(8,128)(2,1)S(1)}, u32[]{:S(2)}, u32[]{:S(2)}) %all-to-all-start) | async-done | bytes 1605664 | tf_op jit(solution)/shard_map/all_to_all | solution.py:411
  31.6 2.4 %collective-permute-start.6 = (bf16[4,256,128]{2,1,0:T(8,128)(2,1)S(1)}, bf16[4,256,128]{2,1,0:T(8,128)(2,1)S(1)}, u32[]{:S(2)}, u32[]{:S(2)}) collective-permute-start(bf16[4,256,128]{2,1,0:T(8,128)(2,1)S(1)} %slice.3), channel_id=1, source_target_pairs={{0,16},{16,32},{32,48},{48,64},{64,80},{80,96},{96,112},{112,128},... | collective-permute-start | bytes 786440 | tf_op jit(solution)/shard_map/ppermute | solution.py:417
  34.0 5.2 %all-to-all-start.1 = ((bf16[8,128,128]{2,1,0:T(8,128)(2,1)}), bf16[8,128,128]{2,1,0:T(8,128)(2,1)S(1)}, u32[]{:S(2)}, u32[]{:S(2)}) async-start(bf16[8,128,128]{2,1,0:T(8,128)(2,1)} %shard_map.156), calls=%async_computation.1 | async-start | bytes 524288 | tf_op jit(solution)/shard_map/all_to_all | solution.py:418
  39.9 4.0 %shard_map.157 = (f32[512,1024]{1,0:T(8,128)}, f32[256,1024]{1,0:T(8,128)}) custom-call(s32[2]{0:T(128)S(1)} %pad_add_fusion.place_ref, f32[16,1024]{1,0:T(8,128)} %pad.4.table_ref, bf16[8,784,128]{2,1,0:T(8,128)(2,1)} %copy-done.7, bf16[512,256]{1,0:T(8,128)(2,1)} %constant.22.clone.forward_high.refs_0_, bf16[512,256]{1,0:T(8,128)(2,1)} %constant.23.clone.forward_low.refs_1_), custom_call_target="tpu_custom_call" | custom-call | flops 536870912 | bytes 2195464 | tf_op jit(solution)/shard_map/pallas_call | solution.py:371
  43.8 1.8 %all-to-all-done.1.lags_ref = bf16[8,128,128]{2,1,0:T(8,128)(2,1)S(1)} async-done(((bf16[8,128,128]{2,1,0:T(8,128)(2,1)}), bf16[8,128,128]{2,1,0:T(8,128)(2,1)S(1)}, u32[]{:S(2)}, u32[]{:S(2)}) %all-to-all-start.1) | async-done | bytes 262176 | tf_op jit(solution)/shard_map/all_to_all | solution.py:418
  45.7 7.6 %shard_map.158 = (f32[512,512]{1,0:T(8,128)}, f32[512,512]{1,0:T(8,128)}, f32[256,1024]{1,0:T(8,128)}, bf16[256,1024]{1,0:T(8,128)(2,1)}, f32[16,8,512]{2,1,0:T(8,128)}) custom-call(s32[2]{0:T(128)S(1)} %pad_add_fusion.place_ref, f32[512,1024]{1,0:T(8,128)} %get-tuple-element.31.own_hbm, f32[256,1024]{1,0:T(8,128)} %get-tuple-element.32.gate_hbm, ...), custom_call_target="tpu_custom_call" | custom-call | flops 1342177280 | bytes 6324232 | tf_op jit(solution)/shard_map/pallas_call | solution.py:371
  53.3 14.7 %all_to_all.20.sums_ref = f32[16,8,512]{2,1,0:T(8,128)} all-to-all(f32[16,8,512]{2,1,0:T(8,128)} %get-tuple-element.34), channel_id=1, replica_groups=mesh['g'=16,'j'=8,'ch'=2] {'j','ch'}, dimensions={0} | all-to-all | bytes 524288 | tf_op jit(solution)/shard_map/all_to_all | solution.py:438
  68.1 3.3 %shard_map.159 = (bf16[256,1024]{1,0:T(8,128)(2,1)S(1)}, bf16[256,512]{1,0:T(8,128)(2,1)S(1)}) custom-call(f32[16,8,512]{2,1,0:T(8,128)} %all_to_all.20.sums_ref, f32[256,1024]{1,0:T(8,128)} %get-tuple-element.35.conv_hbm, f32[256,1024]{1,0:T(8,128)} %get-tuple-element.32.gate_hbm, bf16[8,784,128]{2,1,0:T(8,128)(2,1)} %copy-done.7), custom_call_target="tpu_custom_call" | custom-call | flops 1000 | bytes 3964928 | tf_op jit(solution)/shard_map/pallas_call | solution.py:371
  72.7 5.9 %shard_map.160 = (f32[512,1024]{1,0:T(8,128)}, bf16[4,256,128]{2,1,0:T(8,128)(2,1)}) custom-call(bf16[256,1024]{1,0:T(8,128)(2,1)S(1)} %get-tuple-element.36.grad_ref, f32[512,1024]{1,0:T(8,128)} %get-tuple-element.31.own_hbm, f32[512,512]{1,0:T(8,128)} %get-tuple-element.37.before_hbm, bf16[512,256]{1,0:T(8,128)(2,1)} %constant.22.clone.forward_high.refs_0_, ...), custom_call_target="tpu_custom_call" | custom-call | flops 939524096 | bytes 4718592 | tf_op jit(solution)/shard_map/pallas_call | solution.py:371
  78.6 13.3 %all-to-all-start.3 = ((bf16[128,8,128]{2,1,0:T(8,128)(2,1)}), bf16[128,8,128]{2,1,0:T(8,128)(2,1)S(1)}, u32[]{:S(2)}, u32[]{:S(2)}) async-start(bf16[128,8,128]{2,1,0:T(8,128)(2,1)} %bitcast.6), calls=%async_computation.3 | async-start | bytes 524288 | tf_op jit(solution)/shard_map/all_to_all | solution.py:454
  91.9 5.9 %shard_map.161.result_ref = bf16[256,1024]{1,0:T(8,128)(2,1)} custom-call(f32[512,1024]{1,0:T(8,128)} %get-tuple-element.38.grad_spec_ref, bf16[256,512]{1,0:T(8,128)(2,1)S(1)} %collective-permute-done.7.after_ref, f32[512,512]{1,0:T(8,128)} %get-tuple-element.40.lag_spec_ref, bf16[512,256]{1,0:T(8,128)(2,1)} %constant.22.clone.forward_high.refs_0_, ...), custom_call_target="tpu_custom_call" | custom-call | flops 1073741824 | bytes 4456448 | tf_op jit(solution)/shard_map/pallas_call | solution.py:371
  99.7 1.6 %collective-permute-start.8 = (bf16[512,128]{1,0:T(8,128)(2,1)S(1)}, bf16[512,128]{1,0:T(8,128)(2,1)S(1)}, u32[]{:S(2)}, u32[]{:S(2)}) collective-permute-start(bf16[512,128]{1,0:T(8,128)(2,1)S(1)} %get-tuple-element.43), channel_id=1, source_target_pairs={{0,2},{2,4},{4,6},{6,8},{8,10},{10,12},{12,14},{14,0},{1,3},{3,5},... | collective-permute-start | bytes 393224 | tf_op jit(solution)/shard_map/ppermute | solution.py:385
  102.5 1.6 %collective-permute-start.10 = (bf16[512,128]{1,0:T(8,128)(2,1)S(1)}, bf16[512,128]{1,0:T(8,128)(2,1)S(1)}, u32[]{:S(2)}, u32[]{:S(2)}) collective-permute-start(bf16[512,128]{1,0:T(8,128)(2,1)S(1)} %get-tuple-element.45), channel_id=1, source_target_pairs={{0,6},{2,8},{4,10},{6,12},{8,14},{10,0},{12,2},{14,4},{1,7},{3,9},... | collective-permute-start | bytes 393224 | tf_op jit(solution)/shard_map/ppermute | solution.py:385
  104.8 2.4 %collective-permute-start.12 = (bf16[512,128]{1,0:T(8,128)(2,1)S(1)}, bf16[512,128]{1,0:T(8,128)(2,1)S(1)}, u32[]{:S(2)}, u32[]{:S(2)}) collective-permute-start(bf16[512,128]{1,0:T(8,128)(2,1)S(1)} %get-tuple-element.47), channel_id=1, source_target_pairs={{0,10},{2,12},{4,14},{6,0},{8,2},{10,4},{12,6},{14,8},{1,11},{3,13... | collective-permute-start | bytes 393224 | tf_op jit(solution)/shard_map/ppermute | solution.py:385
  107.2 2.2 %collective-permute-done.9.refs_2_ = bf16[512,128]{1,0:T(8,128)(2,1)S(1)} collective-permute-done((bf16[512,128]{1,0:T(8,128)(2,1)S(1)}, bf16[512,128]{1,0:T(8,128)(2,1)S(1)}, u32[]{:S(2)}, u32[]{:S(2)}) %collective-permute-start.9) | collective-permute-done | bytes 131104 | tf_op jit(solution)/shard_map/ppermute | solution.py:385
  110.6 4.7 %collective-permute-done.11.refs_4_ = bf16[512,128]{1,0:T(8,128)(2,1)S(1)} collective-permute-done((bf16[512,128]{1,0:T(8,128)(2,1)S(1)}, bf16[512,128]{1,0:T(8,128)(2,1)S(1)}, u32[]{:S(2)}, u32[]{:S(2)}) %collective-permute-start.11) | collective-permute-done | bytes 131104 | tf_op jit(solution)/shard_map/ppermute | solution.py:385
  116.7 3.4 %shard_map.163 = (bf16[256,1024]{1,0:T(8,128)(2,1)}, bf16[256,1024]{1,0:T(8,128)(2,1)}, bf16[256,1024]{1,0:T(8,128)(2,1)}, bf16[256,1024]{1,0:T(8,128)(2,1)}) custom-call(s32[2]{0:T(128)S(1)} %pad_add_fusion.place_ref, f32[16,8,512]{2,1,0:T(8,128)S(1)} %copy-done, bf16[256,1024]{1,0:T(8,128)(2,1)S(1)} %copy-done.4, bf16[256,1024]{1,0:T(8,128)(2,1)S(1)} %copy-done.2, ...), custom_call_target="tpu_custom_call" | custom-call | flops 1000 | bytes 3476488 | tf_op jit(solution)/shard_map/pallas_call | solution.py:371
  (47 shorter events, 13.5 us)
Async XLA Ops:
  3.6 35.6 %copy-start.8 = (f32[11,1024]{1,0:T(8,128)S(1)}, f32[11,1024]{1,0:T(8,128)}, u32[]{:S(2)}) copy-start(f32[11,1024]{1,0:T(8,128)} %param.19) | copy-start | bytes 135172
  3.6 28.0 %all-to-all-start = ((bf16[8,784,128]{2,1,0:T(8,128)(2,1)}), bf16[8,784,128]{2,1,0:T(8,128)(2,1)S(1)}, u32[]{:S(2)}, u32[]{:S(2)}) async-start(bf16[8,784,128]{2,1,0:T(8,128)(2,1)} %shard_map.155), calls=%async_computation | async-start | bytes 3211264 | tf_op jit(solution)/shard_map/all_to_all | solution.py:411
  10.5 7.5 %collective-permute-start.2 = (bf16[1,8,1024]{2,1,0:T(8,128)(2,1)S(1)}, bf16[1,8,1024]{2,1,0:T(8,128)(2,1)S(1)}, u32[]{:S(2)}, u32[]{:S(2)}) collective-permute-start(bf16[1,8,1024]{2,1,0:T(8,128)(2,1)S(1)} %bitcast.7), channel_id=1, source_target_pairs={{0,192},{16,208},{32,224},{48,240},{64,128},{80,144},{96,160},{112... | collective-permute-start | bytes 49160 | tf_op jit(solution)/shard_map/ppermute | solution.py:390
  15.8 6.6 %collective-permute-start.1 = (bf16[1,8,1024]{2,1,0:T(8,128)(2,1)S(1)}, bf16[1,8,1024]{2,1,0:T(8,128)(2,1)S(1)}, u32[]{:S(2)}, u32[]{:S(2)}) collective-permute-start(bf16[1,8,1024]{2,1,0:T(8,128)(2,1)S(1)} %bitcast.8), channel_id=1, source_target_pairs={{0,128},{16,144},{32,160},{48,176},{64,192},{80,208},{96,224},{112... | collective-permute-start | bytes 49160 | tf_op jit(solution)/shard_map/ppermute | solution.py:390
  16.8 5.6 %collective-permute-start = (bf16[1,8,1024]{2,1,0:T(8,128)(2,1)S(1)}, bf16[1,8,1024]{2,1,0:T(8,128)(2,1)S(1)}, u32[]{:S(2)}, u32[]{:S(2)}) collective-permute-start(bf16[1,8,1024]{2,1,0:T(8,128)(2,1)S(1)} %bitcast.9), channel_id=1, source_target_pairs={{0,64},{16,80},{32,96},{48,112},{64,0},{80,16},{96,32},{112,48},{1... | collective-permute-start | bytes 49160 | tf_op jit(solution)/shard_map/ppermute | solution.py:390
  22.4 4.3 %collective-permute-start.5 = (bf16[4,8,1024]{2,1,0:T(8,128)(2,1)S(1)}, bf16[4,8,1024]{2,1,0:T(8,128)(2,1)S(1)}, u32[]{:S(2)}, u32[]{:S(2)}) collective-permute-start(bf16[4,8,1024]{2,1,0:T(8,128)(2,1)S(1)} %pad_maximum_fusion.refs_0_), channel_id=1, source_target_pairs={{0,48},{16,32},{32,16},{48,0},{64,112},{80,96},{96,80},{112,64},{1... | collective-permute-start | bytes 196616 | tf_op jit(solution)/shard_map/ppermute | solution.py:390
  24.0 3.2 %collective-permute-start.4 = (bf16[4,8,1024]{2,1,0:T(8,128)(2,1)S(1)}, bf16[4,8,1024]{2,1,0:T(8,128)(2,1)S(1)}, u32[]{:S(2)}, u32[]{:S(2)}) collective-permute-start(bf16[4,8,1024]{2,1,0:T(8,128)(2,1)S(1)} %pad_maximum_fusion.refs_0_), channel_id=1, source_target_pairs={{0,32},{16,48},{32,0},{48,16},{64,96},{80,112},{96,64},{112,80},{1... | collective-permute-start | bytes 196616 | tf_op jit(solution)/shard_map/ppermute | solution.py:390
  24.9 4.1 %collective-permute-start.3 = (bf16[4,8,1024]{2,1,0:T(8,128)(2,1)S(1)}, bf16[4,8,1024]{2,1,0:T(8,128)(2,1)S(1)}, u32[]{:S(2)}, u32[]{:S(2)}) collective-permute-start(bf16[4,8,1024]{2,1,0:T(8,128)(2,1)S(1)} %pad_maximum_fusion.refs_0_), channel_id=1, source_target_pairs={{0,16},{16,0},{32,48},{48,32},{64,80},{80,64},{96,112},{112,96},{1... | collective-permute-start | bytes 196616 | tf_op jit(solution)/shard_map/ppermute | solution.py:390
  31.6 14.1 %collective-permute-start.6 = (bf16[4,256,128]{2,1,0:T(8,128)(2,1)S(1)}, bf16[4,256,128]{2,1,0:T(8,128)(2,1)S(1)}, u32[]{:S(2)}, u32[]{:S(2)}) collective-permute-start(bf16[4,256,128]{2,1,0:T(8,128)(2,1)S(1)} %slice.3), channel_id=1, source_target_pairs={{0,16},{16,32},{32,48},{48,64},{64,80},{80,96},{96,112},{112,128},... | collective-permute-start | bytes 786440 | tf_op jit(solution)/shard_map/ppermute | solution.py:417
  34.0 11.7 %all-to-all-start.1 = ((bf16[8,128,128]{2,1,0:T(8,128)(2,1)}), bf16[8,128,128]{2,1,0:T(8,128)(2,1)S(1)}, u32[]{:S(2)}, u32[]{:S(2)}) async-start(bf16[8,128,128]{2,1,0:T(8,128)(2,1)} %shard_map.156), calls=%async_computation.1 | async-start | bytes 524288 | tf_op jit(solution)/shard_map/all_to_all | solution.py:418
  71.4 20.5 %collective-permute-start.7 = (bf16[256,512]{1,0:T(8,128)(2,1)S(1)}, bf16[256,512]{1,0:T(8,128)(2,1)S(1)}, u32[]{:S(2)}, u32[]{:S(2)}) collective-permute-start(bf16[256,512]{1,0:T(8,128)(2,1)S(1)} %get-tuple-element.39), channel_id=1, source_target_pairs={{16,0},{32,16},{48,32},{64,48},{80,64},{96,80},{112,96},{128,112},... | collective-permute-start | bytes 786440 | tf_op jit(solution)/shard_map/ppermute | solution.py:444
  78.6 41.6 %all-to-all-start.3 = ((bf16[128,8,128]{2,1,0:T(8,128)(2,1)}), bf16[128,8,128]{2,1,0:T(8,128)(2,1)S(1)}, u32[]{:S(2)}, u32[]{:S(2)}) async-start(bf16[128,8,128]{2,1,0:T(8,128)(2,1)} %bitcast.6), calls=%async_computation.3 | async-start | bytes 524288 | tf_op jit(solution)/shard_map/all_to_all | solution.py:454
  91.9 24.8 %copy-start = (f32[16,8,512]{2,1,0:T(8,128)S(1)}, f32[16,8,512]{2,1,0:T(8,128)}, u32[]{:S(2)}) copy-start(f32[16,8,512]{2,1,0:T(8,128)} %all_to_all.20.sums_ref) | copy-start | bytes 786436
  91.9 24.8 %copy-start.2 = (bf16[256,1024]{1,0:T(8,128)(2,1)S(1)}, bf16[256,1024]{1,0:T(8,128)(2,1)}, u32[]{:S(2)}) copy-start(bf16[256,1024]{1,0:T(8,128)(2,1)} %key_ref.3) | copy-start | bytes 1572868
  91.9 24.8 %copy-start.3 = (bf16[256,1024]{1,0:T(8,128)(2,1)S(1)}, bf16[256,1024]{1,0:T(8,128)(2,1)}, u32[]{:S(2)}) copy-start(bf16[256,1024]{1,0:T(8,128)(2,1)} %value_ref.3) | copy-start | bytes 1572868
  91.9 24.8 %copy-start.4 = (bf16[256,1024]{1,0:T(8,128)(2,1)S(1)}, bf16[256,1024]{1,0:T(8,128)(2,1)}, u32[]{:S(2)}) copy-start(bf16[256,1024]{1,0:T(8,128)(2,1)} %query_ref.3) | copy-start | bytes 1572868
  91.9 24.8 %copy-start.5 = (bf16[256,1024]{1,0:T(8,128)(2,1)S(1)}, bf16[256,1024]{1,0:T(8,128)(2,1)}, u32[]{:S(2)}) copy-start(bf16[256,1024]{1,0:T(8,128)(2,1)} %cotangent_ref.3) | copy-start | bytes 1572868
  99.7 7.5 %collective-permute-start.8 = (bf16[512,128]{1,0:T(8,128)(2,1)S(1)}, bf16[512,128]{1,0:T(8,128)(2,1)S(1)}, u32[]{:S(2)}, u32[]{:S(2)}) collective-permute-start(bf16[512,128]{1,0:T(8,128)(2,1)S(1)} %get-tuple-element.43), channel_id=1, source_target_pairs={{0,2},{2,4},{4,6},{6,8},{8,10},{10,12},{12,14},{14,0},{1,3},{3,5},... | collective-permute-start | bytes 393224 | tf_op jit(solution)/shard_map/ppermute | solution.py:385
  101.4 8.1 %collective-permute-start.9 = (bf16[512,128]{1,0:T(8,128)(2,1)S(1)}, bf16[512,128]{1,0:T(8,128)(2,1)S(1)}, u32[]{:S(2)}, u32[]{:S(2)}) collective-permute-start(bf16[512,128]{1,0:T(8,128)(2,1)S(1)} %get-tuple-element.44), channel_id=1, source_target_pairs={{0,4},{2,6},{4,8},{6,10},{8,12},{10,14},{12,0},{14,2},{1,5},{3,7},... | collective-permute-start | bytes 393224 | tf_op jit(solution)/shard_map/ppermute | solution.py:385
  102.5 8.1 %collective-permute-start.10 = (bf16[512,128]{1,0:T(8,128)(2,1)S(1)}, bf16[512,128]{1,0:T(8,128)(2,1)S(1)}, u32[]{:S(2)}, u32[]{:S(2)}) collective-permute-start(bf16[512,128]{1,0:T(8,128)(2,1)S(1)} %get-tuple-element.45), channel_id=1, source_target_pairs={{0,6},{2,8},{4,10},{6,12},{8,14},{10,0},{12,2},{14,4},{1,7},{3,9},... | collective-permute-start | bytes 393224 | tf_op jit(solution)/shard_map/ppermute | solution.py:385
  104.2 11.2 %collective-permute-start.11 = (bf16[512,128]{1,0:T(8,128)(2,1)S(1)}, bf16[512,128]{1,0:T(8,128)(2,1)S(1)}, u32[]{:S(2)}, u32[]{:S(2)}) collective-permute-start(bf16[512,128]{1,0:T(8,128)(2,1)S(1)} %get-tuple-element.46), channel_id=1, source_target_pairs={{0,8},{2,10},{4,12},{6,14},{8,0},{10,2},{12,4},{14,6},{1,9},{3,11}... | collective-permute-start | bytes 393224 | tf_op jit(solution)/shard_map/ppermute | solution.py:385
  104.8 11.3 %collective-permute-start.12 = (bf16[512,128]{1,0:T(8,128)(2,1)S(1)}, bf16[512,128]{1,0:T(8,128)(2,1)S(1)}, u32[]{:S(2)}, u32[]{:S(2)}) collective-permute-start(bf16[512,128]{1,0:T(8,128)(2,1)S(1)} %get-tuple-element.47), channel_id=1, source_target_pairs={{0,10},{2,12},{4,14},{6,0},{8,2},{10,4},{12,6},{14,8},{1,11},{3,13... | collective-permute-start | bytes 393224 | tf_op jit(solution)/shard_map/ppermute | solution.py:385
  107.2 8.9 %collective-permute-start.13 = (bf16[512,128]{1,0:T(8,128)(2,1)S(1)}, bf16[512,128]{1,0:T(8,128)(2,1)S(1)}, u32[]{:S(2)}, u32[]{:S(2)}) collective-permute-start(bf16[512,128]{1,0:T(8,128)(2,1)S(1)} %get-tuple-element.48), channel_id=1, source_target_pairs={{0,12},{2,14},{4,0},{6,2},{8,4},{10,6},{12,8},{14,10},{1,13},{3,15... | collective-permute-start | bytes 393224 | tf_op jit(solution)/shard_map/ppermute | solution.py:385
  109.4 7.3 %collective-permute-start.14 = (bf16[512,128]{1,0:T(8,128)(2,1)S(1)}, bf16[512,128]{1,0:T(8,128)(2,1)S(1)}, u32[]{:S(2)}, u32[]{:S(2)}) collective-permute-start(bf16[512,128]{1,0:T(8,128)(2,1)S(1)} %get-tuple-element.49), channel_id=1, source_target_pairs={{0,14},{2,0},{4,2},{6,4},{8,6},{10,8},{12,10},{14,12},{1,15},{3,1}... | collective-permute-start | bytes 393224 | tf_op jit(solution)/shard_map/ppermute | solution.py:385
  (4 other events, 22.2 us)

commit v3 on v2

--- a/solution.py
+++ b/solution.py
@@ -144,15 +144,18 @@
 
 
 def convolve(near_groups, far_groups, place_ref, own_hbm, gate_hbm, got_hbm, before_ref, lags_ref, *refs):
-    forward, inverse, outs = refs[:2], refs[2:4], refs[4:9]
-    before_spec_ref, lag_spec_ref, conv_ref, rounded_ref, sums_ref = refs[9:14]
-    own_ref, gate_ref, upstream_ref, product_ref, sorted_ref, sems = refs[14:]
+    own_ref, gate_ref, upstream_ref, before_spec_ref, conv_ref = refs[4:9]
+    forward, inverse = refs[9:11], refs[11:13]
+    lag_spec_hbm, rounded_hbm, sums_ref, lag_spec_ref, rounded_ref, product_ref, sorted_ref, sems = refs[13:]
+    tables = [copy_out(refs[i], refs[9 + i], sems.at[5 + i]) for i in range(4)]
     loads = [
         copy_out(own_hbm, own_ref, sems.at[0]),
         copy_out(gate_hbm, gate_ref, sems.at[1]),
         copy_out(got_hbm.at[:, UPSTREAM:CLASS, :], upstream_ref, sems.at[2]),
     ]
     group = place_ref[1]
+    tables[0].wait()
+    tables[1].wait()
     before_spec_ref[...] = spectrum(forward, jnp.concatenate([before_ref[b] for b in range(REACH)], axis=1))
     rows = lags_ref.shape[1] // (near_groups * far_groups)
     for low in range(near_groups):
@@ -163,7 +166,7 @@
             piece = lags_ref[:, at : at + rows, :].astype(F32).reshape(GROUP * rows, LANES)
             sorted_ref[pl.ds(row, GROUP * rows), lane(first // LEN)] = piece
     lag_spec_ref[...] = spectrum(forward, sorted_ref[...].astype(BF16))
-    copies = [copy_out(before_spec_ref, outs[0], sems.at[3]), copy_out(lag_spec_ref, outs[1], sems.at[4])]
+    copies = [copy_out(lag_spec_ref, lag_spec_hbm, sems.at[4])]
     loads[0].wait()
 
     def step(row, sign):
@@ -182,10 +185,12 @@
             product_ref[pl.ds(row + LEN, 8), col(block)] = total_imag
 
     over_frequencies(step)
+    tables[2].wait()
+    tables[3].wait()
     conv = invert(inverse, product_ref[...])
     conv_ref[...] = conv
     rounded_ref[...] = conv.astype(BF16)
-    copies += [copy_out(conv_ref, outs[2], sems.at[5]), copy_out(rounded_ref, outs[3], sems.at[6])]
+    copies.append(copy_out(rounded_ref, rounded_hbm, sems.at[3]))
     loads[1].wait()
     loads[2].wait()
     ones = jnp.ones((8, LANES), BF16)
@@ -205,7 +210,6 @@
             line = index * (GROUP // 2) + pair
             for peer in range(sums_ref.shape[0]):
                 sums_ref[peer, line : line + 1, :] = both
-    copies.append(copy_out(sums_ref, outs[4], sems.at[7]))
     for copy in copies:
         copy.wait()
 
@@ -217,18 +221,9 @@
     return jnp.transpose(jnp.concatenate([inv_rms, total[half:] * inv_rms / channels], axis=0))
 
 
-def finish_norm(
-    channels, sums_ref, conv_hbm, gate_hbm, got_hbm, grad_ref, first_ref, conv_ref, gate_ref, upstream_ref, sems
-):
-    loads = [
-        copy_out(conv_hbm, conv_ref, sems.at[0]),
-        copy_out(gate_hbm, gate_ref, sems.at[1]),
-        copy_out(got_hbm.at[:, UPSTREAM:CLASS, :], upstream_ref, sems.at[2]),
-    ]
+def finish_norm(channels, sums_ref, conv_ref, gate_ref, upstream_ref, grad_ref, first_ref):
     lines = row_lines(channels, sums_ref)
     half = GROUP // 2
-    for load in loads:
-        load.wait()
     for block in range(GROUP):
         rows = slice((block % 2) * LEN, (block % 2 + 1) * LEN)
         inv = lines[rows, block // 2 : block // 2 + 1]
@@ -242,14 +237,11 @@
 
 
 def filter_terms(
-    grad_ref, own_hbm, before_hbm, forward_high, forward_low, inverse_high, inverse_low, spec_out,
-    terms_out, product_ref, terms_ref, grad_spec_ref, own_ref, before_ref, sems,
+    grad_ref, own_ref, before_ref, forward_high, forward_low, inverse_high, inverse_low, grad_spec_hbm, terms_ref,
+    product_ref, grad_spec_ref, sems,
 ):
-    copies = [copy_out(own_hbm, own_ref, sems.at[0]), copy_out(before_hbm, before_ref, sems.at[1])]
     grad_spec_ref[...] = spectrum((forward_high, forward_low), grad_ref[...])
-    for copy in copies:
-        copy.wait()
-    copies = [copy_out(grad_spec_ref, spec_out, sems.at[2])]
+    copy = copy_out(grad_spec_ref, grad_spec_hbm, sems.at[0])
 
     def step(row, sign):
         real, imag = read_blocks(own_ref, before_ref, row)
@@ -270,16 +262,20 @@
     terms = invert((inverse_high, inverse_low), product_ref[...])
     for d in range(REACH):
         terms_ref[d] = terms[:, col(d)].astype(BF16)
-    copies.append(copy_out(terms_ref, terms_out, sems.at[3]))
-    for copy in copies:
-        copy.wait()
+    copy.wait()
 
 
 def correlate_back(
-    grad_spec_ref, after_ref, lag_spec_ref, forward_high, forward_low, inverse_high, inverse_low, result_ref,
-    after_spec_ref, product_ref,
+    grad_spec_hbm, lag_spec_hbm, after_ref, forward_high, forward_low, inverse_high, inverse_low, result_ref,
+    after_spec_ref, product_ref, grad_spec_ref, lag_spec_ref, sems,
 ):
+    loads = [
+        copy_out(grad_spec_hbm, grad_spec_ref, sems.at[0]),
+        copy_out(lag_spec_hbm, lag_spec_ref, sems.at[1]),
+    ]
     after_spec_ref[...] = spectrum((forward_high, forward_low), after_ref[...])
+    for load in loads:
+        load.wait()
 
     def step(row, sign):
         real = [grad_spec_ref[pl.ds(row, 8), col(b)] for b in range(GROUP)]
@@ -362,7 +358,7 @@
     return pltpu.with_memory_space_constraint(value, pltpu.HBM)
 
 
-def call(body, outs, *args, scalars=0, scratch=(), copies=0, left=(), manual=False, cost=1000):
+def call(body, outs, *args, scalars=0, scratch=(), copies=0, left=(), manual=(), cost=1000):
     specs = [pl.BlockSpec(memory_space=pltpu.SMEM)] * scalars
     specs += [
         pl.BlockSpec(memory_space=pl.ANY if index in left else pltpu.VMEM) for index in range(scalars, len(args))
@@ -372,7 +368,7 @@
         body,
         out_shape=list(outs),
         in_specs=specs,
-        out_specs=[pl.BlockSpec(memory_space=pl.ANY if manual else pltpu.VMEM)] * len(outs),
+        out_specs=[pl.BlockSpec(memory_space=pl.ANY if i in manual else pltpu.VMEM) for i in range(len(outs))],
         scratch_shapes=[pltpu.VMEM(shape, dtype) for shape, dtype in scratch]
         + ([pltpu.SemaphoreType.DMA(copies)] if copies else []),
         cost_estimate=pl.CostEstimate(flops=cost, bytes_accessed=moved, transcendentals=0),
@@ -400,13 +396,13 @@
     half = wide // 2
     place = jnp.stack([lax.axis_index("j"), lax.axis_index("g")]).astype(jnp.int32)
     tables = [jnp.asarray(t) for t in transform_tables()]
-    far_tables, near_tables = list(map(far, tables)), list(map(near, tables))
+    far_tables = list(map(far, tables))
     stock_id, stock_class = far(stock_id[None, :]), far(stock_class[None, :])
     table = far(jnp.pad(cond_table, ((0, 16 - cond_table.shape[0]), (0, 0))))
 
     (sent,) = call(
         pack, [off_chip((GROUP, ROWS, LANES), BF16)], *map(far, (key_proj, value_proj, query_proj, cotangent)),
-        stock_id, stock_class, manual=True, copies=(GROUP,), scratch=[((GROUP, ROWS, LANES), BF16)],
+        stock_id, stock_class, manual=(0,), copies=(GROUP,), scratch=[((GROUP, ROWS, LANES), BF16)],
     )
     got = lax.all_to_all(sent, "j", 0, 0)
     lags = filters[None]
@@ -418,51 +414,50 @@
     got, lags = far(got), near(lax.all_to_all(lags, "j", 0, 0))
     own, gate = call(
         prepare, [off_chip((2 * LEN, wide), F32), off_chip((LEN, wide), F32)], place, table, got, *far_tables[:2],
-        scalars=1, copies=(2,), manual=True, scratch=[((2 * LEN, wide), F32), ((LEN, wide), F32)],
+        scalars=1, copies=(2,), manual=(0, 1), scratch=[((2 * LEN, wide), F32), ((LEN, wide), F32)],
         cost=2 * 4 * LEN * LEN * wide,
     )
-    before_spec, lag_spec, conv, rounded, sums = call(
+    results = call(
         functools.partial(convolve, near_groups, far_groups),
         [
-            off_chip((2 * LEN, half), F32), off_chip((2 * LEN, half), F32), off_chip((LEN, wide), F32),
-            off_chip((LEN, wide), BF16), off_chip((GROUP * parts, 8, 2 * LEN), F32),
-        ],
-        place, far(own), far(gate), got, before, lags, *far_tables, scalars=1, copies=(8,), manual=True, left=(1, 2, 3),
-        scratch=[
-            ((2 * LEN, half), F32), ((2 * LEN, half), F32), ((LEN, wide), F32), ((LEN, wide), BF16),
-            ((GROUP * parts, 8, 2 * LEN), F32), ((2 * LEN, wide), F32), ((LEN, wide), F32),
-            ((GROUP, LEN, LANES), BF16), ((2 * LEN, wide), F32), ((LEN, half), F32),
-        ],
+            on_chip((2 * LEN, wide), F32), on_chip((LEN, wide), F32), on_chip((GROUP, LEN, LANES), BF16),
+            on_chip((2 * LEN, half), F32), on_chip((LEN, wide), F32),
+        ]
+        + [on_chip(t.shape, BF16) for t in tables]
+        + [off_chip((2 * LEN, half), F32), off_chip((LEN, wide), BF16), off_chip((GROUP * parts, 8, 2 * LEN), F32)],
+        place, far(own), far(gate), got, before, lags, *far_tables, scalars=1, copies=(9,), manual=(9, 10),
+        left=(1, 2, 3, 6, 7, 8, 9),
+        scratch=[((2 * LEN, half), F32), ((LEN, wide), BF16), ((2 * LEN, wide), F32), ((LEN, half), F32)],
         cost=2 * 10 * LEN * LEN * wide,
     )
+    own, gate, upstream, before_spec, conv, *near_tables = map(near, results[:9])
+    lag_spec, rounded, sums = results[9:]
     sums = lax.all_to_all(sums, ("j", "ch"), 0, 0)
     grad_conv, first = call(
         functools.partial(finish_norm, wide * parts), [on_chip((LEN, wide), BF16), on_chip((LEN, half), BF16)],
-        far(sums), far(conv), far(gate), got, left=(1, 2, 3), copies=(3,),
-        scratch=[((LEN, wide), F32), ((LEN, wide), F32), ((GROUP, LEN, LANES), BF16)],
+        far(sums), conv, gate, upstream,
     )
     after = lax.ppermute(first, "g", [(i, i - 1) for i in range(1, groups)])
     grad_spec, terms = call(
         filter_terms, [off_chip((2 * LEN, wide), F32), off_chip((REACH, LEN, LANES), BF16)],
-        near(grad_conv), far(own), far(before_spec), *far_tables, left=(1, 2), manual=True, copies=(4,),
-        scratch=[
-            ((2 * LEN, half), F32), ((REACH, LEN, LANES), BF16), ((2 * LEN, wide), F32), ((2 * LEN, wide), F32),
-            ((2 * LEN, half), F32),
-        ],
+        near(grad_conv), own, before_spec, *near_tables, copies=(1,), manual=(0,),
+        scratch=[((2 * LEN, half), F32), ((2 * LEN, wide), F32)],
         cost=2 * 7 * LEN * LEN * wide,
     )
+    (back,) = call(
+        correlate_back, [on_chip((LEN, wide), BF16)], far(grad_spec), far(lag_spec), after, *far_tables, left=(0, 1),
+        copies=(2,),
+        scratch=[((2 * LEN, half), F32), ((2 * LEN, wide), F32), ((2 * LEN, wide), F32), ((2 * LEN, half), F32)],
+        cost=2 * 8 * LEN * LEN * wide,
+    )
+    back = call(pack_back, [on_chip((2 * LEN, LANES), BF16)] * GROUP, place, near(back), rounded, scalars=1)
+    back = swap(back)
     terms = lax.all_to_all(terms.reshape(groups * GROUP, lag_rows, LANES), ("g", "j"), 0, 0)
-    (back,) = call(
-        correlate_back, [off_chip((LEN, wide), BF16)], far(grad_spec), after, far(lag_spec), *far_tables,
-        scratch=[((2 * LEN, half), F32), ((2 * LEN, wide), F32)], cost=2 * 8 * LEN * LEN * wide,
-    )
-    back = call(pack_back, [on_chip((2 * LEN, LANES), BF16)] * GROUP, place, back, rounded, scalars=1)
-    back = swap(back)
     (grad_filter,) = call(sum_terms, [off_chip((lag_rows, wide), F32)], terms)
     outs = call(
         functools.partial(finish, wide * parts),
         [off_chip((LEN, wide), BF16)] * 4,
-        place, near(sums), *map(near, (query_proj, key_proj, value_proj, cotangent)), stock_id, stock_class, table,
+        place, far(sums), *map(near, (query_proj, key_proj, value_proj, cotangent)), stock_id, stock_class, table,
         *map(near, back), scalars=1, scratch=[((2 * LEN, GROUP), F32)],
     )
     return *outs, grad_filter

time: 122 us -> 115 us (0.943)
  Pallas kernels: 35.3 us -> 29.9 us
    pallas_call x10, Pallas kernels: 35.3 us -> 29.9 us  [call(): pl.pallas_call(body, out_shape=list(outs), in_specs=specs, out_specs=[pl....]
  transfers between devices with their start and end apart: 18 -> 18, of which waited for: 11 -> 11; matrix products, arithmetic and copies ran while one was open for 1% -> 1% of each run, Pallas kernels for 17% -> 16%
where the time goes in v3:
time: 115 us; the launch traced here: 114 us
  starting transfers between devices  46.7 us (41%)
  Pallas kernels  29.9 us (26%)
  waiting for transfers between devices  21.4 us (19%)
  blocking collectives  14.7 us (13%)
    pallas_call x10, Pallas kernels, call(): pl.pallas_call(body, out_shape=list(outs), in_specs=specs, out_specs=[pl....  29.9 us
    all_to_all x1, blocking collectives, shards(): sums = lax.all_to_all(sums, ('j', 'ch'), 0, 0)  14.7 us
    all_to_all x1, starting transfers between devices, shards(): lax.all_to_all(terms.reshape(groups * GROUP, lag_rows, LANES), ('g', 'j')...  13.3 us
    ppermute x6, starting transfers between devices, trade(): return lax.ppermute(value, 'g', [(i, i ^ mask) for i in range(groups)])  10.2 us
    ppermute x7, waiting for transfers between devices, swap(): lax.ppermute(pieces[step], 'j', [(i, (i + step) % GROUP) for i in range(G...  9.47 us
    ppermute x6, waiting for transfers between devices, trade(): return lax.ppermute(value, 'g', [(i, i ^ mask) for i in range(groups)])  8.26 us
    ppermute x7, starting transfers between devices, swap(): lax.ppermute(pieces[step], 'j', [(i, (i + step) % GROUP) for i in range(G...  7.53 us
    all_to_all x1, starting transfers between devices, shards(): got = lax.all_to_all(sent, 'j', 0, 0)  6.87 us
  transfers between devices with their start and end apart: 18, of which 11 were waited for; matrix products, arithmetic and copies ran while one was open for 1% of the time, Pallas kernels for 16%

profile of v3, /device:TPU:1, one launch (start us, length us, event | category | flops | bytes accessed | tf_op | source)
XLA Modules:
  0.0 114.4 jit_solution(6659170821949499753)
XLA Ops:
  0.6 2.9 %shard_map.155 = bf16[8,784,128]{2,1,0:T(8,128)(2,1)} custom-call(bf16[256,1024]{1,0:T(8,128)(2,1)} %key_ref.3, bf16[256,1024]{1,0:T(8,128)(2,1)} %value_ref.3, bf16[256,1024]{1,0:T(8,128)(2,1)} %query_ref.3, bf16[256,1024]{1,0:T(8,128)(2,1)} %cotangent_ref.3, s32[1,256]{1,0:T(1,128)} %bitcast.13, s32[1,512]{1,0:T(1,128)} %bitcast.11), custom_call_target="tpu_custom_call" | custom-call | flops 1000 | bytes 2100224 | tf_op jit(solution)/shard_map/pallas_call | solution.py:367
  3.6 6.9 %all-to-all-start = ((bf16[8,784,128]{2,1,0:T(8,128)(2,1)}), bf16[8,784,128]{2,1,0:T(8,128)(2,1)S(1)}, u32[]{:S(2)}, u32[]{:S(2)}) async-start(bf16[8,784,128]{2,1,0:T(8,128)(2,1)} %shard_map.155), calls=%async_computation | async-start | bytes 3211264 | tf_op jit(solution)/shard_map/all_to_all | solution.py:407
  10.5 5.3 %collective-permute-start.2 = (bf16[1,8,1024]{2,1,0:T(8,128)(2,1)S(1)}, bf16[1,8,1024]{2,1,0:T(8,128)(2,1)S(1)}, u32[]{:S(2)}, u32[]{:S(2)}) collective-permute-start(bf16[1,8,1024]{2,1,0:T(8,128)(2,1)S(1)} %bitcast.7), channel_id=1, source_target_pairs={{0,192},{16,208},{32,224},{48,240},{64,128},{80,144},{96,160},{112... | collective-permute-start | bytes 49160 | tf_op jit(solution)/shard_map/ppermute | solution.py:386
  17.9 4.4 %collective-permute-done.1 = bf16[1,8,1024]{2,1,0:T(8,128)(2,1)S(1)} collective-permute-done((bf16[1,8,1024]{2,1,0:T(8,128)(2,1)S(1)}, bf16[1,8,1024]{2,1,0:T(8,128)(2,1)S(1)}, u32[]{:S(2)}, u32[]{:S(2)}) %collective-permute-start.1) | collective-permute-done | bytes 16416 | tf_op jit(solution)/shard_map/ppermute | solution.py:386
  22.4 1.7 %collective-permute-start.5 = (bf16[4,8,1024]{2,1,0:T(8,128)(2,1)S(1)}, bf16[4,8,1024]{2,1,0:T(8,128)(2,1)S(1)}, u32[]{:S(2)}, u32[]{:S(2)}) collective-permute-start(bf16[4,8,1024]{2,1,0:T(8,128)(2,1)S(1)} %pad_maximum_fusion.refs_0_), channel_id=1, source_target_pairs={{0,48},{16,32},{32,16},{48,0},{64,112},{80,96},{96,80},{112,64},{1... | collective-permute-start | bytes 196616 | tf_op jit(solution)/shard_map/ppermute | solution.py:386
  25.1 1.6 %collective-permute-done.5.refs_3_ = bf16[4,8,1024]{2,1,0:T(8,128)(2,1)S(1)} collective-permute-done((bf16[4,8,1024]{2,1,0:T(8,128)(2,1)S(1)}, bf16[4,8,1024]{2,1,0:T(8,128)(2,1)S(1)}, u32[]{:S(2)}, u32[]{:S(2)}) %collective-permute-start.5) | collective-permute-done | bytes 65568 | tf_op jit(solution)/shard_map/ppermute | solution.py:386
  27.2 1.8 %collective-permute-done.3.refs_1_ = bf16[4,8,1024]{2,1,0:T(8,128)(2,1)S(1)} collective-permute-done((bf16[4,8,1024]{2,1,0:T(8,128)(2,1)S(1)}, bf16[4,8,1024]{2,1,0:T(8,128)(2,1)S(1)}, u32[]{:S(2)}, u32[]{:S(2)}) %collective-permute-start.3) | collective-permute-done | bytes 65568 | tf_op jit(solution)/shard_map/ppermute | solution.py:386
  29.7 1.9 %all-to-all-done.got_ref.got_hbm = bf16[8,784,128]{2,1,0:T(8,128)(2,1)S(1)} async-done(((bf16[8,784,128]{2,1,0:T(8,128)(2,1)}), bf16[8,784,128]{2,1,0:T(8,128)(2,1)S(1)}, u32[]{:S(2)}, u32[]{:S(2)}) %all-to-all-start) | async-done | bytes 1605664 | tf_op jit(solution)/shard_map/all_to_all | solution.py:407
  31.6 2.4 %collective-permute-start.6 = (bf16[4,256,128]{2,1,0:T(8,128)(2,1)S(1)}, bf16[4,256,128]{2,1,0:T(8,128)(2,1)S(1)}, u32[]{:S(2)}, u32[]{:S(2)}) collective-permute-start(bf16[4,256,128]{2,1,0:T(8,128)(2,1)S(1)} %slice.3), channel_id=1, source_target_pairs={{0,16},{16,32},{32,48},{48,64},{64,80},{80,96},{96,112},{112,128},... | collective-permute-start | bytes 786440 | tf_op jit(solution)/shard_map/ppermute | solution.py:413
  33.9 5.2 %all-to-all-start.1 = ((bf16[8,128,128]{2,1,0:T(8,128)(2,1)}), bf16[8,128,128]{2,1,0:T(8,128)(2,1)S(1)}, u32[]{:S(2)}, u32[]{:S(2)}) async-start(bf16[8,128,128]{2,1,0:T(8,128)(2,1)} %shard_map.156), calls=%async_computation.1 | async-start | bytes 524288 | tf_op jit(solution)/shard_map/all_to_all | solution.py:414
  39.9 3.9 %shard_map.157 = (f32[512,1024]{1,0:T(8,128)}, f32[256,1024]{1,0:T(8,128)}) custom-call(s32[2]{0:T(128)S(1)} %pad_add_fusion.place_ref, f32[16,1024]{1,0:T(8,128)} %pad.4.table_ref, bf16[8,784,128]{2,1,0:T(8,128)(2,1)} %copy-done.5, bf16[512,256]{1,0:T(8,128)(2,1)} %constant.22.clone.forward_high.refs_0_, bf16[512,256]{1,0:T(8,128)(2,1)} %constant.23.clone.forward_low.refs_1_), custom_call_target="tpu_custom_call" | custom-call | flops 536870912 | bytes 2195464 | tf_op jit(solution)/shard_map/pallas_call | solution.py:367
  43.8 1.9 %all-to-all-done.1.lags_ref = bf16[8,128,128]{2,1,0:T(8,128)(2,1)S(1)} async-done(((bf16[8,128,128]{2,1,0:T(8,128)(2,1)}), bf16[8,128,128]{2,1,0:T(8,128)(2,1)S(1)}, u32[]{:S(2)}, u32[]{:S(2)}) %all-to-all-start.1) | async-done | bytes 262176 | tf_op jit(solution)/shard_map/all_to_all | solution.py:414
  45.7 6.4 %shard_map.158 = (f32[512,1024]{1,0:T(8,128)S(1)}, f32[256,1024]{1,0:T(8,128)S(1)}, bf16[8,256,128]{2,1,0:T(8,128)(2,1)S(1)}, f32[512,512]{1,0:T(8,128)S(1)}, f3...) custom-call(s32[2]{0:T(128)S(1)} %pad_add_fusion.place_ref, ...), custom_call_target="tpu_custom_call" | custom-call | flops 1342177280 | bytes 6324232 | tf_op jit(solution)/shard_map/pallas_call | solution.py:367
  52.1 14.7 %all_to_all.20.sums_ref = f32[16,8,512]{2,1,0:T(8,128)} all-to-all(f32[16,8,512]{2,1,0:T(8,128)} %get-tuple-element.41), channel_id=1, replica_groups=mesh['g'=16,'j'=8,'ch'=2] {'j','ch'}, dimensions={0} | all-to-all | bytes 524288 | tf_op jit(solution)/shard_map/all_to_all | solution.py:435
  66.8 1.7 %shard_map.159 = (bf16[256,1024]{1,0:T(8,128)(2,1)S(1)}, bf16[256,512]{1,0:T(8,128)(2,1)S(1)}) custom-call(f32[16,8,512]{2,1,0:T(8,128)} %all_to_all.20.sums_ref, f32[256,1024]{1,0:T(8,128)S(1)} %get-tuple-element.42.conv_ref, f32[256,1024]{1,0:T(8,128)S(1)} %get-tuple-element.43.gate_ref, bf16[8,256,128]{2,1,0:T(8,128)(2,1)S(1)} %get-tuple-element.44.upstream_ref), custom_call_target="tpu_custom_call" | custom-call | flops 1000 | bytes 2883584 | tf_op jit(solution)/shard_map/pallas_call | solution.py:367
  69.9 3.4 %shard_map.160 = (f32[512,1024]{1,0:T(8,128)}, bf16[4,256,128]{2,1,0:T(8,128)(2,1)}) custom-call(bf16[256,1024]{1,0:T(8,128)(2,1)S(1)} %get-tuple-element.45.grad_ref, f32[512,1024]{1,0:T(8,128)S(1)} %get-tuple-element.46.own_ref, f32[512,512]{1,0:T(8,128)S(1)} %get-tuple-element.47.before_ref, bf16[512,256]{1,0:T(8,128)(2,1)S(1)} %get-tuple-element.48.forward_high, ...), custom_call_target="tpu_custom_call" | custom-call | flops 939524096 | bytes 4718592 | tf_op jit(solution)/shard_map/pallas_call | solution.py:367
  73.3 13.3 %all-to-all-start.3 = ((bf16[128,8,128]{2,1,0:T(8,128)(2,1)}), bf16[128,8,128]{2,1,0:T(8,128)(2,1)S(1)}, u32[]{:S(2)}, u32[]{:S(2)}) async-start(bf16[128,8,128]{2,1,0:T(8,128)(2,1)} %bitcast.6), calls=%async_computation.3 | async-start | bytes 524288 | tf_op jit(solution)/shard_map/all_to_all | solution.py:455
  86.7 5.6 %shard_map.161.result_ref = bf16[256,1024]{1,0:T(8,128)(2,1)S(1)} custom-call(f32[512,1024]{1,0:T(8,128)} %get-tuple-element.52.grad_spec_hbm, f32[512,512]{1,0:T(8,128)} %get-tuple-element.53.lag_spec_hbm, bf16[256,512]{1,0:T(8,128)(2,1)S(1)} %collective-permute-done.7.after_ref, bf16[512,256]{1,0:T(8,128)(2,1)} %constant.22.clone.forward_high.refs_0_, ...), custom_call_target="tpu_custom_call" | custom-call | flops 1073741824 | bytes 4456448 | tf_op jit(solution)/shard_map/pallas_call | solution.py:367
  93.2 1.6 %collective-permute-start.8 = (bf16[512,128]{1,0:T(8,128)(2,1)S(1)}, bf16[512,128]{1,0:T(8,128)(2,1)S(1)}, u32[]{:S(2)}, u32[]{:S(2)}) collective-permute-start(bf16[512,128]{1,0:T(8,128)(2,1)S(1)} %get-tuple-element.57), channel_id=1, source_target_pairs={{0,2},{2,4},{4,6},{6,8},{8,10},{10,12},{12,14},{14,0},{1,3},{3,5},... | collective-permute-start | bytes 393224 | tf_op jit(solution)/shard_map/ppermute | solution.py:381
  96.0 1.6 %collective-permute-start.10 = (bf16[512,128]{1,0:T(8,128)(2,1)S(1)}, bf16[512,128]{1,0:T(8,128)(2,1)S(1)}, u32[]{:S(2)}, u32[]{:S(2)}) collective-permute-start(bf16[512,128]{1,0:T(8,128)(2,1)S(1)} %get-tuple-element.59), channel_id=1, source_target_pairs={{0,6},{2,8},{4,10},{6,12},{8,14},{10,0},{12,2},{14,4},{1,7},{3,9},... | collective-permute-start | bytes 393224 | tf_op jit(solution)/shard_map/ppermute | solution.py:381
  98.2 2.4 %collective-permute-start.12 = (bf16[512,128]{1,0:T(8,128)(2,1)S(1)}, bf16[512,128]{1,0:T(8,128)(2,1)S(1)}, u32[]{:S(2)}, u32[]{:S(2)}) collective-permute-start(bf16[512,128]{1,0:T(8,128)(2,1)S(1)} %get-tuple-element.61), channel_id=1, source_target_pairs={{0,10},{2,12},{4,14},{6,0},{8,2},{10,4},{12,6},{14,8},{1,11},{3,13... | collective-permute-start | bytes 393224 | tf_op jit(solution)/shard_map/ppermute | solution.py:381
  100.7 2.5 %collective-permute-done.9.refs_2_ = bf16[512,128]{1,0:T(8,128)(2,1)S(1)} collective-permute-done((bf16[512,128]{1,0:T(8,128)(2,1)S(1)}, bf16[512,128]{1,0:T(8,128)(2,1)S(1)}, u32[]{:S(2)}, u32[]{:S(2)}) %collective-permute-start.9) | collective-permute-done | bytes 131104 | tf_op jit(solution)/shard_map/ppermute | solution.py:381
  104.1 5.0 %collective-permute-done.11.refs_4_ = bf16[512,128]{1,0:T(8,128)(2,1)S(1)} collective-permute-done((bf16[512,128]{1,0:T(8,128)(2,1)S(1)}, bf16[512,128]{1,0:T(8,128)(2,1)S(1)}, u32[]{:S(2)}, u32[]{:S(2)}) %collective-permute-start.11) | collective-permute-done | bytes 131104 | tf_op jit(solution)/shard_map/ppermute | solution.py:381
  110.2 3.6 %shard_map.163 = (bf16[256,1024]{1,0:T(8,128)(2,1)}, bf16[256,1024]{1,0:T(8,128)(2,1)}, bf16[256,1024]{1,0:T(8,128)(2,1)}, bf16[256,1024]{1,0:T(8,128)(2,1)}) custom-call(s32[2]{0:T(128)S(1)} %pad_add_fusion.place_ref, f32[16,8,512]{2,1,0:T(8,128)} %all_to_all.20.sums_ref, bf16[256,1024]{1,0:T(8,128)(2,1)S(1)} %copy-done.2, bf16[256,1024]{1,0:T(8,128)(2,1)S(1)} %copy-done, ...), custom_call_target="tpu_custom_call" | custom-call | flops 1000 | bytes 3476488 | tf_op jit(solution)/shard_map/pallas_call | solution.py:367
  (43 shorter events, 11.8 us)
Async XLA Ops:
  3.6 35.6 %copy-start.6 = (f32[11,1024]{1,0:T(8,128)S(1)}, f32[11,1024]{1,0:T(8,128)}, u32[]{:S(2)}) copy-start(f32[11,1024]{1,0:T(8,128)} %param.19) | copy-start | bytes 135172
  3.6 28.0 %all-to-all-start = ((bf16[8,784,128]{2,1,0:T(8,128)(2,1)}), bf16[8,784,128]{2,1,0:T(8,128)(2,1)S(1)}, u32[]{:S(2)}, u32[]{:S(2)}) async-start(bf16[8,784,128]{2,1,0:T(8,128)(2,1)} %shard_map.155), calls=%async_computation | async-start | bytes 3211264 | tf_op jit(solution)/shard_map/all_to_all | solution.py:407
  10.5 7.5 %collective-permute-start.2 = (bf16[1,8,1024]{2,1,0:T(8,128)(2,1)S(1)}, bf16[1,8,1024]{2,1,0:T(8,128)(2,1)S(1)}, u32[]{:S(2)}, u32[]{:S(2)}) collective-permute-start(bf16[1,8,1024]{2,1,0:T(8,128)(2,1)S(1)} %bitcast.7), channel_id=1, source_target_pairs={{0,192},{16,208},{32,224},{48,240},{64,128},{80,144},{96,160},{112... | collective-permute-start | bytes 49160 | tf_op jit(solution)/shard_map/ppermute | solution.py:386
  15.8 6.6 %collective-permute-start.1 = (bf16[1,8,1024]{2,1,0:T(8,128)(2,1)S(1)}, bf16[1,8,1024]{2,1,0:T(8,128)(2,1)S(1)}, u32[]{:S(2)}, u32[]{:S(2)}) collective-permute-start(bf16[1,8,1024]{2,1,0:T(8,128)(2,1)S(1)} %bitcast.8), channel_id=1, source_target_pairs={{0,128},{16,144},{32,160},{48,176},{64,192},{80,208},{96,224},{112... | collective-permute-start | bytes 49160 | tf_op jit(solution)/shard_map/ppermute | solution.py:386
  16.7 5.6 %collective-permute-start = (bf16[1,8,1024]{2,1,0:T(8,128)(2,1)S(1)}, bf16[1,8,1024]{2,1,0:T(8,128)(2,1)S(1)}, u32[]{:S(2)}, u32[]{:S(2)}) collective-permute-start(bf16[1,8,1024]{2,1,0:T(8,128)(2,1)S(1)} %bitcast.9), channel_id=1, source_target_pairs={{0,64},{16,80},{32,96},{48,112},{64,0},{80,16},{96,32},{112,48},{1... | collective-permute-start | bytes 49160 | tf_op jit(solution)/shard_map/ppermute | solution.py:386
  22.4 4.3 %collective-permute-start.5 = (bf16[4,8,1024]{2,1,0:T(8,128)(2,1)S(1)}, bf16[4,8,1024]{2,1,0:T(8,128)(2,1)S(1)}, u32[]{:S(2)}, u32[]{:S(2)}) collective-permute-start(bf16[4,8,1024]{2,1,0:T(8,128)(2,1)S(1)} %pad_maximum_fusion.refs_0_), channel_id=1, source_target_pairs={{0,48},{16,32},{32,16},{48,0},{64,112},{80,96},{96,80},{112,64},{1... | collective-permute-start | bytes 196616 | tf_op jit(solution)/shard_map/ppermute | solution.py:386
  24.0 3.2 %collective-permute-start.4 = (bf16[4,8,1024]{2,1,0:T(8,128)(2,1)S(1)}, bf16[4,8,1024]{2,1,0:T(8,128)(2,1)S(1)}, u32[]{:S(2)}, u32[]{:S(2)}) collective-permute-start(bf16[4,8,1024]{2,1,0:T(8,128)(2,1)S(1)} %pad_maximum_fusion.refs_0_), channel_id=1, source_target_pairs={{0,32},{16,48},{32,0},{48,16},{64,96},{80,112},{96,64},{112,80},{1... | collective-permute-start | bytes 196616 | tf_op jit(solution)/shard_map/ppermute | solution.py:386
  24.8 4.1 %collective-permute-start.3 = (bf16[4,8,1024]{2,1,0:T(8,128)(2,1)S(1)}, bf16[4,8,1024]{2,1,0:T(8,128)(2,1)S(1)}, u32[]{:S(2)}, u32[]{:S(2)}) collective-permute-start(bf16[4,8,1024]{2,1,0:T(8,128)(2,1)S(1)} %pad_maximum_fusion.refs_0_), channel_id=1, source_target_pairs={{0,16},{16,0},{32,48},{48,32},{64,80},{80,64},{96,112},{112,96},{1... | collective-permute-start | bytes 196616 | tf_op jit(solution)/shard_map/ppermute | solution.py:386
  31.6 8.3 %copy-start.5 = (bf16[8,784,128]{2,1,0:T(8,128)(2,1)}, bf16[8,784,128]{2,1,0:T(8,128)(2,1)S(1)}, u32[]{:S(2)}) copy-start(bf16[8,784,128]{2,1,0:T(8,128)(2,1)S(1)} %all-to-all-done.got_ref.got_hbm) | copy-start | bytes 4816900
  31.6 14.1 %collective-permute-start.6 = (bf16[4,256,128]{2,1,0:T(8,128)(2,1)S(1)}, bf16[4,256,128]{2,1,0:T(8,128)(2,1)S(1)}, u32[]{:S(2)}, u32[]{:S(2)}) collective-permute-start(bf16[4,256,128]{2,1,0:T(8,128)(2,1)S(1)} %slice.3), channel_id=1, source_target_pairs={{0,16},{16,32},{32,48},{48,64},{64,80},{80,96},{96,112},{112,128},... | collective-permute-start | bytes 786440 | tf_op jit(solution)/shard_map/ppermute | solution.py:413
  33.9 11.7 %all-to-all-start.1 = ((bf16[8,128,128]{2,1,0:T(8,128)(2,1)}), bf16[8,128,128]{2,1,0:T(8,128)(2,1)S(1)}, u32[]{:S(2)}, u32[]{:S(2)}) async-start(bf16[8,128,128]{2,1,0:T(8,128)(2,1)} %shard_map.156), calls=%async_computation.1 | async-start | bytes 524288 | tf_op jit(solution)/shard_map/all_to_all | solution.py:414
  68.6 18.0 %collective-permute-start.7 = (bf16[256,512]{1,0:T(8,128)(2,1)S(1)}, bf16[256,512]{1,0:T(8,128)(2,1)S(1)}, u32[]{:S(2)}, u32[]{:S(2)}) collective-permute-start(bf16[256,512]{1,0:T(8,128)(2,1)S(1)} %get-tuple-element.54), channel_id=1, source_target_pairs={{16,0},{32,16},{48,32},{64,48},{80,64},{96,80},{112,96},{128,112},... | collective-permute-start | bytes 786440 | tf_op jit(solution)/shard_map/ppermute | solution.py:440
  73.3 40.4 %all-to-all-start.3 = ((bf16[128,8,128]{2,1,0:T(8,128)(2,1)}), bf16[128,8,128]{2,1,0:T(8,128)(2,1)S(1)}, u32[]{:S(2)}, u32[]{:S(2)}) async-start(bf16[128,8,128]{2,1,0:T(8,128)(2,1)} %bitcast.6), calls=%async_computation.3 | async-start | bytes 524288 | tf_op jit(solution)/shard_map/all_to_all | solution.py:455
  86.7 23.5 %copy-start = (bf16[256,1024]{1,0:T(8,128)(2,1)S(1)}, bf16[256,1024]{1,0:T(8,128)(2,1)}, u32[]{:S(2)}) copy-start(bf16[256,1024]{1,0:T(8,128)(2,1)} %key_ref.3) | copy-start | bytes 1572868
  86.7 23.5 %copy-start.1 = (bf16[256,1024]{1,0:T(8,128)(2,1)S(1)}, bf16[256,1024]{1,0:T(8,128)(2,1)}, u32[]{:S(2)}) copy-start(bf16[256,1024]{1,0:T(8,128)(2,1)} %value_ref.3) | copy-start | bytes 1572868
  86.7 23.5 %copy-start.2 = (bf16[256,1024]{1,0:T(8,128)(2,1)S(1)}, bf16[256,1024]{1,0:T(8,128)(2,1)}, u32[]{:S(2)}) copy-start(bf16[256,1024]{1,0:T(8,128)(2,1)} %query_ref.3) | copy-start | bytes 1572868
  86.7 23.5 %copy-start.3 = (bf16[256,1024]{1,0:T(8,128)(2,1)S(1)}, bf16[256,1024]{1,0:T(8,128)(2,1)}, u32[]{:S(2)}) copy-start(bf16[256,1024]{1,0:T(8,128)(2,1)} %cotangent_ref.3) | copy-start | bytes 1572868
  93.2 7.5 %collective-permute-start.8 = (bf16[512,128]{1,0:T(8,128)(2,1)S(1)}, bf16[512,128]{1,0:T(8,128)(2,1)S(1)}, u32[]{:S(2)}, u32[]{:S(2)}) collective-permute-start(bf16[512,128]{1,0:T(8,128)(2,1)S(1)} %get-tuple-element.57), channel_id=1, source_target_pairs={{0,2},{2,4},{4,6},{6,8},{8,10},{10,12},{12,14},{14,0},{1,3},{3,5},... | collective-permute-start | bytes 393224 | tf_op jit(solution)/shard_map/ppermute | solution.py:381
  94.8 8.4 %collective-permute-start.9 = (bf16[512,128]{1,0:T(8,128)(2,1)S(1)}, bf16[512,128]{1,0:T(8,128)(2,1)S(1)}, u32[]{:S(2)}, u32[]{:S(2)}) collective-permute-start(bf16[512,128]{1,0:T(8,128)(2,1)S(1)} %get-tuple-element.58), channel_id=1, source_target_pairs={{0,4},{2,6},{4,8},{6,10},{8,12},{10,14},{12,0},{14,2},{1,5},{3,7},... | collective-permute-start | bytes 393224 | tf_op jit(solution)/shard_map/ppermute | solution.py:381
  96.0 8.1 %collective-permute-start.10 = (bf16[512,128]{1,0:T(8,128)(2,1)S(1)}, bf16[512,128]{1,0:T(8,128)(2,1)S(1)}, u32[]{:S(2)}, u32[]{:S(2)}) collective-permute-start(bf16[512,128]{1,0:T(8,128)(2,1)S(1)} %get-tuple-element.59), channel_id=1, source_target_pairs={{0,6},{2,8},{4,10},{6,12},{8,14},{10,0},{12,2},{14,4},{1,7},{3,9},... | collective-permute-start | bytes 393224 | tf_op jit(solution)/shard_map/ppermute | solution.py:381
  97.6 11.5 %collective-permute-start.11 = (bf16[512,128]{1,0:T(8,128)(2,1)S(1)}, bf16[512,128]{1,0:T(8,128)(2,1)S(1)}, u32[]{:S(2)}, u32[]{:S(2)}) collective-permute-start(bf16[512,128]{1,0:T(8,128)(2,1)S(1)} %get-tuple-element.60), channel_id=1, source_target_pairs={{0,8},{2,10},{4,12},{6,14},{8,0},{10,2},{12,4},{14,6},{1,9},{3,11}... | collective-permute-start | bytes 393224 | tf_op jit(solution)/shard_map/ppermute | solution.py:381
  98.2 11.5 %collective-permute-start.12 = (bf16[512,128]{1,0:T(8,128)(2,1)S(1)}, bf16[512,128]{1,0:T(8,128)(2,1)S(1)}, u32[]{:S(2)}, u32[]{:S(2)}) collective-permute-start(bf16[512,128]{1,0:T(8,128)(2,1)S(1)} %get-tuple-element.61), channel_id=1, source_target_pairs={{0,10},{2,12},{4,14},{6,0},{8,2},{10,4},{12,6},{14,8},{1,11},{3,13... | collective-permute-start | bytes 393224 | tf_op jit(solution)/shard_map/ppermute | solution.py:381
  100.6 9.1 %collective-permute-start.13 = (bf16[512,128]{1,0:T(8,128)(2,1)S(1)}, bf16[512,128]{1,0:T(8,128)(2,1)S(1)}, u32[]{:S(2)}, u32[]{:S(2)}) collective-permute-start(bf16[512,128]{1,0:T(8,128)(2,1)S(1)} %get-tuple-element.62), channel_id=1, source_target_pairs={{0,12},{2,14},{4,0},{6,2},{8,4},{10,6},{12,8},{14,10},{1,13},{3,15... | collective-permute-start | bytes 393224 | tf_op jit(solution)/shard_map/ppermute | solution.py:381
  103.2 6.9 %collective-permute-start.14 = (bf16[512,128]{1,0:T(8,128)(2,1)S(1)}, bf16[512,128]{1,0:T(8,128)(2,1)S(1)}, u32[]{:S(2)}, u32[]{:S(2)}) collective-permute-start(bf16[512,128]{1,0:T(8,128)(2,1)S(1)} %get-tuple-element.63), channel_id=1, source_target_pairs={{0,14},{2,0},{4,2},{6,4},{8,6},{10,8},{12,10},{14,12},{1,15},{3,1}... | collective-permute-start | bytes 393224 | tf_op jit(solution)/shard_map/ppermute | solution.py:381
  (2 other events, 12.6 us)

commit v4 on v3

--- a/solution.py
+++ b/solution.py
@@ -265,14 +265,28 @@
     copy.wait()
 
 
-def correlate_back(
-    grad_spec_hbm, lag_spec_hbm, after_ref, forward_high, forward_low, inverse_high, inverse_low, result_ref,
-    after_spec_ref, product_ref, grad_spec_ref, lag_spec_ref, sems,
-):
+def correlate_back(place_ref, *refs):
+    tables_hbm, (grad_spec_hbm, lag_spec_hbm, rounded_hbm, after_ref) = refs[:4], refs[4:8]
+    out_refs, tables = refs[8 : 8 + GROUP], refs[8 + GROUP : 12 + GROUP]
+    result_ref, after_spec_ref, product_ref, grad_spec_ref, lag_spec_ref, sems = refs[12 + GROUP :]
+    place = place_ref[0]
+    table_loads = [copy_out(tables_hbm[i], tables[i], sems.at[i]) for i in range(2)]
     loads = [
-        copy_out(grad_spec_hbm, grad_spec_ref, sems.at[0]),
-        copy_out(lag_spec_hbm, lag_spec_ref, sems.at[1]),
+        copy_out(grad_spec_hbm, grad_spec_ref, sems.at[4]),
+        copy_out(lag_spec_hbm, lag_spec_ref, sems.at[5]),
     ]
+    table_loads += [copy_out(tables_hbm[i], tables[i], sems.at[i]) for i in range(2, 4)]
+    copies = [
+        copy_out(
+            rounded_hbm.at[:, lane((place + step_number) & (GROUP - 1))],
+            out_refs[step_number].at[LEN:, :],
+            sems.at[6 + step_number],
+        )
+        for step_number in range(GROUP)
+    ]
+    (forward_high, forward_low), (inverse_high, inverse_low) = tables[:2], tables[2:]
+    table_loads[0].wait()
+    table_loads[1].wait()
     after_spec_ref[...] = spectrum((forward_high, forward_low), after_ref[...])
     for load in loads:
         load.wait()
@@ -298,14 +312,13 @@
             product_ref[pl.ds(row + LEN, 8), col(block)] = total_imag
 
     over_frequencies(step)
+    table_loads[2].wait()
+    table_loads[3].wait()
     result_ref[...] = invert((inverse_high, inverse_low), product_ref[...]).astype(BF16)
-
-
-def pack_back(place_ref, result_ref, rounded_ref, *out_refs):
-    for step in range(GROUP):
-        there = lane((place_ref[0] + step) & (GROUP - 1))
-        out_refs[step][:LEN, :] = result_ref[:, there]
-        out_refs[step][LEN:, :] = rounded_ref[:, there]
+    for step_number in range(GROUP):
+        out_refs[step_number][:LEN, :] = result_ref[:, lane((place + step_number) & (GROUP - 1))]
+    for copy in copies:
+        copy.wait()
 
 
 def sum_terms(terms_ref, out_ref):
@@ -317,9 +330,8 @@
 def finish(
     channels, place_ref, sums_ref, query_ref, key_ref, value_ref, cotangent_ref, stock_ref, class_ref, table_ref, *refs
 ):
-    pieces, (normed_ref, grad_query_ref, grad_key_ref, grad_value_ref, lines_ref) = (
-        refs[:GROUP], refs[GROUP:]
-    )
+    pieces = refs[:GROUP]
+    normed_ref, grad_query_ref, grad_key_ref, grad_value_ref, factor_ref, lines_ref = refs[GROUP:]
     place = place_ref[0]
     half = GROUP // 2
     lines_ref[...] = row_lines(channels, sums_ref)
@@ -327,19 +339,19 @@
     number = lax.broadcasted_iota(jnp.int32, (LEN, GROUP), 1)
     inv = jnp.sum(jnp.where(number == place >> 1, lines, 0.0), axis=1, keepdims=True)
     mean = jnp.sum(jnp.where(number == half + (place >> 1), lines, 0.0), axis=1, keepdims=True)
-    event_class = event_classes(stock_ref, class_ref)[:1]
+    factor_ref[...] = modulation(event_classes(stock_ref, class_ref)[:1], table_ref[...])
     for step in range(GROUP):
         there = lane((place - step) & (GROUP - 1))
         piece = pieces[step]
-        factor = modulation(event_class, table_ref[:, there])
+        grad_mixed = piece[:LEN, :].astype(F32)
+        grad_key_ref[:, there] = (grad_mixed * value_ref[:, there].astype(F32)).astype(BF16)
+        grad_value_ref[:, there] = (grad_mixed * key_ref[:, there].astype(F32)).astype(BF16)
+        factor = factor_ref[:, there]
         conv = piece[LEN:, :].astype(F32)
         normed = query_ref[:, there].astype(F32) * factor * conv * inv
         normed_ref[:, there] = normed.astype(BF16)
         grad_scaled = inv * (cotangent_ref[:, there].astype(F32) - normed * mean)
         grad_query_ref[:, there] = (grad_scaled * conv * factor).astype(BF16)
-        grad_mixed = piece[:LEN, :].astype(F32)
-        grad_key_ref[:, there] = (grad_mixed * value_ref[:, there].astype(F32)).astype(BF16)
-        grad_value_ref[:, there] = (grad_mixed * key_ref[:, there].astype(F32)).astype(BF16)
 
 
 def on_chip(shape, dtype):
@@ -424,7 +436,7 @@
             on_chip((2 * LEN, half), F32), on_chip((LEN, wide), F32),
         ]
         + [on_chip(t.shape, BF16) for t in tables]
-        + [off_chip((2 * LEN, half), F32), off_chip((LEN, wide), BF16), off_chip((GROUP * parts, 8, 2 * LEN), F32)],
+        + [off_chip((2 * LEN, half), F32), off_chip((LEN, wide), BF16), on_chip((GROUP * parts, 8, 2 * LEN), F32)],
         place, far(own), far(gate), got, before, lags, *far_tables, scalars=1, copies=(9,), manual=(9, 10),
         left=(1, 2, 3, 6, 7, 8, 9),
         scratch=[((2 * LEN, half), F32), ((LEN, wide), BF16), ((2 * LEN, wide), F32), ((LEN, half), F32)],
@@ -435,7 +447,7 @@
     sums = lax.all_to_all(sums, ("j", "ch"), 0, 0)
     grad_conv, first = call(
         functools.partial(finish_norm, wide * parts), [on_chip((LEN, wide), BF16), on_chip((LEN, half), BF16)],
-        far(sums), conv, gate, upstream,
+        near(sums), conv, gate, upstream,
     )
     after = lax.ppermute(first, "g", [(i, i - 1) for i in range(1, groups)])
     grad_spec, terms = call(
@@ -444,13 +456,16 @@
         scratch=[((2 * LEN, half), F32), ((2 * LEN, wide), F32)],
         cost=2 * 7 * LEN * LEN * wide,
     )
-    (back,) = call(
-        correlate_back, [on_chip((LEN, wide), BF16)], far(grad_spec), far(lag_spec), after, *far_tables, left=(0, 1),
-        copies=(2,),
-        scratch=[((2 * LEN, half), F32), ((2 * LEN, wide), F32), ((2 * LEN, wide), F32), ((2 * LEN, half), F32)],
+    back = call(
+        correlate_back, [on_chip((2 * LEN, LANES), BF16)] * GROUP, place, *far_tables, far(grad_spec), far(lag_spec),
+        far(rounded), after, scalars=1, left=range(1, 8), copies=(6 + GROUP,),
+        scratch=[(t.shape, BF16) for t in tables]
+        + [
+            ((LEN, wide), BF16), ((2 * LEN, half), F32), ((2 * LEN, wide), F32), ((2 * LEN, wide), F32),
+            ((2 * LEN, half), F32),
+        ],
         cost=2 * 8 * LEN * LEN * wide,
     )
-    back = call(pack_back, [on_chip((2 * LEN, LANES), BF16)] * GROUP, place, near(back), rounded, scalars=1)
     back = swap(back)
     terms = lax.all_to_all(terms.reshape(groups * GROUP, lag_rows, LANES), ("g", "j"), 0, 0)
     (grad_filter,) = call(sum_terms, [off_chip((lag_rows, wide), F32)], terms)
@@ -458,7 +473,7 @@
         functools.partial(finish, wide * parts),
         [off_chip((LEN, wide), BF16)] * 4,
         place, far(sums), *map(near, (query_proj, key_proj, value_proj, cotangent)), stock_id, stock_class, table,
-        *map(near, back), scalars=1, scratch=[((2 * LEN, GROUP), F32)],
+        *map(near, back), scalars=1, scratch=[((LEN, wide), F32), ((2 * LEN, GROUP), F32)],
     )
     return *outs, grad_filter
 

time: 115 us -> 112 us (0.974)
  Pallas kernels: 29.9 us -> 27.2 us
    pallas_call x10 -> x9, Pallas kernels: 29.9 us -> 27.2 us  [call(): pl.pallas_call(body, out_shape=list(outs), in_specs=specs, out_specs=[pl....]
  transfers between devices with their start and end apart: 18 -> 18, of which waited for: 11 -> 11; matrix products, arithmetic and copies ran while one was open for 1% -> 1% of each run, Pallas kernels for 16% -> 15%
where the time goes in v4:
time: 112 us; the launch traced here: 111 us
  starting transfers between devices  46.7 us (42%)
  Pallas kernels  27.2 us (24%)
  waiting for transfers between devices  21.5 us (19%)
  blocking collectives  14.4 us (13%)
    pallas_call x9, Pallas kernels, call(): pl.pallas_call(body, out_shape=list(outs), in_specs=specs, out_specs=[pl....  27.2 us
    all_to_all x1, blocking collectives, shards(): sums = lax.all_to_all(sums, ('j', 'ch'), 0, 0)  14.4 us
    all_to_all x1, starting transfers between devices, shards(): lax.all_to_all(terms.reshape(groups * GROUP, lag_rows, LANES), ('g', 'j')...  13.3 us
    ppermute x6, starting transfers between devices, trade(): return lax.ppermute(value, 'g', [(i, i ^ mask) for i in range(groups)])  10.2 us
    ppermute x7, waiting for transfers between devices, swap(): lax.ppermute(pieces[step], 'j', [(i, (i + step) % GROUP) for i in range(G...  9.49 us
    ppermute x6, waiting for transfers between devices, trade(): return lax.ppermute(value, 'g', [(i, i ^ mask) for i in range(groups)])  8.26 us
    ppermute x7, starting transfers between devices, swap(): lax.ppermute(pieces[step], 'j', [(i, (i + step) % GROUP) for i in range(G...  7.55 us
    all_to_all x1, starting transfers between devices, shards(): got = lax.all_to_all(sent, 'j', 0, 0)  6.87 us
  transfers between devices with their start and end apart: 18, of which 11 were waited for; matrix products, arithmetic and copies ran while one was open for 1% of the time, Pallas kernels for 15%

profile of v4, /device:TPU:1, one launch (start us, length us, event | category | flops | bytes accessed | tf_op | source)
XLA Modules:
  0.0 111.4 jit_solution(5176443959535718571)
XLA Ops:
  0.6 2.9 %shard_map.155 = bf16[8,784,128]{2,1,0:T(8,128)(2,1)} custom-call(bf16[256,1024]{1,0:T(8,128)(2,1)} %key_ref.3, bf16[256,1024]{1,0:T(8,128)(2,1)} %value_ref.3, bf16[256,1024]{1,0:T(8,128)(2,1)} %query_ref.3, bf16[256,1024]{1,0:T(8,128)(2,1)} %cotangent_ref.3, s32[1,256]{1,0:T(1,128)} %bitcast.13, s32[1,512]{1,0:T(1,128)} %bitcast.11), custom_call_target="tpu_custom_call" | custom-call | flops 1000 | bytes 2100224 | tf_op jit(solution)/shard_map/pallas_call | solution.py:379
  3.6 6.9 %all-to-all-start = ((bf16[8,784,128]{2,1,0:T(8,128)(2,1)}), bf16[8,784,128]{2,1,0:T(8,128)(2,1)S(1)}, u32[]{:S(2)}, u32[]{:S(2)}) async-start(bf16[8,784,128]{2,1,0:T(8,128)(2,1)} %shard_map.155), calls=%async_computation | async-start | bytes 3211264 | tf_op jit(solution)/shard_map/all_to_all | solution.py:419
  10.5 5.3 %collective-permute-start.2 = (bf16[1,8,1024]{2,1,0:T(8,128)(2,1)S(1)}, bf16[1,8,1024]{2,1,0:T(8,128)(2,1)S(1)}, u32[]{:S(2)}, u32[]{:S(2)}) collective-permute-start(bf16[1,8,1024]{2,1,0:T(8,128)(2,1)S(1)} %bitcast.7), channel_id=1, source_target_pairs={{0,192},{16,208},{32,224},{48,240},{64,128},{80,144},{96,160},{112... | collective-permute-start | bytes 49160 | tf_op jit(solution)/shard_map/ppermute | solution.py:398
  17.9 4.4 %collective-permute-done.1 = bf16[1,8,1024]{2,1,0:T(8,128)(2,1)S(1)} collective-permute-done((bf16[1,8,1024]{2,1,0:T(8,128)(2,1)S(1)}, bf16[1,8,1024]{2,1,0:T(8,128)(2,1)S(1)}, u32[]{:S(2)}, u32[]{:S(2)}) %collective-permute-start.1) | collective-permute-done | bytes 16416 | tf_op jit(solution)/shard_map/ppermute | solution.py:398
  22.4 1.7 %collective-permute-start.5 = (bf16[4,8,1024]{2,1,0:T(8,128)(2,1)S(1)}, bf16[4,8,1024]{2,1,0:T(8,128)(2,1)S(1)}, u32[]{:S(2)}, u32[]{:S(2)}) collective-permute-start(bf16[4,8,1024]{2,1,0:T(8,128)(2,1)S(1)} %pad_maximum_fusion.refs_0_), channel_id=1, source_target_pairs={{0,48},{16,32},{32,16},{48,0},{64,112},{80,96},{96,80},{112,64},{1... | collective-permute-start | bytes 196616 | tf_op jit(solution)/shard_map/ppermute | solution.py:398
  25.1 1.6 %collective-permute-done.5.refs_3_ = bf16[4,8,1024]{2,1,0:T(8,128)(2,1)S(1)} collective-permute-done((bf16[4,8,1024]{2,1,0:T(8,128)(2,1)S(1)}, bf16[4,8,1024]{2,1,0:T(8,128)(2,1)S(1)}, u32[]{:S(2)}, u32[]{:S(2)}) %collective-permute-start.5) | collective-permute-done | bytes 65568 | tf_op jit(solution)/shard_map/ppermute | solution.py:398
  27.2 1.8 %collective-permute-done.3.refs_1_ = bf16[4,8,1024]{2,1,0:T(8,128)(2,1)S(1)} collective-permute-done((bf16[4,8,1024]{2,1,0:T(8,128)(2,1)S(1)}, bf16[4,8,1024]{2,1,0:T(8,128)(2,1)S(1)}, u32[]{:S(2)}, u32[]{:S(2)}) %collective-permute-start.3) | collective-permute-done | bytes 65568 | tf_op jit(solution)/shard_map/ppermute | solution.py:398
  29.7 1.9 %all-to-all-done.got_ref.got_hbm = bf16[8,784,128]{2,1,0:T(8,128)(2,1)S(1)} async-done(((bf16[8,784,128]{2,1,0:T(8,128)(2,1)}), bf16[8,784,128]{2,1,0:T(8,128)(2,1)S(1)}, u32[]{:S(2)}, u32[]{:S(2)}) %all-to-all-start) | async-done | bytes 1605664 | tf_op jit(solution)/shard_map/all_to_all | solution.py:419
  31.6 2.4 %collective-permute-start.6 = (bf16[4,256,128]{2,1,0:T(8,128)(2,1)S(1)}, bf16[4,256,128]{2,1,0:T(8,128)(2,1)S(1)}, u32[]{:S(2)}, u32[]{:S(2)}) collective-permute-start(bf16[4,256,128]{2,1,0:T(8,128)(2,1)S(1)} %slice.3), channel_id=1, source_target_pairs={{0,16},{16,32},{32,48},{48,64},{64,80},{80,96},{96,112},{112,128},... | collective-permute-start | bytes 786440 | tf_op jit(solution)/shard_map/ppermute | solution.py:425
  33.9 5.2 %all-to-all-start.1 = ((bf16[8,128,128]{2,1,0:T(8,128)(2,1)}), bf16[8,128,128]{2,1,0:T(8,128)(2,1)S(1)}, u32[]{:S(2)}, u32[]{:S(2)}) async-start(bf16[8,128,128]{2,1,0:T(8,128)(2,1)} %shard_map.156), calls=%async_computation.1 | async-start | bytes 524288 | tf_op jit(solution)/shard_map/all_to_all | solution.py:426
  39.9 3.9 %shard_map.157 = (f32[512,1024]{1,0:T(8,128)}, f32[256,1024]{1,0:T(8,128)}) custom-call(s32[2]{0:T(128)S(1)} %pad_add_fusion.place_ref, f32[16,1024]{1,0:T(8,128)} %pad.4.table_ref, bf16[8,784,128]{2,1,0:T(8,128)(2,1)} %copy-done.5, bf16[512,256]{1,0:T(8,128)(2,1)} %constant.22.clone.forward_high.refs_0_, bf16[512,256]{1,0:T(8,128)(2,1)} %constant.23.clone.forward_low.refs_1_), custom_call_target="tpu_custom_call" | custom-call | flops 536870912 | bytes 2195464 | tf_op jit(solution)/shard_map/pallas_call | solution.py:379
  43.8 1.9 %all-to-all-done.1.lags_ref = bf16[8,128,128]{2,1,0:T(8,128)(2,1)S(1)} async-done(((bf16[8,128,128]{2,1,0:T(8,128)(2,1)}), bf16[8,128,128]{2,1,0:T(8,128)(2,1)S(1)}, u32[]{:S(2)}, u32[]{:S(2)}) %all-to-all-start.1) | async-done | bytes 262176 | tf_op jit(solution)/shard_map/all_to_all | solution.py:426
  45.7 5.7 %shard_map.158 = (f32[512,1024]{1,0:T(8,128)S(1)}, f32[256,1024]{1,0:T(8,128)S(1)}, bf16[8,256,128]{2,1,0:T(8,128)(2,1)S(1)}, f32[512,512]{1,0:T(8,128)S(1)}, f3...) custom-call(s32[2]{0:T(128)S(1)} %pad_add_fusion.place_ref, ...), custom_call_target="tpu_custom_call" | custom-call | flops 1342177280 | bytes 6324232 | tf_op jit(solution)/shard_map/pallas_call | solution.py:379
  51.4 14.4 %all_to_all.20.sums_ref = f32[16,8,512]{2,1,0:T(8,128)S(1)} all-to-all(f32[16,8,512]{2,1,0:T(8,128)S(1)} %get-tuple-element.41), channel_id=1, replica_groups=mesh['g'=16,'j'=8,'ch'=2] {'j','ch'}, dimensions={0} | all-to-all | bytes 524288 | tf_op jit(solution)/shard_map/all_to_all | solution.py:447
  66.6 1.3 %collective-permute-start.7 = (bf16[256,512]{1,0:T(8,128)(2,1)S(1)}, bf16[256,512]{1,0:T(8,128)(2,1)S(1)}, u32[]{:S(2)}, u32[]{:S(2)}) collective-permute-start(bf16[256,512]{1,0:T(8,128)(2,1)S(1)} %get-tuple-element.55), channel_id=1, source_target_pairs={{16,0},{32,16},{48,32},{64,48},{80,64},{96,80},{112,96},{128,112},... | collective-permute-start | bytes 786440 | tf_op jit(solution)/shard_map/ppermute | solution.py:452
  67.9 3.5 %shard_map.160 = (f32[512,1024]{1,0:T(8,128)}, bf16[4,256,128]{2,1,0:T(8,128)(2,1)}) custom-call(bf16[256,1024]{1,0:T(8,128)(2,1)S(1)} %get-tuple-element.45.grad_ref, f32[512,1024]{1,0:T(8,128)S(1)} %get-tuple-element.46.own_ref, f32[512,512]{1,0:T(8,128)S(1)} %get-tuple-element.47.before_ref, bf16[512,256]{1,0:T(8,128)(2,1)S(1)} %get-tuple-element.48.forward_high, ...), custom_call_target="tpu_custom_call" | custom-call | flops 939524096 | bytes 4718592 | tf_op jit(solution)/shard_map/pallas_call | solution.py:379
  71.4 13.3 %all-to-all-start.3 = ((bf16[128,8,128]{2,1,0:T(8,128)(2,1)}), bf16[128,8,128]{2,1,0:T(8,128)(2,1)S(1)}, u32[]{:S(2)}, u32[]{:S(2)}) async-start(bf16[128,8,128]{2,1,0:T(8,128)(2,1)} %bitcast.6), calls=%async_computation.3 | async-start | bytes 524288 | tf_op jit(solution)/shard_map/all_to_all | solution.py:470
  84.7 5.3 %shard_map.161 = (bf16[512,128]{1,0:T(8,128)(2,1)S(1)}, bf16[512,128]{1,0:T(8,128)(2,1)S(1)}, bf16[512,128]{1,0:T(8,128)(2,1)S(1)}, bf16[512,128]{1,0:T(8,128)(2...) custom-call(s32[2]{0:T(128)S(1)} %pad_add_fusion.place_ref, ...), custom_call_target="tpu_custom_call" | custom-call | flops 1073741824 | bytes 4980744 | tf_op jit(solution)/shard_map/pallas_call | solution.py:379
  90.0 1.6 %collective-permute-start.8 = (bf16[512,128]{1,0:T(8,128)(2,1)S(1)}, bf16[512,128]{1,0:T(8,128)(2,1)S(1)}, u32[]{:S(2)}, u32[]{:S(2)}) collective-permute-start(bf16[512,128]{1,0:T(8,128)(2,1)S(1)} %get-tuple-element.57), channel_id=1, source_target_pairs={{0,2},{2,4},{4,6},{6,8},{8,10},{10,12},{12,14},{14,0},{1,3},{3,5},... | collective-permute-start | bytes 393224 | tf_op jit(solution)/shard_map/ppermute | solution.py:393
  92.8 1.6 %collective-permute-start.10 = (bf16[512,128]{1,0:T(8,128)(2,1)S(1)}, bf16[512,128]{1,0:T(8,128)(2,1)S(1)}, u32[]{:S(2)}, u32[]{:S(2)}) collective-permute-start(bf16[512,128]{1,0:T(8,128)(2,1)S(1)} %get-tuple-element.59), channel_id=1, source_target_pairs={{0,6},{2,8},{4,10},{6,12},{8,14},{10,0},{12,2},{14,4},{1,7},{3,9},... | collective-permute-start | bytes 393224 | tf_op jit(solution)/shard_map/ppermute | solution.py:393
  95.0 2.4 %collective-permute-start.12 = (bf16[512,128]{1,0:T(8,128)(2,1)S(1)}, bf16[512,128]{1,0:T(8,128)(2,1)S(1)}, u32[]{:S(2)}, u32[]{:S(2)}) collective-permute-start(bf16[512,128]{1,0:T(8,128)(2,1)S(1)} %get-tuple-element.61), channel_id=1, source_target_pairs={{0,10},{2,12},{4,14},{6,0},{8,2},{10,4},{12,6},{14,8},{1,11},{3,13... | collective-permute-start | bytes 393224 | tf_op jit(solution)/shard_map/ppermute | solution.py:393
  97.6 2.9 %collective-permute-done.9.refs_2_ = bf16[512,128]{1,0:T(8,128)(2,1)S(1)} collective-permute-done((bf16[512,128]{1,0:T(8,128)(2,1)S(1)}, bf16[512,128]{1,0:T(8,128)(2,1)S(1)}, u32[]{:S(2)}, u32[]{:S(2)}) %collective-permute-start.9) | collective-permute-done | bytes 131104 | tf_op jit(solution)/shard_map/ppermute | solution.py:393
  101.5 4.7 %collective-permute-done.11.refs_4_ = bf16[512,128]{1,0:T(8,128)(2,1)S(1)} collective-permute-done((bf16[512,128]{1,0:T(8,128)(2,1)S(1)}, bf16[512,128]{1,0:T(8,128)(2,1)S(1)}, u32[]{:S(2)}, u32[]{:S(2)}) %collective-permute-start.11) | collective-permute-done | bytes 131104 | tf_op jit(solution)/shard_map/ppermute | solution.py:393
  107.1 3.7 %shard_map.162 = (bf16[256,1024]{1,0:T(8,128)(2,1)}, bf16[256,1024]{1,0:T(8,128)(2,1)}, bf16[256,1024]{1,0:T(8,128)(2,1)}, bf16[256,1024]{1,0:T(8,128)(2,1)}) custom-call(s32[2]{0:T(128)S(1)} %pad_add_fusion.place_ref, f32[16,8,512]{2,1,0:T(8,128)} %copy-done, bf16[256,1024]{1,0:T(8,128)(2,1)S(1)} %copy-done.3, bf16[256,1024]{1,0:T(8,128)(2,1)S(1)} %copy-done.1, ...), custom_call_target="tpu_custom_call" | custom-call | flops 1000 | bytes 3476488 | tf_op jit(solution)/shard_map/pallas_call | solution.py:379
  (42 shorter events, 10.5 us)
Async XLA Ops:
  3.6 35.6 %copy-start.6 = (f32[11,1024]{1,0:T(8,128)S(1)}, f32[11,1024]{1,0:T(8,128)}, u32[]{:S(2)}) copy-start(f32[11,1024]{1,0:T(8,128)} %param.19) | copy-start | bytes 135172
  3.6 28.0 %all-to-all-start = ((bf16[8,784,128]{2,1,0:T(8,128)(2,1)}), bf16[8,784,128]{2,1,0:T(8,128)(2,1)S(1)}, u32[]{:S(2)}, u32[]{:S(2)}) async-start(bf16[8,784,128]{2,1,0:T(8,128)(2,1)} %shard_map.155), calls=%async_computation | async-start | bytes 3211264 | tf_op jit(solution)/shard_map/all_to_all | solution.py:419
  10.5 7.5 %collective-permute-start.2 = (bf16[1,8,1024]{2,1,0:T(8,128)(2,1)S(1)}, bf16[1,8,1024]{2,1,0:T(8,128)(2,1)S(1)}, u32[]{:S(2)}, u32[]{:S(2)}) collective-permute-start(bf16[1,8,1024]{2,1,0:T(8,128)(2,1)S(1)} %bitcast.7), channel_id=1, source_target_pairs={{0,192},{16,208},{32,224},{48,240},{64,128},{80,144},{96,160},{112... | collective-permute-start | bytes 49160 | tf_op jit(solution)/shard_map/ppermute | solution.py:398
  15.8 6.6 %collective-permute-start.1 = (bf16[1,8,1024]{2,1,0:T(8,128)(2,1)S(1)}, bf16[1,8,1024]{2,1,0:T(8,128)(2,1)S(1)}, u32[]{:S(2)}, u32[]{:S(2)}) collective-permute-start(bf16[1,8,1024]{2,1,0:T(8,128)(2,1)S(1)} %bitcast.8), channel_id=1, source_target_pairs={{0,128},{16,144},{32,160},{48,176},{64,192},{80,208},{96,224},{112... | collective-permute-start | bytes 49160 | tf_op jit(solution)/shard_map/ppermute | solution.py:398
  16.7 5.6 %collective-permute-start = (bf16[1,8,1024]{2,1,0:T(8,128)(2,1)S(1)}, bf16[1,8,1024]{2,1,0:T(8,128)(2,1)S(1)}, u32[]{:S(2)}, u32[]{:S(2)}) collective-permute-start(bf16[1,8,1024]{2,1,0:T(8,128)(2,1)S(1)} %bitcast.9), channel_id=1, source_target_pairs={{0,64},{16,80},{32,96},{48,112},{64,0},{80,16},{96,32},{112,48},{1... | collective-permute-start | bytes 49160 | tf_op jit(solution)/shard_map/ppermute | solution.py:398
  22.4 4.3 %collective-permute-start.5 = (bf16[4,8,1024]{2,1,0:T(8,128)(2,1)S(1)}, bf16[4,8,1024]{2,1,0:T(8,128)(2,1)S(1)}, u32[]{:S(2)}, u32[]{:S(2)}) collective-permute-start(bf16[4,8,1024]{2,1,0:T(8,128)(2,1)S(1)} %pad_maximum_fusion.refs_0_), channel_id=1, source_target_pairs={{0,48},{16,32},{32,16},{48,0},{64,112},{80,96},{96,80},{112,64},{1... | collective-permute-start | bytes 196616 | tf_op jit(solution)/shard_map/ppermute | solution.py:398
  24.0 3.2 %collective-permute-start.4 = (bf16[4,8,1024]{2,1,0:T(8,128)(2,1)S(1)}, bf16[4,8,1024]{2,1,0:T(8,128)(2,1)S(1)}, u32[]{:S(2)}, u32[]{:S(2)}) collective-permute-start(bf16[4,8,1024]{2,1,0:T(8,128)(2,1)S(1)} %pad_maximum_fusion.refs_0_), channel_id=1, source_target_pairs={{0,32},{16,48},{32,0},{48,16},{64,96},{80,112},{96,64},{112,80},{1... | collective-permute-start | bytes 196616 | tf_op jit(solution)/shard_map/ppermute | solution.py:398
  24.8 4.1 %collective-permute-start.3 = (bf16[4,8,1024]{2,1,0:T(8,128)(2,1)S(1)}, bf16[4,8,1024]{2,1,0:T(8,128)(2,1)S(1)}, u32[]{:S(2)}, u32[]{:S(2)}) collective-permute-start(bf16[4,8,1024]{2,1,0:T(8,128)(2,1)S(1)} %pad_maximum_fusion.refs_0_), channel_id=1, source_target_pairs={{0,16},{16,0},{32,48},{48,32},{64,80},{80,64},{96,112},{112,96},{1... | collective-permute-start | bytes 196616 | tf_op jit(solution)/shard_map/ppermute | solution.py:398
  31.6 8.3 %copy-start.5 = (bf16[8,784,128]{2,1,0:T(8,128)(2,1)}, bf16[8,784,128]{2,1,0:T(8,128)(2,1)S(1)}, u32[]{:S(2)}) copy-start(bf16[8,784,128]{2,1,0:T(8,128)(2,1)S(1)} %all-to-all-done.got_ref.got_hbm) | copy-start | bytes 4816900
  31.6 14.1 %collective-permute-start.6 = (bf16[4,256,128]{2,1,0:T(8,128)(2,1)S(1)}, bf16[4,256,128]{2,1,0:T(8,128)(2,1)S(1)}, u32[]{:S(2)}, u32[]{:S(2)}) collective-permute-start(bf16[4,256,128]{2,1,0:T(8,128)(2,1)S(1)} %slice.3), channel_id=1, source_target_pairs={{0,16},{16,32},{32,48},{48,64},{64,80},{80,96},{96,112},{112,128},... | collective-permute-start | bytes 786440 | tf_op jit(solution)/shard_map/ppermute | solution.py:425
  33.9 11.7 %all-to-all-start.1 = ((bf16[8,128,128]{2,1,0:T(8,128)(2,1)}), bf16[8,128,128]{2,1,0:T(8,128)(2,1)S(1)}, u32[]{:S(2)}, u32[]{:S(2)}) async-start(bf16[8,128,128]{2,1,0:T(8,128)(2,1)} %shard_map.156), calls=%async_computation.1 | async-start | bytes 524288 | tf_op jit(solution)/shard_map/all_to_all | solution.py:426
  66.6 18.1 %collective-permute-start.7 = (bf16[256,512]{1,0:T(8,128)(2,1)S(1)}, bf16[256,512]{1,0:T(8,128)(2,1)S(1)}, u32[]{:S(2)}, u32[]{:S(2)}) collective-permute-start(bf16[256,512]{1,0:T(8,128)(2,1)S(1)} %get-tuple-element.55), channel_id=1, source_target_pairs={{16,0},{32,16},{48,32},{64,48},{80,64},{96,80},{112,96},{128,112},... | collective-permute-start | bytes 786440 | tf_op jit(solution)/shard_map/ppermute | solution.py:452
  71.4 39.4 %all-to-all-start.3 = ((bf16[128,8,128]{2,1,0:T(8,128)(2,1)}), bf16[128,8,128]{2,1,0:T(8,128)(2,1)S(1)}, u32[]{:S(2)}, u32[]{:S(2)}) async-start(bf16[128,8,128]{2,1,0:T(8,128)(2,1)} %bitcast.6), calls=%async_computation.3 | async-start | bytes 524288 | tf_op jit(solution)/shard_map/all_to_all | solution.py:470
  84.7 22.4 %copy-start.1 = (bf16[256,1024]{1,0:T(8,128)(2,1)S(1)}, bf16[256,1024]{1,0:T(8,128)(2,1)}, u32[]{:S(2)}) copy-start(bf16[256,1024]{1,0:T(8,128)(2,1)} %key_ref.3) | copy-start | bytes 1572868
  84.7 22.3 %copy-start.2 = (bf16[256,1024]{1,0:T(8,128)(2,1)S(1)}, bf16[256,1024]{1,0:T(8,128)(2,1)}, u32[]{:S(2)}) copy-start(bf16[256,1024]{1,0:T(8,128)(2,1)} %value_ref.3) | copy-start | bytes 1572868
  84.7 22.3 %copy-start.3 = (bf16[256,1024]{1,0:T(8,128)(2,1)S(1)}, bf16[256,1024]{1,0:T(8,128)(2,1)}, u32[]{:S(2)}) copy-start(bf16[256,1024]{1,0:T(8,128)(2,1)} %query_ref.3) | copy-start | bytes 1572868
  84.7 22.3 %copy-start.4 = (bf16[256,1024]{1,0:T(8,128)(2,1)S(1)}, bf16[256,1024]{1,0:T(8,128)(2,1)}, u32[]{:S(2)}) copy-start(bf16[256,1024]{1,0:T(8,128)(2,1)} %cotangent_ref.3) | copy-start | bytes 1572868
  90.0 7.5 %collective-permute-start.8 = (bf16[512,128]{1,0:T(8,128)(2,1)S(1)}, bf16[512,128]{1,0:T(8,128)(2,1)S(1)}, u32[]{:S(2)}, u32[]{:S(2)}) collective-permute-start(bf16[512,128]{1,0:T(8,128)(2,1)S(1)} %get-tuple-element.57), channel_id=1, source_target_pairs={{0,2},{2,4},{4,6},{6,8},{8,10},{10,12},{12,14},{14,0},{1,3},{3,5},... | collective-permute-start | bytes 393224 | tf_op jit(solution)/shard_map/ppermute | solution.py:393
  91.6 8.8 %collective-permute-start.9 = (bf16[512,128]{1,0:T(8,128)(2,1)S(1)}, bf16[512,128]{1,0:T(8,128)(2,1)S(1)}, u32[]{:S(2)}, u32[]{:S(2)}) collective-permute-start(bf16[512,128]{1,0:T(8,128)(2,1)S(1)} %get-tuple-element.58), channel_id=1, source_target_pairs={{0,4},{2,6},{4,8},{6,10},{8,12},{10,14},{12,0},{14,2},{1,5},{3,7},... | collective-permute-start | bytes 393224 | tf_op jit(solution)/shard_map/ppermute | solution.py:393
  92.8 8.6 %collective-permute-start.10 = (bf16[512,128]{1,0:T(8,128)(2,1)S(1)}, bf16[512,128]{1,0:T(8,128)(2,1)S(1)}, u32[]{:S(2)}, u32[]{:S(2)}) collective-permute-start(bf16[512,128]{1,0:T(8,128)(2,1)S(1)} %get-tuple-element.59), channel_id=1, source_target_pairs={{0,6},{2,8},{4,10},{6,12},{8,14},{10,0},{12,2},{14,4},{1,7},{3,9},... | collective-permute-start | bytes 393224 | tf_op jit(solution)/shard_map/ppermute | solution.py:393
  94.5 11.7 %collective-permute-start.11 = (bf16[512,128]{1,0:T(8,128)(2,1)S(1)}, bf16[512,128]{1,0:T(8,128)(2,1)S(1)}, u32[]{:S(2)}, u32[]{:S(2)}) collective-permute-start(bf16[512,128]{1,0:T(8,128)(2,1)S(1)} %get-tuple-element.60), channel_id=1, source_target_pairs={{0,8},{2,10},{4,12},{6,14},{8,0},{10,2},{12,4},{14,6},{1,9},{3,11}... | collective-permute-start | bytes 393224 | tf_op jit(solution)/shard_map/ppermute | solution.py:393
  95.0 11.7 %collective-permute-start.12 = (bf16[512,128]{1,0:T(8,128)(2,1)S(1)}, bf16[512,128]{1,0:T(8,128)(2,1)S(1)}, u32[]{:S(2)}, u32[]{:S(2)}) collective-permute-start(bf16[512,128]{1,0:T(8,128)(2,1)S(1)} %get-tuple-element.61), channel_id=1, source_target_pairs={{0,10},{2,12},{4,14},{6,0},{8,2},{10,4},{12,6},{14,8},{1,11},{3,13... | collective-permute-start | bytes 393224 | tf_op jit(solution)/shard_map/ppermute | solution.py:393
  97.5 9.3 %collective-permute-start.13 = (bf16[512,128]{1,0:T(8,128)(2,1)S(1)}, bf16[512,128]{1,0:T(8,128)(2,1)S(1)}, u32[]{:S(2)}, u32[]{:S(2)}) collective-permute-start(bf16[512,128]{1,0:T(8,128)(2,1)S(1)} %get-tuple-element.62), channel_id=1, source_target_pairs={{0,12},{2,14},{4,0},{6,2},{8,4},{10,6},{12,8},{14,10},{1,13},{3,15... | collective-permute-start | bytes 393224 | tf_op jit(solution)/shard_map/ppermute | solution.py:393
  100.5 6.6 %collective-permute-start.14 = (bf16[512,128]{1,0:T(8,128)(2,1)S(1)}, bf16[512,128]{1,0:T(8,128)(2,1)S(1)}, u32[]{:S(2)}, u32[]{:S(2)}) collective-permute-start(bf16[512,128]{1,0:T(8,128)(2,1)S(1)} %get-tuple-element.63), channel_id=1, source_target_pairs={{0,14},{2,0},{4,2},{6,4},{8,6},{10,8},{12,10},{14,12},{1,15},{3,1}... | collective-permute-start | bytes 393224 | tf_op jit(solution)/shard_map/ppermute | solution.py:393
  (2 other events, 12.4 us)

commit v5 on v4

--- a/solution.py
+++ b/solution.py
@@ -73,17 +73,18 @@
 QUERY, UPSTREAM, CLASS, ROWS = LEN, 2 * LEN, 3 * LEN, 3 * LEN + 16
 
 
-def pack(key_ref, value_ref, query_ref, cotangent_ref, stock_ref, class_ref, out_hbm, out_ref, sems):
-    event_class = event_classes(stock_ref, class_ref).astype(BF16)
+def pack(key_ref, value_ref, query_ref, cotangent_ref, stock_ref, class_ref, out_hbm, out_ref, event_ref, sems):
     copies = []
     for place in range(GROUP):
         product = key_ref[:, col(place)].astype(F32) * value_ref[:, col(place)].astype(F32)
         out_ref[place, :LEN, :] = product.astype(BF16)
         out_ref[place, QUERY:UPSTREAM, :] = query_ref[:, col(place)]
-        out_ref[place, UPSTREAM:CLASS, :] = cotangent_ref[:, col(place)]
-        out_ref[place, CLASS : CLASS + 8, :] = event_class[:, :LANES]
-        out_ref[place, CLASS + 8 :, :] = event_class[:, LANES:]
-        copies.append(copy_out(out_ref.at[place], out_hbm.at[place], sems.at[place]))
+        out_ref[place, UPSTREAM:, :] = cotangent_ref[:, col(place)]
+        copies.append(copy_out(out_ref.at[place], out_hbm.at[place, :CLASS, :], sems.at[place]))
+    event_class = event_classes(stock_ref, class_ref).astype(BF16)
+    event_ref[...] = jnp.concatenate([event_class[:, :LANES], event_class[:, LANES:]], axis=0)
+    for place in range(GROUP):
+        copies.append(copy_out(event_ref, out_hbm.at[place, CLASS:, :], sems.at[GROUP + place]))
     for copy in copies:
         copy.wait()
 
@@ -129,7 +130,10 @@
     return real, imag
 
 
-def prepare(place_ref, table_ref, got_ref, forward_high, forward_low, own_out, gate_out, own_ref, gate_ref, sems):
+def prepare(
+    place_ref, table_ref, got_ref, stock_ref, class_ref, forward_high, forward_low, own_out, gate_out, factor_out, own_ref,
+    gate_ref, factor_ref, sems,
+):
     rows = jnp.concatenate([got_ref[b, :LEN, :] for b in range(GROUP)], axis=1)
     own_ref[...] = spectrum((forward_high, forward_low), rows)
     copies = [copy_out(own_ref, own_out, sems.at[0])]
@@ -139,6 +143,8 @@
         event_class = jnp.concatenate([classes[:1], classes[8:9]], axis=1)
         gate_ref[:, col(block)] = got_ref[block, QUERY:UPSTREAM, :].astype(F32) * modulation(event_class, table)
     copies.append(copy_out(gate_ref, gate_out, sems.at[1]))
+    factor_ref[...] = modulation(event_classes(stock_ref, class_ref)[:1], table_ref[...])
+    copies.append(copy_out(factor_ref, factor_out, sems.at[2]))
     for copy in copies:
         copy.wait()
 
@@ -147,9 +153,10 @@
     own_ref, gate_ref, upstream_ref, before_spec_ref, conv_ref = refs[4:9]
     forward, inverse = refs[9:11], refs[11:13]
     lag_spec_hbm, rounded_hbm, sums_ref, lag_spec_ref, rounded_ref, product_ref, sorted_ref, sems = refs[13:]
-    tables = [copy_out(refs[i], refs[9 + i], sems.at[5 + i]) for i in range(4)]
-    loads = [
-        copy_out(own_hbm, own_ref, sems.at[0]),
+    tables = [copy_out(refs[i], refs[9 + i], sems.at[5 + i]) for i in range(2)]
+    loads = [copy_out(own_hbm, own_ref, sems.at[0])]
+    tables += [copy_out(refs[i], refs[9 + i], sems.at[5 + i]) for i in range(2, 4)]
+    loads += [
         copy_out(gate_hbm, gate_ref, sems.at[1]),
         copy_out(got_hbm.at[:, UPSTREAM:CLASS, :], upstream_ref, sems.at[2]),
     ]
@@ -328,10 +335,10 @@
 
 
 def finish(
-    channels, place_ref, sums_ref, query_ref, key_ref, value_ref, cotangent_ref, stock_ref, class_ref, table_ref, *refs
+    channels, place_ref, sums_ref, query_ref, key_ref, value_ref, cotangent_ref, factor_ref, *refs
 ):
     pieces = refs[:GROUP]
-    normed_ref, grad_query_ref, grad_key_ref, grad_value_ref, factor_ref, lines_ref = refs[GROUP:]
+    normed_ref, grad_query_ref, grad_key_ref, grad_value_ref, lines_ref = refs[GROUP:]
     place = place_ref[0]
     half = GROUP // 2
     lines_ref[...] = row_lines(channels, sums_ref)
@@ -339,7 +346,6 @@
     number = lax.broadcasted_iota(jnp.int32, (LEN, GROUP), 1)
     inv = jnp.sum(jnp.where(number == place >> 1, lines, 0.0), axis=1, keepdims=True)
     mean = jnp.sum(jnp.where(number == half + (place >> 1), lines, 0.0), axis=1, keepdims=True)
-    factor_ref[...] = modulation(event_classes(stock_ref, class_ref)[:1], table_ref[...])
     for step in range(GROUP):
         there = lane((place - step) & (GROUP - 1))
         piece = pieces[step]
@@ -414,7 +420,8 @@
 
     (sent,) = call(
         pack, [off_chip((GROUP, ROWS, LANES), BF16)], *map(far, (key_proj, value_proj, query_proj, cotangent)),
-        stock_id, stock_class, manual=(0,), copies=(GROUP,), scratch=[((GROUP, ROWS, LANES), BF16)],
+        stock_id, stock_class, manual=(0,), copies=(2 * GROUP,),
+        scratch=[((GROUP, CLASS, LANES), BF16), ((16, LANES), BF16)],
     )
     got = lax.all_to_all(sent, "j", 0, 0)
     lags = filters[None]
@@ -424,10 +431,10 @@
     got, lags = lax.optimization_barrier((got, lags))
     before = lax.ppermute(got[GROUP - REACH :, :LEN, :], "g", [(i, i + 1) for i in range(groups - 1)])
     got, lags = far(got), near(lax.all_to_all(lags, "j", 0, 0))
-    own, gate = call(
-        prepare, [off_chip((2 * LEN, wide), F32), off_chip((LEN, wide), F32)], place, table, got, *far_tables[:2],
-        scalars=1, copies=(2,), manual=(0, 1), scratch=[((2 * LEN, wide), F32), ((LEN, wide), F32)],
-        cost=2 * 4 * LEN * LEN * wide,
+    own, gate, factor = call(
+        prepare, [off_chip((2 * LEN, wide), F32), off_chip((LEN, wide), F32), off_chip((LEN, wide), F32)], place, table,
+        got, stock_id, stock_class, *far_tables[:2], scalars=1, copies=(3,), manual=(0, 1, 2),
+        scratch=[((2 * LEN, wide), F32), ((LEN, wide), F32), ((LEN, wide), F32)], cost=2 * 4 * LEN * LEN * wide,
     )
     results = call(
         functools.partial(convolve, near_groups, far_groups),
@@ -472,8 +479,8 @@
     outs = call(
         functools.partial(finish, wide * parts),
         [off_chip((LEN, wide), BF16)] * 4,
-        place, far(sums), *map(near, (query_proj, key_proj, value_proj, cotangent)), stock_id, stock_class, table,
-        *map(near, back), scalars=1, scratch=[((LEN, wide), F32), ((2 * LEN, GROUP), F32)],
+        place, far(sums), *map(near, (query_proj, key_proj, value_proj, cotangent, factor)), *map(near, back),
+        scalars=1, scratch=[((2 * LEN, GROUP), F32)],
     )
     return *outs, grad_filter
 

time: 112 us -> 111 us (level)
  no operation moved by 1% of the time
where the time goes in v5:
time: 111 us
  starting transfers between devices  46.7 us (42%)
  Pallas kernels  27.2 us (25%)
  waiting for transfers between devices  21 us (19%)
  blocking collectives  14.4 us (13%)
    pallas_call x9, Pallas kernels, call(): pl.pallas_call(body, out_shape=list(outs), in_specs=specs, out_specs=[pl....  27.2 us
    all_to_all x1, blocking collectives, shards(): sums = lax.all_to_all(sums, ('j', 'ch'), 0, 0)  14.4 us
    all_to_all x1, starting transfers between devices, shards(): lax.all_to_all(terms.reshape(groups * GROUP, lag_rows, LANES), ('g', 'j')...  13.3 us
    ppermute x6, starting transfers between devices, trade(): return lax.ppermute(value, 'g', [(i, i ^ mask) for i in range(groups)])  10.2 us
    ppermute x7, waiting for transfers between devices, swap(): lax.ppermute(pieces[step], 'j', [(i, (i + step) % GROUP) for i in range(G...  9.48 us
    ppermute x6, waiting for transfers between devices, trade(): return lax.ppermute(value, 'g', [(i, i ^ mask) for i in range(groups)])  8.26 us
    ppermute x7, starting transfers between devices, swap(): lax.ppermute(pieces[step], 'j', [(i, (i + step) % GROUP) for i in range(G...  7.55 us
    all_to_all x1, starting transfers between devices, shards(): got = lax.all_to_all(sent, 'j', 0, 0)  6.87 us
  transfers between devices with their start and end apart: 18, of which 11 were waited for; matrix products, arithmetic and copies ran while one was open for 1% of the time, Pallas kernels for 15%

profile of v5, /device:TPU:1, one launch (start us, length us, event | category | flops | bytes accessed | tf_op | source)
XLA Modules:
  0.0 111.0 jit_solution(3948052435938282722)
XLA Ops:
  0.6 3.0 %shard_map.155 = bf16[8,784,128]{2,1,0:T(8,128)(2,1)} custom-call(bf16[256,1024]{1,0:T(8,128)(2,1)} %key_ref.3, bf16[256,1024]{1,0:T(8,128)(2,1)} %value_ref.3, bf16[256,1024]{1,0:T(8,128)(2,1)} %query_ref.3, bf16[256,1024]{1,0:T(8,128)(2,1)} %cotangent_ref.3, s32[1,256]{1,0:T(1,128)} %bitcast.13, s32[1,512]{1,0:T(1,128)} %bitcast.11), custom_call_target="tpu_custom_call" | custom-call | flops 1000 | bytes 2100224 | tf_op jit(solution)/shard_map/pallas_call | solution.py:385
  3.6 6.9 %all-to-all-start = ((bf16[8,784,128]{2,1,0:T(8,128)(2,1)}), bf16[8,784,128]{2,1,0:T(8,128)(2,1)S(1)}, u32[]{:S(2)}, u32[]{:S(2)}) async-start(bf16[8,784,128]{2,1,0:T(8,128)(2,1)} %shard_map.155), calls=%async_computation | async-start | bytes 3211264 | tf_op jit(solution)/shard_map/all_to_all | solution.py:426
  10.5 5.3 %collective-permute-start.2 = (bf16[1,8,1024]{2,1,0:T(8,128)(2,1)S(1)}, bf16[1,8,1024]{2,1,0:T(8,128)(2,1)S(1)}, u32[]{:S(2)}, u32[]{:S(2)}) collective-permute-start(bf16[1,8,1024]{2,1,0:T(8,128)(2,1)S(1)} %bitcast.7), channel_id=1, source_target_pairs={{0,192},{16,208},{32,224},{48,240},{64,128},{80,144},{96,160},{112... | collective-permute-start | bytes 49160 | tf_op jit(solution)/shard_map/ppermute | solution.py:404
  18.0 4.4 %collective-permute-done.1 = bf16[1,8,1024]{2,1,0:T(8,128)(2,1)S(1)} collective-permute-done((bf16[1,8,1024]{2,1,0:T(8,128)(2,1)S(1)}, bf16[1,8,1024]{2,1,0:T(8,128)(2,1)S(1)}, u32[]{:S(2)}, u32[]{:S(2)}) %collective-permute-start.1) | collective-permute-done | bytes 16416 | tf_op jit(solution)/shard_map/ppermute | solution.py:404
  22.4 1.7 %collective-permute-start.5 = (bf16[4,8,1024]{2,1,0:T(8,128)(2,1)S(1)}, bf16[4,8,1024]{2,1,0:T(8,128)(2,1)S(1)}, u32[]{:S(2)}, u32[]{:S(2)}) collective-permute-start(bf16[4,8,1024]{2,1,0:T(8,128)(2,1)S(1)} %pad_maximum_fusion.refs_0_), channel_id=1, source_target_pairs={{0,48},{16,32},{32,16},{48,0},{64,112},{80,96},{96,80},{112,64},{1... | collective-permute-start | bytes 196616 | tf_op jit(solution)/shard_map/ppermute | solution.py:404
  25.1 1.6 %collective-permute-done.5.refs_3_ = bf16[4,8,1024]{2,1,0:T(8,128)(2,1)S(1)} collective-permute-done((bf16[4,8,1024]{2,1,0:T(8,128)(2,1)S(1)}, bf16[4,8,1024]{2,1,0:T(8,128)(2,1)S(1)}, u32[]{:S(2)}, u32[]{:S(2)}) %collective-permute-start.5) | collective-permute-done | bytes 65568 | tf_op jit(solution)/shard_map/ppermute | solution.py:404
  27.2 1.8 %collective-permute-done.3.refs_1_ = bf16[4,8,1024]{2,1,0:T(8,128)(2,1)S(1)} collective-permute-done((bf16[4,8,1024]{2,1,0:T(8,128)(2,1)S(1)}, bf16[4,8,1024]{2,1,0:T(8,128)(2,1)S(1)}, u32[]{:S(2)}, u32[]{:S(2)}) %collective-permute-start.3) | collective-permute-done | bytes 65568 | tf_op jit(solution)/shard_map/ppermute | solution.py:404
  29.7 1.9 %all-to-all-done.got_ref.got_hbm = bf16[8,784,128]{2,1,0:T(8,128)(2,1)S(1)} async-done(((bf16[8,784,128]{2,1,0:T(8,128)(2,1)}), bf16[8,784,128]{2,1,0:T(8,128)(2,1)S(1)}, u32[]{:S(2)}, u32[]{:S(2)}) %all-to-all-start) | async-done | bytes 1605664 | tf_op jit(solution)/shard_map/all_to_all | solution.py:426
  31.6 2.4 %collective-permute-start.6 = (bf16[4,256,128]{2,1,0:T(8,128)(2,1)S(1)}, bf16[4,256,128]{2,1,0:T(8,128)(2,1)S(1)}, u32[]{:S(2)}, u32[]{:S(2)}) collective-permute-start(bf16[4,256,128]{2,1,0:T(8,128)(2,1)S(1)} %slice.3), channel_id=1, source_target_pairs={{0,16},{16,32},{32,48},{48,64},{64,80},{80,96},{96,112},{112,128},... | collective-permute-start | bytes 786440 | tf_op jit(solution)/shard_map/ppermute | solution.py:432
  34.0 5.2 %all-to-all-start.1 = ((bf16[8,128,128]{2,1,0:T(8,128)(2,1)}), bf16[8,128,128]{2,1,0:T(8,128)(2,1)S(1)}, u32[]{:S(2)}, u32[]{:S(2)}) async-start(bf16[8,128,128]{2,1,0:T(8,128)(2,1)} %shard_map.156), calls=%async_computation.1 | async-start | bytes 524288 | tf_op jit(solution)/shard_map/all_to_all | solution.py:433
  39.9 4.3 %shard_map.157 = (f32[512,1024]{1,0:T(8,128)}, f32[256,1024]{1,0:T(8,128)}, f32[256,1024]{1,0:T(8,128)}) custom-call(s32[2]{0:T(128)S(1)} %pad_add_fusion.place_ref, f32[16,1024]{1,0:T(8,128)} %pad.4.table_ref, bf16[8,784,128]{2,1,0:T(8,128)(2,1)} %copy-done.6, s32[1,256]{1,0:T(1,128)} %bitcast.14, s32[1,512]{1,0:T(1,128)} %bitcast.12, ...), custom_call_target="tpu_custom_call" | custom-call | flops 536870912 | bytes 2198536 | tf_op jit(solution)/shard_map/pallas_call | solution.py:385
  44.2 1.4 %all-to-all-done.1.lags_ref = bf16[8,128,128]{2,1,0:T(8,128)(2,1)S(1)} async-done(((bf16[8,128,128]{2,1,0:T(8,128)(2,1)}), bf16[8,128,128]{2,1,0:T(8,128)(2,1)S(1)}, u32[]{:S(2)}, u32[]{:S(2)}) %all-to-all-start.1) | async-done | bytes 262176 | tf_op jit(solution)/shard_map/all_to_all | solution.py:433
  45.7 5.6 %shard_map.158 = (f32[512,1024]{1,0:T(8,128)S(1)}, f32[256,1024]{1,0:T(8,128)S(1)}, bf16[8,256,128]{2,1,0:T(8,128)(2,1)S(1)}, f32[512,512]{1,0:T(8,128)S(1)}, f3...) custom-call(s32[2]{0:T(128)S(1)} %pad_add_fusion.place_ref, ...), custom_call_target="tpu_custom_call" | custom-call | flops 1342177280 | bytes 6324232 | tf_op jit(solution)/shard_map/pallas_call | solution.py:385
  51.3 14.4 %all_to_all.20.sums_ref = f32[16,8,512]{2,1,0:T(8,128)S(1)} all-to-all(f32[16,8,512]{2,1,0:T(8,128)S(1)} %get-tuple-element.42), channel_id=1, replica_groups=mesh['g'=16,'j'=8,'ch'=2] {'j','ch'}, dimensions={0} | all-to-all | bytes 524288 | tf_op jit(solution)/shard_map/all_to_all | solution.py:454
  66.5 1.3 %collective-permute-start.7 = (bf16[256,512]{1,0:T(8,128)(2,1)S(1)}, bf16[256,512]{1,0:T(8,128)(2,1)S(1)}, u32[]{:S(2)}, u32[]{:S(2)}) collective-permute-start(bf16[256,512]{1,0:T(8,128)(2,1)S(1)} %get-tuple-element.57), channel_id=1, source_target_pairs={{16,0},{32,16},{48,32},{64,48},{80,64},{96,80},{112,96},{128,112},... | collective-permute-start | bytes 786440 | tf_op jit(solution)/shard_map/ppermute | solution.py:459
  67.8 3.5 %shard_map.160 = (f32[512,1024]{1,0:T(8,128)}, bf16[4,256,128]{2,1,0:T(8,128)(2,1)}) custom-call(bf16[256,1024]{1,0:T(8,128)(2,1)S(1)} %get-tuple-element.47.grad_ref, f32[512,1024]{1,0:T(8,128)S(1)} %get-tuple-element.48.own_ref, f32[512,512]{1,0:T(8,128)S(1)} %get-tuple-element.49.before_ref, bf16[512,256]{1,0:T(8,128)(2,1)S(1)} %get-tuple-element.50.forward_high, ...), custom_call_target="tpu_custom_call" | custom-call | flops 939524096 | bytes 4718592 | tf_op jit(solution)/shard_map/pallas_call | solution.py:385
  71.3 13.3 %all-to-all-start.3 = ((bf16[128,8,128]{2,1,0:T(8,128)(2,1)}), bf16[128,8,128]{2,1,0:T(8,128)(2,1)S(1)}, u32[]{:S(2)}, u32[]{:S(2)}) async-start(bf16[128,8,128]{2,1,0:T(8,128)(2,1)} %bitcast.6), calls=%async_computation.3 | async-start | bytes 524288 | tf_op jit(solution)/shard_map/all_to_all | solution.py:477
  84.6 5.6 %shard_map.161 = (bf16[512,128]{1,0:T(8,128)(2,1)S(1)}, bf16[512,128]{1,0:T(8,128)(2,1)S(1)}, bf16[512,128]{1,0:T(8,128)(2,1)S(1)}, bf16[512,128]{1,0:T(8,128)(2...) custom-call(s32[2]{0:T(128)S(1)} %pad_add_fusion.place_ref, ...), custom_call_target="tpu_custom_call" | custom-call | flops 1073741824 | bytes 4980744 | tf_op jit(solution)/shard_map/pallas_call | solution.py:385
  90.2 1.6 %collective-permute-start.8 = (bf16[512,128]{1,0:T(8,128)(2,1)S(1)}, bf16[512,128]{1,0:T(8,128)(2,1)S(1)}, u32[]{:S(2)}, u32[]{:S(2)}) collective-permute-start(bf16[512,128]{1,0:T(8,128)(2,1)S(1)} %get-tuple-element.59), channel_id=1, source_target_pairs={{0,2},{2,4},{4,6},{6,8},{8,10},{10,12},{12,14},{14,0},{1,3},{3,5},... | collective-permute-start | bytes 393224 | tf_op jit(solution)/shard_map/ppermute | solution.py:399
  93.0 1.6 %collective-permute-start.10 = (bf16[512,128]{1,0:T(8,128)(2,1)S(1)}, bf16[512,128]{1,0:T(8,128)(2,1)S(1)}, u32[]{:S(2)}, u32[]{:S(2)}) collective-permute-start(bf16[512,128]{1,0:T(8,128)(2,1)S(1)} %get-tuple-element.61), channel_id=1, source_target_pairs={{0,6},{2,8},{4,10},{6,12},{8,14},{10,0},{12,2},{14,4},{1,7},{3,9},... | collective-permute-start | bytes 393224 | tf_op jit(solution)/shard_map/ppermute | solution.py:399
  95.2 2.4 %collective-permute-start.12 = (bf16[512,128]{1,0:T(8,128)(2,1)S(1)}, bf16[512,128]{1,0:T(8,128)(2,1)S(1)}, u32[]{:S(2)}, u32[]{:S(2)}) collective-permute-start(bf16[512,128]{1,0:T(8,128)(2,1)S(1)} %get-tuple-element.63), channel_id=1, source_target_pairs={{0,10},{2,12},{4,14},{6,0},{8,2},{10,4},{12,6},{14,8},{1,11},{3,13... | collective-permute-start | bytes 393224 | tf_op jit(solution)/shard_map/ppermute | solution.py:399
  97.7 2.7 %collective-permute-done.9.refs_2_ = bf16[512,128]{1,0:T(8,128)(2,1)S(1)} collective-permute-done((bf16[512,128]{1,0:T(8,128)(2,1)S(1)}, bf16[512,128]{1,0:T(8,128)(2,1)S(1)}, u32[]{:S(2)}, u32[]{:S(2)}) %collective-permute-start.9) | collective-permute-done | bytes 131104 | tf_op jit(solution)/shard_map/ppermute | solution.py:399
  101.3 5.1 %collective-permute-done.11.refs_4_ = bf16[512,128]{1,0:T(8,128)(2,1)S(1)} collective-permute-done((bf16[512,128]{1,0:T(8,128)(2,1)S(1)}, bf16[512,128]{1,0:T(8,128)(2,1)S(1)}, u32[]{:S(2)}, u32[]{:S(2)}) %collective-permute-start.11) | collective-permute-done | bytes 131104 | tf_op jit(solution)/shard_map/ppermute | solution.py:399
  107.2 3.1 %shard_map.162 = (bf16[256,1024]{1,0:T(8,128)(2,1)}, bf16[256,1024]{1,0:T(8,128)(2,1)}, bf16[256,1024]{1,0:T(8,128)(2,1)}, bf16[256,1024]{1,0:T(8,128)(2,1)}) custom-call(s32[2]{0:T(128)S(1)} %pad_add_fusion.place_ref, f32[16,8,512]{2,1,0:T(8,128)} %copy-done, bf16[256,1024]{1,0:T(8,128)(2,1)S(1)} %copy-done.3, bf16[256,1024]{1,0:T(8,128)(2,1)S(1)} %copy-done.1, ...), custom_call_target="tpu_custom_call" | custom-call | flops 1000 | bytes 4456456 | tf_op jit(solution)/shard_map/pallas_call | solution.py:385
  (44 shorter events, 10.3 us)
Async XLA Ops:
  3.6 35.6 %copy-start.7 = (f32[11,1024]{1,0:T(8,128)S(1)}, f32[11,1024]{1,0:T(8,128)}, u32[]{:S(2)}) copy-start(f32[11,1024]{1,0:T(8,128)} %param.19) | copy-start | bytes 135172
  3.6 28.0 %all-to-all-start = ((bf16[8,784,128]{2,1,0:T(8,128)(2,1)}), bf16[8,784,128]{2,1,0:T(8,128)(2,1)S(1)}, u32[]{:S(2)}, u32[]{:S(2)}) async-start(bf16[8,784,128]{2,1,0:T(8,128)(2,1)} %shard_map.155), calls=%async_computation | async-start | bytes 3211264 | tf_op jit(solution)/shard_map/all_to_all | solution.py:426
  10.5 7.5 %collective-permute-start.2 = (bf16[1,8,1024]{2,1,0:T(8,128)(2,1)S(1)}, bf16[1,8,1024]{2,1,0:T(8,128)(2,1)S(1)}, u32[]{:S(2)}, u32[]{:S(2)}) collective-permute-start(bf16[1,8,1024]{2,1,0:T(8,128)(2,1)S(1)} %bitcast.7), channel_id=1, source_target_pairs={{0,192},{16,208},{32,224},{48,240},{64,128},{80,144},{96,160},{112... | collective-permute-start | bytes 49160 | tf_op jit(solution)/shard_map/ppermute | solution.py:404
  15.8 6.6 %collective-permute-start.1 = (bf16[1,8,1024]{2,1,0:T(8,128)(2,1)S(1)}, bf16[1,8,1024]{2,1,0:T(8,128)(2,1)S(1)}, u32[]{:S(2)}, u32[]{:S(2)}) collective-permute-start(bf16[1,8,1024]{2,1,0:T(8,128)(2,1)S(1)} %bitcast.8), channel_id=1, source_target_pairs={{0,128},{16,144},{32,160},{48,176},{64,192},{80,208},{96,224},{112... | collective-permute-start | bytes 49160 | tf_op jit(solution)/shard_map/ppermute | solution.py:404
  16.8 5.6 %collective-permute-start = (bf16[1,8,1024]{2,1,0:T(8,128)(2,1)S(1)}, bf16[1,8,1024]{2,1,0:T(8,128)(2,1)S(1)}, u32[]{:S(2)}, u32[]{:S(2)}) collective-permute-start(bf16[1,8,1024]{2,1,0:T(8,128)(2,1)S(1)} %bitcast.9), channel_id=1, source_target_pairs={{0,64},{16,80},{32,96},{48,112},{64,0},{80,16},{96,32},{112,48},{1... | collective-permute-start | bytes 49160 | tf_op jit(solution)/shard_map/ppermute | solution.py:404
  22.4 4.3 %collective-permute-start.5 = (bf16[4,8,1024]{2,1,0:T(8,128)(2,1)S(1)}, bf16[4,8,1024]{2,1,0:T(8,128)(2,1)S(1)}, u32[]{:S(2)}, u32[]{:S(2)}) collective-permute-start(bf16[4,8,1024]{2,1,0:T(8,128)(2,1)S(1)} %pad_maximum_fusion.refs_0_), channel_id=1, source_target_pairs={{0,48},{16,32},{32,16},{48,0},{64,112},{80,96},{96,80},{112,64},{1... | collective-permute-start | bytes 196616 | tf_op jit(solution)/shard_map/ppermute | solution.py:404
  24.0 3.2 %collective-permute-start.4 = (bf16[4,8,1024]{2,1,0:T(8,128)(2,1)S(1)}, bf16[4,8,1024]{2,1,0:T(8,128)(2,1)S(1)}, u32[]{:S(2)}, u32[]{:S(2)}) collective-permute-start(bf16[4,8,1024]{2,1,0:T(8,128)(2,1)S(1)} %pad_maximum_fusion.refs_0_), channel_id=1, source_target_pairs={{0,32},{16,48},{32,0},{48,16},{64,96},{80,112},{96,64},{112,80},{1... | collective-permute-start | bytes 196616 | tf_op jit(solution)/shard_map/ppermute | solution.py:404
  24.9 4.1 %collective-permute-start.3 = (bf16[4,8,1024]{2,1,0:T(8,128)(2,1)S(1)}, bf16[4,8,1024]{2,1,0:T(8,128)(2,1)S(1)}, u32[]{:S(2)}, u32[]{:S(2)}) collective-permute-start(bf16[4,8,1024]{2,1,0:T(8,128)(2,1)S(1)} %pad_maximum_fusion.refs_0_), channel_id=1, source_target_pairs={{0,16},{16,0},{32,48},{48,32},{64,80},{80,64},{96,112},{112,96},{1... | collective-permute-start | bytes 196616 | tf_op jit(solution)/shard_map/ppermute | solution.py:404
  31.6 14.1 %collective-permute-start.6 = (bf16[4,256,128]{2,1,0:T(8,128)(2,1)S(1)}, bf16[4,256,128]{2,1,0:T(8,128)(2,1)S(1)}, u32[]{:S(2)}, u32[]{:S(2)}) collective-permute-start(bf16[4,256,128]{2,1,0:T(8,128)(2,1)S(1)} %slice.3), channel_id=1, source_target_pairs={{0,16},{16,32},{32,48},{48,64},{64,80},{80,96},{96,112},{112,128},... | collective-permute-start | bytes 786440 | tf_op jit(solution)/shard_map/ppermute | solution.py:432
  34.0 11.7 %all-to-all-start.1 = ((bf16[8,128,128]{2,1,0:T(8,128)(2,1)}), bf16[8,128,128]{2,1,0:T(8,128)(2,1)S(1)}, u32[]{:S(2)}, u32[]{:S(2)}) async-start(bf16[8,128,128]{2,1,0:T(8,128)(2,1)} %shard_map.156), calls=%async_computation.1 | async-start | bytes 524288 | tf_op jit(solution)/shard_map/all_to_all | solution.py:433
  66.5 18.1 %collective-permute-start.7 = (bf16[256,512]{1,0:T(8,128)(2,1)S(1)}, bf16[256,512]{1,0:T(8,128)(2,1)S(1)}, u32[]{:S(2)}, u32[]{:S(2)}) collective-permute-start(bf16[256,512]{1,0:T(8,128)(2,1)S(1)} %get-tuple-element.57), channel_id=1, source_target_pairs={{16,0},{32,16},{48,32},{64,48},{80,64},{96,80},{112,96},{128,112},... | collective-permute-start | bytes 786440 | tf_op jit(solution)/shard_map/ppermute | solution.py:459
  71.3 39.0 %all-to-all-start.3 = ((bf16[128,8,128]{2,1,0:T(8,128)(2,1)}), bf16[128,8,128]{2,1,0:T(8,128)(2,1)S(1)}, u32[]{:S(2)}, u32[]{:S(2)}) async-start(bf16[128,8,128]{2,1,0:T(8,128)(2,1)} %bitcast.6), calls=%async_computation.3 | async-start | bytes 524288 | tf_op jit(solution)/shard_map/all_to_all | solution.py:477
  84.6 22.7 %copy-start.1 = (bf16[256,1024]{1,0:T(8,128)(2,1)S(1)}, bf16[256,1024]{1,0:T(8,128)(2,1)}, u32[]{:S(2)}) copy-start(bf16[256,1024]{1,0:T(8,128)(2,1)} %key_ref.3) | copy-start | bytes 1572868
  84.6 22.7 %copy-start.2 = (bf16[256,1024]{1,0:T(8,128)(2,1)S(1)}, bf16[256,1024]{1,0:T(8,128)(2,1)}, u32[]{:S(2)}) copy-start(bf16[256,1024]{1,0:T(8,128)(2,1)} %value_ref.3) | copy-start | bytes 1572868
  84.6 22.6 %copy-start.3 = (bf16[256,1024]{1,0:T(8,128)(2,1)S(1)}, bf16[256,1024]{1,0:T(8,128)(2,1)}, u32[]{:S(2)}) copy-start(bf16[256,1024]{1,0:T(8,128)(2,1)} %query_ref.3) | copy-start | bytes 1572868
  84.6 22.6 %copy-start.4 = (bf16[256,1024]{1,0:T(8,128)(2,1)S(1)}, bf16[256,1024]{1,0:T(8,128)(2,1)}, u32[]{:S(2)}) copy-start(bf16[256,1024]{1,0:T(8,128)(2,1)} %cotangent_ref.3) | copy-start | bytes 1572868
  84.6 22.6 %copy-start.5 = (f32[256,1024]{1,0:T(8,128)S(1)}, f32[256,1024]{1,0:T(8,128)}, u32[]{:S(2)}) copy-start(f32[256,1024]{1,0:T(8,128)} %get-tuple-element.43.factor_ref) | copy-start | bytes 3145732
  90.2 7.5 %collective-permute-start.8 = (bf16[512,128]{1,0:T(8,128)(2,1)S(1)}, bf16[512,128]{1,0:T(8,128)(2,1)S(1)}, u32[]{:S(2)}, u32[]{:S(2)}) collective-permute-start(bf16[512,128]{1,0:T(8,128)(2,1)S(1)} %get-tuple-element.59), channel_id=1, source_target_pairs={{0,2},{2,4},{4,6},{6,8},{8,10},{10,12},{12,14},{14,0},{1,3},{3,5},... | collective-permute-start | bytes 393224 | tf_op jit(solution)/shard_map/ppermute | solution.py:399
  91.8 8.6 %collective-permute-start.9 = (bf16[512,128]{1,0:T(8,128)(2,1)S(1)}, bf16[512,128]{1,0:T(8,128)(2,1)S(1)}, u32[]{:S(2)}, u32[]{:S(2)}) collective-permute-start(bf16[512,128]{1,0:T(8,128)(2,1)S(1)} %get-tuple-element.60), channel_id=1, source_target_pairs={{0,4},{2,6},{4,8},{6,10},{8,12},{10,14},{12,0},{14,2},{1,5},{3,7},... | collective-permute-start | bytes 393224 | tf_op jit(solution)/shard_map/ppermute | solution.py:399
  93.0 8.3 %collective-permute-start.10 = (bf16[512,128]{1,0:T(8,128)(2,1)S(1)}, bf16[512,128]{1,0:T(8,128)(2,1)S(1)}, u32[]{:S(2)}, u32[]{:S(2)}) collective-permute-start(bf16[512,128]{1,0:T(8,128)(2,1)S(1)} %get-tuple-element.61), channel_id=1, source_target_pairs={{0,6},{2,8},{4,10},{6,12},{8,14},{10,0},{12,2},{14,4},{1,7},{3,9},... | collective-permute-start | bytes 393224 | tf_op jit(solution)/shard_map/ppermute | solution.py:399
  94.7 11.7 %collective-permute-start.11 = (bf16[512,128]{1,0:T(8,128)(2,1)S(1)}, bf16[512,128]{1,0:T(8,128)(2,1)S(1)}, u32[]{:S(2)}, u32[]{:S(2)}) collective-permute-start(bf16[512,128]{1,0:T(8,128)(2,1)S(1)} %get-tuple-element.62), channel_id=1, source_target_pairs={{0,8},{2,10},{4,12},{6,14},{8,0},{10,2},{12,4},{14,6},{1,9},{3,11}... | collective-permute-start | bytes 393224 | tf_op jit(solution)/shard_map/ppermute | solution.py:399
  95.2 11.7 %collective-permute-start.12 = (bf16[512,128]{1,0:T(8,128)(2,1)S(1)}, bf16[512,128]{1,0:T(8,128)(2,1)S(1)}, u32[]{:S(2)}, u32[]{:S(2)}) collective-permute-start(bf16[512,128]{1,0:T(8,128)(2,1)S(1)} %get-tuple-element.63), channel_id=1, source_target_pairs={{0,10},{2,12},{4,14},{6,0},{8,2},{10,4},{12,6},{14,8},{1,11},{3,13... | collective-permute-start | bytes 393224 | tf_op jit(solution)/shard_map/ppermute | solution.py:399
  97.6 9.3 %collective-permute-start.13 = (bf16[512,128]{1,0:T(8,128)(2,1)S(1)}, bf16[512,128]{1,0:T(8,128)(2,1)S(1)}, u32[]{:S(2)}, u32[]{:S(2)}) collective-permute-start(bf16[512,128]{1,0:T(8,128)(2,1)S(1)} %get-tuple-element.64), channel_id=1, source_target_pairs={{0,12},{2,14},{4,0},{6,2},{8,4},{10,6},{12,8},{14,10},{1,13},{3,15... | collective-permute-start | bytes 393224 | tf_op jit(solution)/shard_map/ppermute | solution.py:399
  100.4 6.8 %collective-permute-start.14 = (bf16[512,128]{1,0:T(8,128)(2,1)S(1)}, bf16[512,128]{1,0:T(8,128)(2,1)S(1)}, u32[]{:S(2)}, u32[]{:S(2)}) collective-permute-start(bf16[512,128]{1,0:T(8,128)(2,1)S(1)} %get-tuple-element.65), channel_id=1, source_target_pairs={{0,14},{2,0},{4,2},{6,4},{8,6},{10,8},{12,10},{14,12},{1,15},{3,1}... | collective-permute-start | bytes 393224 | tf_op jit(solution)/shard_map/ppermute | solution.py:399
  (3 other events, 20.8 us)

commit v6 on v4

--- a/solution.py
+++ b/solution.py
@@ -237,11 +237,11 @@
 
 
 def filter_terms(
-    grad_ref, own_ref, before_ref, forward_high, forward_low, inverse_high, inverse_low, grad_spec_hbm, terms_ref,
+    grad_ref, own_ref, before_ref, forward_high, forward_low, inverse_high, inverse_low, grad_hbm, terms_ref,
     product_ref, grad_spec_ref, sems,
 ):
     grad_spec_ref[...] = spectrum((forward_high, forward_low), grad_ref[...])
-    copy = copy_out(grad_spec_ref, grad_spec_hbm, sems.at[0])
+    copy = copy_out(grad_ref, grad_hbm, sems.at[0])
 
     def step(row, sign):
         real, imag = read_blocks(own_ref, before_ref, row)
@@ -266,13 +266,13 @@
 
 
 def correlate_back(place_ref, *refs):
-    tables_hbm, (grad_spec_hbm, lag_spec_hbm, rounded_hbm, after_ref) = refs[:4], refs[4:8]
+    tables_hbm, (grad_hbm, lag_spec_hbm, rounded_hbm, after_ref) = refs[:4], refs[4:8]
     out_refs, tables = refs[8 : 8 + GROUP], refs[8 + GROUP : 12 + GROUP]
-    result_ref, after_spec_ref, product_ref, grad_spec_ref, lag_spec_ref, sems = refs[12 + GROUP :]
+    result_ref, after_spec_ref, product_ref, grad_spec_ref, lag_spec_ref, grad_ref, sems = refs[12 + GROUP :]
     place = place_ref[0]
     table_loads = [copy_out(tables_hbm[i], tables[i], sems.at[i]) for i in range(2)]
     loads = [
-        copy_out(grad_spec_hbm, grad_spec_ref, sems.at[4]),
+        copy_out(grad_hbm, grad_ref, sems.at[4]),
         copy_out(lag_spec_hbm, lag_spec_ref, sems.at[5]),
     ]
     table_loads += [copy_out(tables_hbm[i], tables[i], sems.at[i]) for i in range(2, 4)]
@@ -288,8 +288,9 @@
     table_loads[0].wait()
     table_loads[1].wait()
     after_spec_ref[...] = spectrum((forward_high, forward_low), after_ref[...])
-    for load in loads:
-        load.wait()
+    loads[0].wait()
+    grad_spec_ref[...] = spectrum((forward_high, forward_low), grad_ref[...])
+    loads[1].wait()
 
     def step(row, sign):
         real = [grad_spec_ref[pl.ds(row, 8), col(b)] for b in range(GROUP)]
@@ -451,7 +452,7 @@
     )
     after = lax.ppermute(first, "g", [(i, i - 1) for i in range(1, groups)])
     grad_spec, terms = call(
-        filter_terms, [off_chip((2 * LEN, wide), F32), off_chip((REACH, LEN, LANES), BF16)],
+        filter_terms, [off_chip((LEN, wide), BF16), off_chip((REACH, LEN, LANES), BF16)],
         near(grad_conv), own, before_spec, *near_tables, copies=(1,), manual=(0,),
         scratch=[((2 * LEN, half), F32), ((2 * LEN, wide), F32)],
         cost=2 * 7 * LEN * LEN * wide,
@@ -462,7 +463,7 @@
         scratch=[(t.shape, BF16) for t in tables]
         + [
             ((LEN, wide), BF16), ((2 * LEN, half), F32), ((2 * LEN, wide), F32), ((2 * LEN, wide), F32),
-            ((2 * LEN, half), F32),
+            ((2 * LEN, half), F32), ((LEN, wide), BF16),
         ],
         cost=2 * 8 * LEN * LEN * wide,
     )

time: 112 us -> 112 us (level)
  no operation moved by 1% of the time
where the time goes in v6:
time: 112 us
  starting transfers between devices  46.7 us (42%)
  Pallas kernels  27.3 us (24%)
  waiting for transfers between devices  21.5 us (19%)
  blocking collectives  14.4 us (13%)
    pallas_call x9, Pallas kernels, call(): pl.pallas_call(body, out_shape=list(outs), in_specs=specs, out_specs=[pl....  27.3 us
    all_to_all x1, blocking collectives, shards(): sums = lax.all_to_all(sums, ('j', 'ch'), 0, 0)  14.4 us
    all_to_all x1, starting transfers between devices, shards(): lax.all_to_all(terms.reshape(groups * GROUP, lag_rows, LANES), ('g', 'j')...  13.3 us
    ppermute x6, starting transfers between devices, trade(): return lax.ppermute(value, 'g', [(i, i ^ mask) for i in range(groups)])  10.2 us
    ppermute x7, waiting for transfers between devices, swap(): lax.ppermute(pieces[step], 'j', [(i, (i + step) % GROUP) for i in range(G...  9.49 us
    ppermute x6, waiting for transfers between devices, trade(): return lax.ppermute(value, 'g', [(i, i ^ mask) for i in range(groups)])  8.26 us
    ppermute x7, starting transfers between devices, swap(): lax.ppermute(pieces[step], 'j', [(i, (i + step) % GROUP) for i in range(G...  7.55 us
    all_to_all x1, starting transfers between devices, shards(): got = lax.all_to_all(sent, 'j', 0, 0)  6.87 us
  transfers between devices with their start and end apart: 18, of which 11 were waited for; matrix products, arithmetic and copies ran while one was open for 1% of the time, Pallas kernels for 15%

profile of v6, /device:TPU:1, one launch (start us, length us, event | category | flops | bytes accessed | tf_op | source)
XLA Modules:
  0.0 111.6 jit_solution(11203428174432422147)
XLA Ops:
  0.6 2.9 %shard_map.155 = bf16[8,784,128]{2,1,0:T(8,128)(2,1)} custom-call(bf16[256,1024]{1,0:T(8,128)(2,1)} %key_ref.3, bf16[256,1024]{1,0:T(8,128)(2,1)} %value_ref.3, bf16[256,1024]{1,0:T(8,128)(2,1)} %query_ref.3, bf16[256,1024]{1,0:T(8,128)(2,1)} %cotangent_ref.3, s32[1,256]{1,0:T(1,128)} %bitcast.13, s32[1,512]{1,0:T(1,128)} %bitcast.11), custom_call_target="tpu_custom_call" | custom-call | flops 1000 | bytes 2100224 | tf_op jit(solution)/shard_map/pallas_call | solution.py:380
  3.6 6.9 %all-to-all-start = ((bf16[8,784,128]{2,1,0:T(8,128)(2,1)}), bf16[8,784,128]{2,1,0:T(8,128)(2,1)S(1)}, u32[]{:S(2)}, u32[]{:S(2)}) async-start(bf16[8,784,128]{2,1,0:T(8,128)(2,1)} %shard_map.155), calls=%async_computation | async-start | bytes 3211264 | tf_op jit(solution)/shard_map/all_to_all | solution.py:420
  10.5 5.3 %collective-permute-start.2 = (bf16[1,8,1024]{2,1,0:T(8,128)(2,1)S(1)}, bf16[1,8,1024]{2,1,0:T(8,128)(2,1)S(1)}, u32[]{:S(2)}, u32[]{:S(2)}) collective-permute-start(bf16[1,8,1024]{2,1,0:T(8,128)(2,1)S(1)} %bitcast.7), channel_id=1, source_target_pairs={{0,192},{16,208},{32,224},{48,240},{64,128},{80,144},{96,160},{112... | collective-permute-start | bytes 49160 | tf_op jit(solution)/shard_map/ppermute | solution.py:399
  17.9 4.4 %collective-permute-done.1 = bf16[1,8,1024]{2,1,0:T(8,128)(2,1)S(1)} collective-permute-done((bf16[1,8,1024]{2,1,0:T(8,128)(2,1)S(1)}, bf16[1,8,1024]{2,1,0:T(8,128)(2,1)S(1)}, u32[]{:S(2)}, u32[]{:S(2)}) %collective-permute-start.1) | collective-permute-done | bytes 16416 | tf_op jit(solution)/shard_map/ppermute | solution.py:399
  22.4 1.7 %collective-permute-start.5 = (bf16[4,8,1024]{2,1,0:T(8,128)(2,1)S(1)}, bf16[4,8,1024]{2,1,0:T(8,128)(2,1)S(1)}, u32[]{:S(2)}, u32[]{:S(2)}) collective-permute-start(bf16[4,8,1024]{2,1,0:T(8,128)(2,1)S(1)} %pad_maximum_fusion.refs_0_), channel_id=1, source_target_pairs={{0,48},{16,32},{32,16},{48,0},{64,112},{80,96},{96,80},{112,64},{1... | collective-permute-start | bytes 196616 | tf_op jit(solution)/shard_map/ppermute | solution.py:399
  25.1 1.6 %collective-permute-done.5.refs_3_ = bf16[4,8,1024]{2,1,0:T(8,128)(2,1)S(1)} collective-permute-done((bf16[4,8,1024]{2,1,0:T(8,128)(2,1)S(1)}, bf16[4,8,1024]{2,1,0:T(8,128)(2,1)S(1)}, u32[]{:S(2)}, u32[]{:S(2)}) %collective-permute-start.5) | collective-permute-done | bytes 65568 | tf_op jit(solution)/shard_map/ppermute | solution.py:399
  27.2 1.8 %collective-permute-done.3.refs_1_ = bf16[4,8,1024]{2,1,0:T(8,128)(2,1)S(1)} collective-permute-done((bf16[4,8,1024]{2,1,0:T(8,128)(2,1)S(1)}, bf16[4,8,1024]{2,1,0:T(8,128)(2,1)S(1)}, u32[]{:S(2)}, u32[]{:S(2)}) %collective-permute-start.3) | collective-permute-done | bytes 65568 | tf_op jit(solution)/shard_map/ppermute | solution.py:399
  29.7 1.9 %all-to-all-done.got_ref.got_hbm = bf16[8,784,128]{2,1,0:T(8,128)(2,1)S(1)} async-done(((bf16[8,784,128]{2,1,0:T(8,128)(2,1)}), bf16[8,784,128]{2,1,0:T(8,128)(2,1)S(1)}, u32[]{:S(2)}, u32[]{:S(2)}) %all-to-all-start) | async-done | bytes 1605664 | tf_op jit(solution)/shard_map/all_to_all | solution.py:420
  31.6 2.4 %collective-permute-start.6 = (bf16[4,256,128]{2,1,0:T(8,128)(2,1)S(1)}, bf16[4,256,128]{2,1,0:T(8,128)(2,1)S(1)}, u32[]{:S(2)}, u32[]{:S(2)}) collective-permute-start(bf16[4,256,128]{2,1,0:T(8,128)(2,1)S(1)} %slice.3), channel_id=1, source_target_pairs={{0,16},{16,32},{32,48},{48,64},{64,80},{80,96},{96,112},{112,128},... | collective-permute-start | bytes 786440 | tf_op jit(solution)/shard_map/ppermute | solution.py:426
  33.9 5.2 %all-to-all-start.1 = ((bf16[8,128,128]{2,1,0:T(8,128)(2,1)}), bf16[8,128,128]{2,1,0:T(8,128)(2,1)S(1)}, u32[]{:S(2)}, u32[]{:S(2)}) async-start(bf16[8,128,128]{2,1,0:T(8,128)(2,1)} %shard_map.156), calls=%async_computation.1 | async-start | bytes 524288 | tf_op jit(solution)/shard_map/all_to_all | solution.py:427
  39.9 3.9 %shard_map.157 = (f32[512,1024]{1,0:T(8,128)}, f32[256,1024]{1,0:T(8,128)}) custom-call(s32[2]{0:T(128)S(1)} %pad_add_fusion.place_ref, f32[16,1024]{1,0:T(8,128)} %pad.4.table_ref, bf16[8,784,128]{2,1,0:T(8,128)(2,1)} %copy-done.5, bf16[512,256]{1,0:T(8,128)(2,1)} %constant.22.clone.forward_high.refs_0_, bf16[512,256]{1,0:T(8,128)(2,1)} %constant.23.clone.forward_low.refs_1_), custom_call_target="tpu_custom_call" | custom-call | flops 536870912 | bytes 2195464 | tf_op jit(solution)/shard_map/pallas_call | solution.py:380
  43.8 1.9 %all-to-all-done.1.lags_ref = bf16[8,128,128]{2,1,0:T(8,128)(2,1)S(1)} async-done(((bf16[8,128,128]{2,1,0:T(8,128)(2,1)}), bf16[8,128,128]{2,1,0:T(8,128)(2,1)S(1)}, u32[]{:S(2)}, u32[]{:S(2)}) %all-to-all-start.1) | async-done | bytes 262176 | tf_op jit(solution)/shard_map/all_to_all | solution.py:427
  45.7 5.7 %shard_map.158 = (f32[512,1024]{1,0:T(8,128)S(1)}, f32[256,1024]{1,0:T(8,128)S(1)}, bf16[8,256,128]{2,1,0:T(8,128)(2,1)S(1)}, f32[512,512]{1,0:T(8,128)S(1)}, f3...) custom-call(s32[2]{0:T(128)S(1)} %pad_add_fusion.place_ref, ...), custom_call_target="tpu_custom_call" | custom-call | flops 1342177280 | bytes 6324232 | tf_op jit(solution)/shard_map/pallas_call | solution.py:380
  51.4 14.4 %all_to_all.20.sums_ref = f32[16,8,512]{2,1,0:T(8,128)S(1)} all-to-all(f32[16,8,512]{2,1,0:T(8,128)S(1)} %get-tuple-element.41), channel_id=1, replica_groups=mesh['g'=16,'j'=8,'ch'=2] {'j','ch'}, dimensions={0} | all-to-all | bytes 524288 | tf_op jit(solution)/shard_map/all_to_all | solution.py:448
  66.6 1.3 %collective-permute-start.7 = (bf16[256,512]{1,0:T(8,128)(2,1)S(1)}, bf16[256,512]{1,0:T(8,128)(2,1)S(1)}, u32[]{:S(2)}, u32[]{:S(2)}) collective-permute-start(bf16[256,512]{1,0:T(8,128)(2,1)S(1)} %get-tuple-element.55), channel_id=1, source_target_pairs={{16,0},{32,16},{48,32},{64,48},{80,64},{96,80},{112,96},{128,112},... | collective-permute-start | bytes 786440 | tf_op jit(solution)/shard_map/ppermute | solution.py:453
  67.9 3.4 %shard_map.160 = (bf16[256,1024]{1,0:T(8,128)(2,1)}, bf16[4,256,128]{2,1,0:T(8,128)(2,1)}) custom-call(bf16[256,1024]{1,0:T(8,128)(2,1)S(1)} %get-tuple-element.45.grad_ref, f32[512,1024]{1,0:T(8,128)S(1)} %get-tuple-element.46.own_ref, f32[512,512]{1,0:T(8,128)S(1)} %get-tuple-element.47.before_ref, bf16[512,256]{1,0:T(8,128)(2,1)S(1)} %get-tuple-element.48.forward_high, ...), custom_call_target="tpu_custom_call" | custom-call | flops 939524096 | bytes 4718592 | tf_op jit(solution)/shard_map/pallas_call | solution.py:380
  71.4 13.3 %all-to-all-start.3 = ((bf16[128,8,128]{2,1,0:T(8,128)(2,1)}), bf16[128,8,128]{2,1,0:T(8,128)(2,1)S(1)}, u32[]{:S(2)}, u32[]{:S(2)}) async-start(bf16[128,8,128]{2,1,0:T(8,128)(2,1)} %bitcast.6), calls=%async_computation.3 | async-start | bytes 524288 | tf_op jit(solution)/shard_map/all_to_all | solution.py:471
  84.7 5.4 %shard_map.161 = (bf16[512,128]{1,0:T(8,128)(2,1)S(1)}, bf16[512,128]{1,0:T(8,128)(2,1)S(1)}, bf16[512,128]{1,0:T(8,128)(2,1)S(1)}, bf16[512,128]{1,0:T(8,128)(2...) custom-call(s32[2]{0:T(128)S(1)} %pad_add_fusion.place_ref, ...), custom_call_target="tpu_custom_call" | custom-call | flops 1073741824 | bytes 3407880 | tf_op jit(solution)/shard_map/pallas_call | solution.py:380
  90.1 1.6 %collective-permute-start.8 = (bf16[512,128]{1,0:T(8,128)(2,1)S(1)}, bf16[512,128]{1,0:T(8,128)(2,1)S(1)}, u32[]{:S(2)}, u32[]{:S(2)}) collective-permute-start(bf16[512,128]{1,0:T(8,128)(2,1)S(1)} %get-tuple-element.57), channel_id=1, source_target_pairs={{0,2},{2,4},{4,6},{6,8},{8,10},{10,12},{12,14},{14,0},{1,3},{3,5},... | collective-permute-start | bytes 393224 | tf_op jit(solution)/shard_map/ppermute | solution.py:394
  93.0 1.6 %collective-permute-start.10 = (bf16[512,128]{1,0:T(8,128)(2,1)S(1)}, bf16[512,128]{1,0:T(8,128)(2,1)S(1)}, u32[]{:S(2)}, u32[]{:S(2)}) collective-permute-start(bf16[512,128]{1,0:T(8,128)(2,1)S(1)} %get-tuple-element.59), channel_id=1, source_target_pairs={{0,6},{2,8},{4,10},{6,12},{8,14},{10,0},{12,2},{14,4},{1,7},{3,9},... | collective-permute-start | bytes 393224 | tf_op jit(solution)/shard_map/ppermute | solution.py:394
  95.2 2.4 %collective-permute-start.12 = (bf16[512,128]{1,0:T(8,128)(2,1)S(1)}, bf16[512,128]{1,0:T(8,128)(2,1)S(1)}, u32[]{:S(2)}, u32[]{:S(2)}) collective-permute-start(bf16[512,128]{1,0:T(8,128)(2,1)S(1)} %get-tuple-element.61), channel_id=1, source_target_pairs={{0,10},{2,12},{4,14},{6,0},{8,2},{10,4},{12,6},{14,8},{1,11},{3,13... | collective-permute-start | bytes 393224 | tf_op jit(solution)/shard_map/ppermute | solution.py:394
  97.7 2.7 %collective-permute-done.9.refs_2_ = bf16[512,128]{1,0:T(8,128)(2,1)S(1)} collective-permute-done((bf16[512,128]{1,0:T(8,128)(2,1)S(1)}, bf16[512,128]{1,0:T(8,128)(2,1)S(1)}, u32[]{:S(2)}, u32[]{:S(2)}) %collective-permute-start.9) | collective-permute-done | bytes 131104 | tf_op jit(solution)/shard_map/ppermute | solution.py:394
  101.4 4.9 %collective-permute-done.11.refs_4_ = bf16[512,128]{1,0:T(8,128)(2,1)S(1)} collective-permute-done((bf16[512,128]{1,0:T(8,128)(2,1)S(1)}, bf16[512,128]{1,0:T(8,128)(2,1)S(1)}, u32[]{:S(2)}, u32[]{:S(2)}) %collective-permute-start.11) | collective-permute-done | bytes 131104 | tf_op jit(solution)/shard_map/ppermute | solution.py:394
  107.2 3.7 %shard_map.162 = (bf16[256,1024]{1,0:T(8,128)(2,1)}, bf16[256,1024]{1,0:T(8,128)(2,1)}, bf16[256,1024]{1,0:T(8,128)(2,1)}, bf16[256,1024]{1,0:T(8,128)(2,1)}) custom-call(s32[2]{0:T(128)S(1)} %pad_add_fusion.place_ref, f32[16,8,512]{2,1,0:T(8,128)} %copy-done, bf16[256,1024]{1,0:T(8,128)(2,1)S(1)} %copy-done.3, bf16[256,1024]{1,0:T(8,128)(2,1)S(1)} %copy-done.1, ...), custom_call_target="tpu_custom_call" | custom-call | flops 1000 | bytes 3476488 | tf_op jit(solution)/shard_map/pallas_call | solution.py:380
  (42 shorter events, 10.4 us)
Async XLA Ops:
  3.6 35.6 %copy-start.6 = (f32[11,1024]{1,0:T(8,128)S(1)}, f32[11,1024]{1,0:T(8,128)}, u32[]{:S(2)}) copy-start(f32[11,1024]{1,0:T(8,128)} %param.19) | copy-start | bytes 135172
  3.6 28.0 %all-to-all-start = ((bf16[8,784,128]{2,1,0:T(8,128)(2,1)}), bf16[8,784,128]{2,1,0:T(8,128)(2,1)S(1)}, u32[]{:S(2)}, u32[]{:S(2)}) async-start(bf16[8,784,128]{2,1,0:T(8,128)(2,1)} %shard_map.155), calls=%async_computation | async-start | bytes 3211264 | tf_op jit(solution)/shard_map/all_to_all | solution.py:420
  10.5 7.5 %collective-permute-start.2 = (bf16[1,8,1024]{2,1,0:T(8,128)(2,1)S(1)}, bf16[1,8,1024]{2,1,0:T(8,128)(2,1)S(1)}, u32[]{:S(2)}, u32[]{:S(2)}) collective-permute-start(bf16[1,8,1024]{2,1,0:T(8,128)(2,1)S(1)} %bitcast.7), channel_id=1, source_target_pairs={{0,192},{16,208},{32,224},{48,240},{64,128},{80,144},{96,160},{112... | collective-permute-start | bytes 49160 | tf_op jit(solution)/shard_map/ppermute | solution.py:399
  15.8 6.6 %collective-permute-start.1 = (bf16[1,8,1024]{2,1,0:T(8,128)(2,1)S(1)}, bf16[1,8,1024]{2,1,0:T(8,128)(2,1)S(1)}, u32[]{:S(2)}, u32[]{:S(2)}) collective-permute-start(bf16[1,8,1024]{2,1,0:T(8,128)(2,1)S(1)} %bitcast.8), channel_id=1, source_target_pairs={{0,128},{16,144},{32,160},{48,176},{64,192},{80,208},{96,224},{112... | collective-permute-start | bytes 49160 | tf_op jit(solution)/shard_map/ppermute | solution.py:399
  16.7 5.6 %collective-permute-start = (bf16[1,8,1024]{2,1,0:T(8,128)(2,1)S(1)}, bf16[1,8,1024]{2,1,0:T(8,128)(2,1)S(1)}, u32[]{:S(2)}, u32[]{:S(2)}) collective-permute-start(bf16[1,8,1024]{2,1,0:T(8,128)(2,1)S(1)} %bitcast.9), channel_id=1, source_target_pairs={{0,64},{16,80},{32,96},{48,112},{64,0},{80,16},{96,32},{112,48},{1... | collective-permute-start | bytes 49160 | tf_op jit(solution)/shard_map/ppermute | solution.py:399
  22.4 4.3 %collective-permute-start.5 = (bf16[4,8,1024]{2,1,0:T(8,128)(2,1)S(1)}, bf16[4,8,1024]{2,1,0:T(8,128)(2,1)S(1)}, u32[]{:S(2)}, u32[]{:S(2)}) collective-permute-start(bf16[4,8,1024]{2,1,0:T(8,128)(2,1)S(1)} %pad_maximum_fusion.refs_0_), channel_id=1, source_target_pairs={{0,48},{16,32},{32,16},{48,0},{64,112},{80,96},{96,80},{112,64},{1... | collective-permute-start | bytes 196616 | tf_op jit(solution)/shard_map/ppermute | solution.py:399
  24.0 3.2 %collective-permute-start.4 = (bf16[4,8,1024]{2,1,0:T(8,128)(2,1)S(1)}, bf16[4,8,1024]{2,1,0:T(8,128)(2,1)S(1)}, u32[]{:S(2)}, u32[]{:S(2)}) collective-permute-start(bf16[4,8,1024]{2,1,0:T(8,128)(2,1)S(1)} %pad_maximum_fusion.refs_0_), channel_id=1, source_target_pairs={{0,32},{16,48},{32,0},{48,16},{64,96},{80,112},{96,64},{112,80},{1... | collective-permute-start | bytes 196616 | tf_op jit(solution)/shard_map/ppermute | solution.py:399
  24.8 4.1 %collective-permute-start.3 = (bf16[4,8,1024]{2,1,0:T(8,128)(2,1)S(1)}, bf16[4,8,1024]{2,1,0:T(8,128)(2,1)S(1)}, u32[]{:S(2)}, u32[]{:S(2)}) collective-permute-start(bf16[4,8,1024]{2,1,0:T(8,128)(2,1)S(1)} %pad_maximum_fusion.refs_0_), channel_id=1, source_target_pairs={{0,16},{16,0},{32,48},{48,32},{64,80},{80,64},{96,112},{112,96},{1... | collective-permute-start | bytes 196616 | tf_op jit(solution)/shard_map/ppermute | solution.py:399
  31.6 8.3 %copy-start.5 = (bf16[8,784,128]{2,1,0:T(8,128)(2,1)}, bf16[8,784,128]{2,1,0:T(8,128)(2,1)S(1)}, u32[]{:S(2)}) copy-start(bf16[8,784,128]{2,1,0:T(8,128)(2,1)S(1)} %all-to-all-done.got_ref.got_hbm) | copy-start | bytes 4816900
  31.6 14.1 %collective-permute-start.6 = (bf16[4,256,128]{2,1,0:T(8,128)(2,1)S(1)}, bf16[4,256,128]{2,1,0:T(8,128)(2,1)S(1)}, u32[]{:S(2)}, u32[]{:S(2)}) collective-permute-start(bf16[4,256,128]{2,1,0:T(8,128)(2,1)S(1)} %slice.3), channel_id=1, source_target_pairs={{0,16},{16,32},{32,48},{48,64},{64,80},{80,96},{96,112},{112,128},... | collective-permute-start | bytes 786440 | tf_op jit(solution)/shard_map/ppermute | solution.py:426
  33.9 11.7 %all-to-all-start.1 = ((bf16[8,128,128]{2,1,0:T(8,128)(2,1)}), bf16[8,128,128]{2,1,0:T(8,128)(2,1)S(1)}, u32[]{:S(2)}, u32[]{:S(2)}) async-start(bf16[8,128,128]{2,1,0:T(8,128)(2,1)} %shard_map.156), calls=%async_computation.1 | async-start | bytes 524288 | tf_op jit(solution)/shard_map/all_to_all | solution.py:427
  66.6 18.1 %collective-permute-start.7 = (bf16[256,512]{1,0:T(8,128)(2,1)S(1)}, bf16[256,512]{1,0:T(8,128)(2,1)S(1)}, u32[]{:S(2)}, u32[]{:S(2)}) collective-permute-start(bf16[256,512]{1,0:T(8,128)(2,1)S(1)} %get-tuple-element.55), channel_id=1, source_target_pairs={{16,0},{32,16},{48,32},{64,48},{80,64},{96,80},{112,96},{128,112},... | collective-permute-start | bytes 786440 | tf_op jit(solution)/shard_map/ppermute | solution.py:453
  71.4 39.6 %all-to-all-start.3 = ((bf16[128,8,128]{2,1,0:T(8,128)(2,1)}), bf16[128,8,128]{2,1,0:T(8,128)(2,1)S(1)}, u32[]{:S(2)}, u32[]{:S(2)}) async-start(bf16[128,8,128]{2,1,0:T(8,128)(2,1)} %bitcast.6), calls=%async_computation.3 | async-start | bytes 524288 | tf_op jit(solution)/shard_map/all_to_all | solution.py:471
  84.7 22.5 %copy-start.1 = (bf16[256,1024]{1,0:T(8,128)(2,1)S(1)}, bf16[256,1024]{1,0:T(8,128)(2,1)}, u32[]{:S(2)}) copy-start(bf16[256,1024]{1,0:T(8,128)(2,1)} %key_ref.3) | copy-start | bytes 1572868
  84.7 22.5 %copy-start.2 = (bf16[256,1024]{1,0:T(8,128)(2,1)S(1)}, bf16[256,1024]{1,0:T(8,128)(2,1)}, u32[]{:S(2)}) copy-start(bf16[256,1024]{1,0:T(8,128)(2,1)} %value_ref.3) | copy-start | bytes 1572868
  84.7 22.5 %copy-start.3 = (bf16[256,1024]{1,0:T(8,128)(2,1)S(1)}, bf16[256,1024]{1,0:T(8,128)(2,1)}, u32[]{:S(2)}) copy-start(bf16[256,1024]{1,0:T(8,128)(2,1)} %query_ref.3) | copy-start | bytes 1572868
  84.7 22.5 %copy-start.4 = (bf16[256,1024]{1,0:T(8,128)(2,1)S(1)}, bf16[256,1024]{1,0:T(8,128)(2,1)}, u32[]{:S(2)}) copy-start(bf16[256,1024]{1,0:T(8,128)(2,1)} %cotangent_ref.3) | copy-start | bytes 1572868
  90.1 7.5 %collective-permute-start.8 = (bf16[512,128]{1,0:T(8,128)(2,1)S(1)}, bf16[512,128]{1,0:T(8,128)(2,1)S(1)}, u32[]{:S(2)}, u32[]{:S(2)}) collective-permute-start(bf16[512,128]{1,0:T(8,128)(2,1)S(1)} %get-tuple-element.57), channel_id=1, source_target_pairs={{0,2},{2,4},{4,6},{6,8},{8,10},{10,12},{12,14},{14,0},{1,3},{3,5},... | collective-permute-start | bytes 393224 | tf_op jit(solution)/shard_map/ppermute | solution.py:394
  91.8 8.6 %collective-permute-start.9 = (bf16[512,128]{1,0:T(8,128)(2,1)S(1)}, bf16[512,128]{1,0:T(8,128)(2,1)S(1)}, u32[]{:S(2)}, u32[]{:S(2)}) collective-permute-start(bf16[512,128]{1,0:T(8,128)(2,1)S(1)} %get-tuple-element.58), channel_id=1, source_target_pairs={{0,4},{2,6},{4,8},{6,10},{8,12},{10,14},{12,0},{14,2},{1,5},{3,7},... | collective-permute-start | bytes 393224 | tf_op jit(solution)/shard_map/ppermute | solution.py:394
  93.0 8.4 %collective-permute-start.10 = (bf16[512,128]{1,0:T(8,128)(2,1)S(1)}, bf16[512,128]{1,0:T(8,128)(2,1)S(1)}, u32[]{:S(2)}, u32[]{:S(2)}) collective-permute-start(bf16[512,128]{1,0:T(8,128)(2,1)S(1)} %get-tuple-element.59), channel_id=1, source_target_pairs={{0,6},{2,8},{4,10},{6,12},{8,14},{10,0},{12,2},{14,4},{1,7},{3,9},... | collective-permute-start | bytes 393224 | tf_op jit(solution)/shard_map/ppermute | solution.py:394
  94.6 11.7 %collective-permute-start.11 = (bf16[512,128]{1,0:T(8,128)(2,1)S(1)}, bf16[512,128]{1,0:T(8,128)(2,1)S(1)}, u32[]{:S(2)}, u32[]{:S(2)}) collective-permute-start(bf16[512,128]{1,0:T(8,128)(2,1)S(1)} %get-tuple-element.60), channel_id=1, source_target_pairs={{0,8},{2,10},{4,12},{6,14},{8,0},{10,2},{12,4},{14,6},{1,9},{3,11}... | collective-permute-start | bytes 393224 | tf_op jit(solution)/shard_map/ppermute | solution.py:394
  95.2 11.7 %collective-permute-start.12 = (bf16[512,128]{1,0:T(8,128)(2,1)S(1)}, bf16[512,128]{1,0:T(8,128)(2,1)S(1)}, u32[]{:S(2)}, u32[]{:S(2)}) collective-permute-start(bf16[512,128]{1,0:T(8,128)(2,1)S(1)} %get-tuple-element.61), channel_id=1, source_target_pairs={{0,10},{2,12},{4,14},{6,0},{8,2},{10,4},{12,6},{14,8},{1,11},{3,13... | collective-permute-start | bytes 393224 | tf_op jit(solution)/shard_map/ppermute | solution.py:394
  97.6 9.3 %collective-permute-start.13 = (bf16[512,128]{1,0:T(8,128)(2,1)S(1)}, bf16[512,128]{1,0:T(8,128)(2,1)S(1)}, u32[]{:S(2)}, u32[]{:S(2)}) collective-permute-start(bf16[512,128]{1,0:T(8,128)(2,1)S(1)} %get-tuple-element.62), channel_id=1, source_target_pairs={{0,12},{2,14},{4,0},{6,2},{8,4},{10,6},{12,8},{14,10},{1,13},{3,15... | collective-permute-start | bytes 393224 | tf_op jit(solution)/shard_map/ppermute | solution.py:394
  100.4 6.8 %collective-permute-start.14 = (bf16[512,128]{1,0:T(8,128)(2,1)S(1)}, bf16[512,128]{1,0:T(8,128)(2,1)S(1)}, u32[]{:S(2)}, u32[]{:S(2)}) collective-permute-start(bf16[512,128]{1,0:T(8,128)(2,1)S(1)} %get-tuple-element.63), channel_id=1, source_target_pairs={{0,14},{2,0},{4,2},{6,4},{8,6},{10,8},{12,10},{14,12},{1,15},{3,1}... | collective-permute-start | bytes 393224 | tf_op jit(solution)/shard_map/ppermute | solution.py:394
  (2 other events, 12.4 us)
